TPU v7x, 32 devices: a whole 2x2x4 slice. The times are simulated.
32 devices in a mesh: wa: 8 (over z, x), an: 4 (over y, core).
Axes of the slice: x: 2, y: 2, z: 4, core: 2. Of those that a mesh axis runs over, the one named last changes fastest.
Arguments:
- span_states: bfloat16 [192, 512, 640], P(('wa', 'an')), may hold values from -16 to 16
- offsets: int32 [192], P(('wa', 'an')), may hold values from 0 to 128, as said below
- lengths: int32 [192], P(('wa', 'an')), may hold values from 48 to 384, as said below
- cotangent: bfloat16 [192, 384, 640], P(('wa', 'an')), may hold values from -6 to 6
- qkv_weight: bfloat16 [1228800], P(('wa', 'an')), may hold values from -0.25 to 0.25
- out_weight: bfloat16 [409600], P(('wa', 'an')), may hold values from -1.25 to 1.25
- up_weight: bfloat16 [1638400], P(('wa', 'an')), may hold values from -0.25 to 0.25
- down_weight: bfloat16 [1638400], P(('wa', 'an')), may hold values from -0.125 to 0.125
- up_bias: bfloat16 [2560], P(('wa', 'an')), may hold values from -1.5 to 1.5
- norm_gains: bfloat16 [2, 640], P(None, 'wa'), may hold values from 0.5 to 1.5
- norm_shifts: bfloat16 [2, 640], P(None, 'wa'), may hold values from -1 to 1
- qkv_bias: bfloat16 [3, 640], P(None, 'wa'), may hold values from -1.5 to 1.5
- out_biases: bfloat16 [2, 640], P(None, 'wa'), may hold values from -1.5 to 1.5
Outputs:
- activations: bfloat16 [192, 384, 640], P(('wa', 'an'))
- span_grad: bfloat16 [192, 512, 640], P(('wa', 'an'))
- qkv_weight_grad: float32 [1228800], P(('wa', 'an'))
- out_weight_grad: float32 [409600], P(('wa', 'an'))
- up_weight_grad: float32 [1638400], P(('wa', 'an'))
- down_weight_grad: float32 [1638400], P(('wa', 'an'))
- up_bias_grad: float32 [2560], P(('wa', 'an'))
- norm_gains_grad: float32 [2, 640], P(None, 'wa')
- norm_shifts_grad: float32 [2, 640], P(None, 'wa')
- qkv_bias_grad: float32 [3, 640], P(None, 'wa')
- out_biases_grad: float32 [2, 640], P(None, 'wa')
- rms_values: float32 [3], replicated
Inputs may be any that keep to these rules, and one draw needn't show every extreme that they name: `offsets`: A window whose offset is above 0 is full (length 384); some window starts at 128 in every draw. `lengths`: the valid tokens of a window are its first ones; some window is full in every draw.
All inputs are finite; a program needn't handle non-finite values.
Results may differ from a plain program's by a relative error of at most 0.0095.
Values may be sent and summed in bfloat16 or wider, within the bound.
No kernel may reach another device: no remote copies, remote signals or barrier semaphores. Data moves between devices by JAX's collectives and lax.ppermute only.
A program may use at most 256 MiB of HBM per device.

v0:
```python
import jax
import jax.numpy as jnp
from jax import lax
from jax.sharding import PartitionSpec as P

D = 640
HEADS = 20
FF = 2560
L = 384
CROP = 128


def layer_norm(values, gain, shift):
    mean_value = jnp.mean(values, axis=-1, keepdims=True)
    centred = values - mean_value
    inverse = lax.rsqrt(jnp.mean(centred * centred, axis=-1, keepdims=True) + 1e-05)
    return centred * inverse * gain + shift


def rotate_half(values):
    middle_col = values.shape[-1] // 2
    return jnp.concatenate([-values[..., middle_col:], values[..., :middle_col]], axis=-1)


def rotary_tables(positions, width):
    inverse = 10000.0 ** (-jnp.arange(0, width, 2, dtype=jnp.float32) / width)
    angles = positions[..., None] * inverse
    angles = jnp.concatenate([angles, angles], axis=-1)
    return (jnp.cos(angles), jnp.sin(angles))


def exact_gelu(values):
    return jax.nn.gelu(values, approximate=False)


def crop_window(span_one, start):
    return lax.dynamic_slice_in_dim(span_one, start, L, 0)


def spread_window(padded_one, start):
    return lax.dynamic_slice_in_dim(padded_one, CROP - start, L + CROP, 0)


def split_heads(values):
    return values.reshape(values.shape[0], HEADS, D // HEADS)


def window_scores(queries, key_rows, mask_row):
    scores = jnp.einsum("qhd,khd->hqk", queries, key_rows, preferred_element_type=jnp.float32)
    return jnp.where(mask_row[None, None, :], scores, -1e30)


def attend(pieces):
    query_flat, key_flat, value_flat, mask_row = pieces
    queries = split_heads(query_flat)
    key_rows = split_heads(key_flat)
    value_rows = split_heads(value_flat)
    scores = window_scores(queries, key_rows, mask_row)
    row_max = jnp.max(scores, axis=-1, keepdims=True)
    raised = jnp.exp(scores - row_max)
    row_total = jnp.sum(raised, axis=-1, keepdims=True)
    probs = (raised / row_total).astype(jnp.bfloat16)
    mixed = jnp.einsum("hqk,khd->qhd", probs, value_rows, preferred_element_type=jnp.float32)
    return (mixed.reshape(query_flat.shape[0], D), (row_max + jnp.log(row_total))[..., 0])


def attend_back(pieces):
    query_flat, key_flat, value_flat, mask_row, log_total, grad_flat = pieces
    queries = split_heads(query_flat)
    key_rows = split_heads(key_flat)
    value_rows = split_heads(value_flat)
    grad_mixed = split_heads(grad_flat)
    rows = query_flat.shape[0]
    scores = window_scores(queries, key_rows, mask_row)
    probs = jnp.exp(scores - log_total[:, :, None])
    probs_low = probs.astype(jnp.bfloat16)
    grad_probs = jnp.einsum(
        "qhd,khd->hqk", grad_mixed, value_rows, preferred_element_type=jnp.float32
    )
    grad_values = jnp.einsum(
        "hqk,qhd->khd", probs_low, grad_mixed, preferred_element_type=jnp.float32
    )
    grad_scores = probs * (grad_probs - jnp.sum(probs * grad_probs, axis=-1, keepdims=True))
    grad_scores = grad_scores.astype(jnp.bfloat16)
    grad_queries = jnp.einsum(
        "hqk,khd->qhd", grad_scores, key_rows, preferred_element_type=jnp.float32
    )
    grad_keys = jnp.einsum("hqk,qhd->khd", grad_scores, queries, preferred_element_type=jnp.float32)
    return (grad_queries.reshape(rows, D), grad_keys.reshape(rows, D), grad_values.reshape(rows, D))


def unpack(gathered):
    return (
        gathered[0].reshape(D, 3 * D),
        gathered[1].reshape(D, D),
        gathered[2].reshape(D, FF),
        gathered[3].reshape(FF, D),
        gathered[4].astype(jnp.float32),
    )


def body(
    span_states,
    offsets,
    lengths,
    cotangent,
    qkv_weight,
    out_weight,
    up_weight,
    down_weight,
    up_bias,
    norm_gains,
    norm_shifts,
    qkv_bias,
    out_biases,
):
    windows = span_states.shape[0]
    row_count = windows * L
    width = D // HEADS
    scale_factor = width ** (-0.5)
    gathered = (
        lax.all_gather(qkv_weight, ("wa", "an"), axis=0, tiled=True),
        lax.all_gather(out_weight, ("wa", "an"), axis=0, tiled=True),
        lax.all_gather(up_weight, ("wa", "an"), axis=0, tiled=True),
        lax.all_gather(down_weight, ("wa", "an"), axis=0, tiled=True),
        lax.all_gather(up_bias, ("wa", "an"), axis=0, tiled=True),
    )
    w_qkv, w_out, w_up, w_down, bias_up = unpack(gathered)
    vectors = (
        lax.all_gather(norm_gains, "wa", axis=1, tiled=True),
        lax.all_gather(norm_shifts, "wa", axis=1, tiled=True),
        lax.all_gather(qkv_bias, "wa", axis=1, tiled=True),
        lax.all_gather(out_biases, "wa", axis=1, tiled=True),
    )
    gains = vectors[0].astype(jnp.float32)
    shifts = vectors[1].astype(jnp.float32)
    bias_qkv = vectors[2].astype(jnp.float32)
    bias_out = vectors[3].astype(jnp.float32)
    inputs = jax.vmap(crop_window)(span_states, offsets)
    slot_index = jnp.arange(L, dtype=jnp.int32)
    key_mask = slot_index[None, :] < lengths[:, None]
    row_valid = key_mask.astype(jnp.float32).reshape(row_count)
    stream = inputs.astype(jnp.float32).reshape(row_count, D)
    normed_one, norm_back_one = jax.vjp(layer_norm, stream, gains[0], shifts[0])
    normed_one_low = normed_one.astype(jnp.bfloat16)
    projected = jnp.dot(
        normed_one_low, w_qkv, preferred_element_type=jnp.float32
    ) + bias_qkv.reshape(3 * D)
    positions = (offsets[:, None] + slot_index[None, :]).astype(jnp.float32)
    cosine, sine = rotary_tables(positions, width)
    cosine = cosine[:, :, None, :]
    sine = sine[:, :, None, :]

    def turn(values):
        return values * cosine + rotate_half(values) * sine

    shaped = projected.reshape(windows, L, 3, HEADS, width)
    query_pre = shaped[:, :, 0] * scale_factor
    rotated_queries, turn_back = jax.vjp(turn, query_pre)
    queries = rotated_queries.astype(jnp.bfloat16).reshape(windows, L, D)
    key_rows = turn(shaped[:, :, 1]).astype(jnp.bfloat16).reshape(windows, L, D)
    value_rows = shaped[:, :, 2].astype(jnp.bfloat16).reshape(windows, L, D)
    mixed, log_total = lax.map(attend, (queries, key_rows, value_rows, key_mask))
    mixed_low = mixed.reshape(row_count, D).astype(jnp.bfloat16)
    attn_out = jnp.dot(mixed_low, w_out, preferred_element_type=jnp.float32) + bias_out[0]
    middle = stream + attn_out
    normed_two, norm_back_two = jax.vjp(layer_norm, middle, gains[1], shifts[1])
    normed_two_low = normed_two.astype(jnp.bfloat16)
    hidden_pre = jnp.dot(normed_two_low, w_up, preferred_element_type=jnp.float32) + bias_up
    hidden_full, gelu_back = jax.vjp(exact_gelu, hidden_pre)
    hidden_low = hidden_full.astype(jnp.bfloat16)
    ffn_out = jnp.dot(hidden_low, w_down, preferred_element_type=jnp.float32) + bias_out[1]
    result = middle + ffn_out
    activations = result.astype(jnp.bfloat16).reshape(windows, L, D)

    def squares(values):
        return jnp.sum(row_valid * jnp.sum(values * values, axis=-1))

    square_result = squares(result)
    square_attn = squares(attn_out)
    square_ffn = squares(ffn_out)
    token_count = jnp.sum(lengths).astype(jnp.float32)
    stat_totals = lax.psum((square_result, square_attn, square_ffn, token_count), ("wa", "an"))
    gathered_back = (
        lax.all_gather(qkv_weight, ("wa", "an"), axis=0, tiled=True),
        lax.all_gather(out_weight, ("wa", "an"), axis=0, tiled=True),
        lax.all_gather(up_weight, ("wa", "an"), axis=0, tiled=True),
        lax.all_gather(down_weight, ("wa", "an"), axis=0, tiled=True),
        lax.all_gather(up_bias, ("wa", "an"), axis=0, tiled=True),
    )
    back_qkv, back_out, back_up, back_down, bias_unused = unpack(gathered_back)
    grad_result = cotangent.astype(jnp.float32).reshape(row_count, D) * row_valid[:, None]
    grad_ffn = grad_result.astype(jnp.bfloat16)
    grad_down = jnp.einsum("rf,rd->fd", hidden_low, grad_ffn, preferred_element_type=jnp.float32)
    grad_bias_down = jnp.sum(grad_ffn.astype(jnp.float32), axis=0)
    grad_hidden = jnp.einsum("rd,fd->rf", grad_ffn, back_down, preferred_element_type=jnp.float32)
    grad_pre = gelu_back(grad_hidden)[0].astype(jnp.bfloat16)
    grad_up = jnp.einsum("rd,rf->df", normed_two_low, grad_pre, preferred_element_type=jnp.float32)
    grad_bias_up = jnp.sum(grad_pre.astype(jnp.float32), axis=0)
    grad_normed_two = jnp.einsum("rf,df->rd", grad_pre, back_up, preferred_element_type=jnp.float32)
    grad_mid_part, grad_gain_two, grad_shift_two = norm_back_two(grad_normed_two)
    grad_middle = grad_result + grad_mid_part
    grad_attn = grad_middle.astype(jnp.bfloat16)
    grad_out = jnp.einsum("rd,re->de", mixed_low, grad_attn, preferred_element_type=jnp.float32)
    grad_bias_attn = jnp.sum(grad_attn.astype(jnp.float32), axis=0)
    grad_mixed = jnp.einsum("re,de->rd", grad_attn, back_out, preferred_element_type=jnp.float32)
    grad_mixed = grad_mixed.astype(jnp.bfloat16).reshape(windows, L, D)
    grad_queries, grad_keys, grad_values = lax.map(
        attend_back, (queries, key_rows, value_rows, key_mask, log_total, grad_mixed)
    )
    grad_query_pre = turn_back(grad_queries.reshape(windows, L, HEADS, width))[0] * scale_factor
    grad_key_pre = turn_back(grad_keys.reshape(windows, L, HEADS, width))[0]
    grad_value_pre = grad_values.reshape(windows, L, HEADS, width)
    grad_projected = jnp.stack([grad_query_pre, grad_key_pre, grad_value_pre], axis=2)
    grad_projected = grad_projected.reshape(row_count, 3 * D).astype(jnp.bfloat16)
    grad_qkv = jnp.einsum(
        "rd,re->de", normed_one_low, grad_projected, preferred_element_type=jnp.float32
    )
    grad_bias_qkv = jnp.sum(grad_projected.astype(jnp.float32), axis=0).reshape(3, D)
    grad_normed_one = jnp.einsum(
        "re,de->rd", grad_projected, back_qkv, preferred_element_type=jnp.float32
    )
    grad_stream_part, grad_gain_one, grad_shift_one = norm_back_one(grad_normed_one)
    grad_stream = (grad_middle + grad_stream_part).reshape(windows, L, D).astype(jnp.bfloat16)
    padded_grad = jnp.pad(grad_stream, ((0, 0), (CROP, CROP), (0, 0)))
    span_grad = jax.vmap(spread_window)(padded_grad, offsets)
    weight_shards = (
        lax.psum_scatter(
            grad_qkv.reshape(3 * D * D), ("wa", "an"), scatter_dimension=0, tiled=True
        ),
        lax.psum_scatter(grad_out.reshape(D * D), ("wa", "an"), scatter_dimension=0, tiled=True),
        lax.psum_scatter(grad_up.reshape(D * FF), ("wa", "an"), scatter_dimension=0, tiled=True),
        lax.psum_scatter(grad_down.reshape(FF * D), ("wa", "an"), scatter_dimension=0, tiled=True),
        lax.psum_scatter(grad_bias_up, ("wa", "an"), scatter_dimension=0, tiled=True),
    )
    gain_terms = jnp.stack([grad_gain_one, grad_gain_two])
    shift_terms = jnp.stack([grad_shift_one, grad_shift_two])
    out_terms = jnp.stack([grad_bias_attn, grad_bias_down])
    vector_totals = lax.psum((gain_terms, shift_terms, grad_bias_qkv, out_terms), ("wa", "an"))
    share_cols = D // lax.axis_size("wa")
    first_col = lax.axis_index("wa") * share_cols
    vector_shards = [
        lax.dynamic_slice_in_dim(total, first_col, share_cols, 1) for total in vector_totals
    ]
    root_means = jnp.sqrt(
        jnp.stack([stat_totals[0], stat_totals[1], stat_totals[2]]) / (stat_totals[3] * D)
    )
    return (
        activations,
        span_grad,
        weight_shards[0],
        weight_shards[1],
        weight_shards[2],
        weight_shards[3],
        weight_shards[4],
        vector_shards[0],
        vector_shards[1],
        vector_shards[2],
        vector_shards[3],
        root_means,
    )


def solution(mesh):
    return jax.shard_map(
        body,
        mesh=mesh,
        in_specs=(
            P(("wa", "an"), None, None),
            P(("wa", "an")),
            P(("wa", "an")),
            P(("wa", "an"), None, None),
            P(("wa", "an")),
            P(("wa", "an")),
            P(("wa", "an")),
            P(("wa", "an")),
            P(("wa", "an")),
            P(None, "wa"),
            P(None, "wa"),
            P(None, "wa"),
            P(None, "wa"),
        ),
        out_specs=(
            P(("wa", "an"), None, None),
            P(("wa", "an"), None, None),
            P(("wa", "an")),
            P(("wa", "an")),
            P(("wa", "an")),
            P(("wa", "an")),
            P(("wa", "an")),
            P(None, "wa"),
            P(None, "wa"),
            P(None, "wa"),
            P(None, "wa"),
            P(),
        ),
        check_vma=False,
    )
```

profile of v0, /device:TPU:0, one launch (start us, length us, event | category | flops | bytes accessed | tf_op | source)
XLA Modules:
  0.0 1579.0 jit_solution(11134644912222877471)
XLA Ops:
  12.5 18.5 %while.30 = (s32[]{:T(128)}, bf16[6,512,640]{2,1,0:T(8,128)(2,1)}, s32[6,3]{0,1:T(4,128)S(1)}, bf16[6,384,640]{2,1,0:T(8,128)(2,1)S(1)}, s32[]{:T(128)}) while((s32[]{:T(128)}, bf16[6,512,640]{2,1,0:T(8,128)(2,1)}, s32[6,3]{0,1:T(4,128)S(1)}, bf16[6,384,640]{2,1,0:T(8,128)(2,1)S(1)}, s32[]{:T(128)}) %tuple.126), condition=%wide.while_cond, body=%wide.while_body.sunk | while | flops 2 | bytes 983157 | solution.py:37
  33.2 22.4 %all-gather = bf16[8,80,2]{1,2,0:T(2,128)(2,1)S(1)} all-gather(bf16[1,80,2]{1,2,0:T(2,128)(2,1)S(1)} %bitcast.262), channel_id=1, replica_groups=mesh['wa'=8,'an'=4] {'wa'}, dimensions={0}, use_global_device_ids=true | all-gather | bytes 2880 | tf_op jit(solution)/shard_map/all_gather | solution.py:130
  55.6 16.3 %all-gather.1 = bf16[8,80,2]{1,2,0:T(2,128)(2,1)S(1)} all-gather(bf16[1,80,2]{1,2,0:T(2,128)(2,1)S(1)} %bitcast.263), channel_id=1, replica_groups=mesh['wa'=8,'an'=4] {'wa'}, dimensions={0}, use_global_device_ids=true | all-gather | bytes 2880 | tf_op jit(solution)/shard_map/all_gather | solution.py:131
  72.0 18.5 %all-gather.3 = bf16[8,80,3]{1,2,0:T(4,128)(2,1)S(1)} all-gather(bf16[1,80,3]{1,2,0:T(4,128)(2,1)S(1)} %bitcast.261), channel_id=1, replica_groups=mesh['wa'=8,'an'=4] {'wa'}, dimensions={0}, use_global_device_ids=true | all-gather | bytes 4320 | tf_op jit(solution)/shard_map/all_gather | solution.py:132
  94.0 45.8 %all-gather.4 = bf16[32,1,12800]{2,1,0:T(2,128)(2,1)} all-gather(bf16[1,1,12800]{2,1,0:T(2,128)(2,1)S(1)} %reshape.621), channel_id=1, replica_groups=mesh['wa'=8,'an'=4] {'wa','an'}, dimensions={0}, use_global_device_ids=true | all-gather | bytes 844800 | tf_op jit(solution)/shard_map/all_gather | solution.py:123
  149.8 16.8 %all-gather.5 = bf16[8,80,2]{1,2,0:T(2,128)(2,1)S(1)} all-gather(bf16[1,80,2]{1,2,0:T(2,128)(2,1)S(1)} %bitcast.264), channel_id=1, replica_groups=mesh['wa'=8,'an'=4] {'wa'}, dimensions={0}, use_global_device_ids=true | all-gather | bytes 2880 | tf_op jit(solution)/shard_map/all_gather | solution.py:133
  167.5 39.2 %all-reduce.7 = bf16[2560]{0:T(1024)(128)(2,1)S(1)} all-reduce(bf16[2560]{0:T(1024)(128)(2,1)S(1)} %dynamic-update-slice.4), channel_id=1, replica_groups=mesh['wa'=8,'an'=4] {'wa','an'}, use_global_device_ids=true, to_apply=%add.7 | all-reduce | flops 2560 | bytes 10240
  216.3 14.4 reduce.20
  248.5 18.2 %copy.94 = f32[2304,1920]{0,1:T(8,128)} copy(f32[2304,1920]{1,0:T(8,128)} %convolution_add_fusion) | data formatting | bytes 35389440 | tf_op jit(solution)/shard_map/add | solution.py:146
  266.8 20.7 %reshape.545 = f32[6,384,3,20,32]{1,0,4,3,2:T(8,128)} reshape(f32[2304,1920]{0,1:T(8,128)} %copy.94) | data formatting | bytes 35389440 | tf_op jit(solution)/shard_map/reshape | solution.py:157
  341.7 79.9 %while.28 = (s32[]{:T(128)}, bf16[6,384,640]{2,1,0:T(8,128)(2,1)}, f32[6,20,384]{2,1,0:T(8,128)}, bf16[6,384,640]{1,2,0:T(8,128)(2,1)}, pred[6,384]{1,0:T(8,128)...) while((s32[]{:T(128)}, bf16[6,384,640]{2,1,0:T(8,128)(2,1)}, ...), condition=%wide.region_5.6_spmd, body=%wide.region_2.5_spmd.sunk | while | flops 404021760 | bytes 42525664 | solution.py:163
  438.3 61.5 %multiply_convert_fusion.1 = (bf16[2304,2560]{1,0:T(8,128)(2,1)}, f32[2304,2560]{1,0:T(8,128)}, f32[2304,2560]{1,0:T(8,128)}) fusion(f32[2560]{0:T(1024)S(1)} %copy-done.40, bf16[640,2560]{1,0:T(8,128)(2,1)S(1)} %reshape.547, f32[2304,640]{1,0:T(8,128)} %copy-done.9, f32[640]{0:T(1024)S(1)} %copy-done.49, f32[640]{0:T(1024)S(1)} %copy-done.39, ...), kind=kOutput, calls=%fused_computation.35 | convolution fusion | flops 7946403840 | bytes 68191232 | tf_op jit(solution)/shard_map/dot_general | solution.py:169
  505.2 26.3 %convert_reduce_fusion.1 = (f32[2560]{0:T(1024)}, bf16[2304,2560]{1,0:T(8,128)(2,1)}) fusion(f32[2304,2560]{1,0:T(8,128)} %get-tuple-element.278, bf16[2304,640]{1,0:T(8,128)(2,1)} %bitcast.255, bf16[2560,640]{1,0:T(8,128)(2,1)S(1)} %reshape.548, f32[2304,2560]{1,0:T(8,128)} %get-tuple-element.328, f32[2560]{0:T(1024)S(1)} %copy-done.40), kind=kOutput, calls=%fused_computation.33 | convolution fusion | flops 7650014720 | bytes 65228800 | tf_op jit(solution)/shard_map/rd,fd->rf/dot_general | solution.py:196
  558.6 16.6 %multiply_reduce_fusion.3 = (f32[2304]{0:T(1024)}, f32[2304]{0:T(1024)}, f32[2304]{0:T(1024)S(1)}, f32[640]{0:T(1024)}, f32[640]{0:T(1024)}, /*index=5*/bf16[2304,640]{1,0:T(8,128)(2,1)}) fusion(f32[2304,640]{1,0:T(8,128)S(1)} %copy-done.10, f32[640]{0:T(1024)S(1)} %copy-done.45, f32[2304,640]{1,0:T(8,128)S(1)} %fusion.58, f32[640]{0:T(1024)S(1)} %copy-done.39, ...), kind=kOutput, calls=%fused_computation.84 | convolution fusion | flops 7571858432 | bytes 29875200 | tf_op jit(solution)/shard_map/dot_general | solution.py:172
  588.4 509.3 %while.29 = (s32[]{:T(128)}, f32[6,384,640]{1,0,2:T(8,128)}, f32[6,384,640]{1,0,2:T(8,128)}, bf16[6,384,640]{1,2,0:T(8,128)(2,1)}, bf16[6,384,640]{1,2,0:T(8,128...) while((s32[]{:T(128)}, f32[6,384,640]{1,0,2:T(8,128)}, ...), condition=%wide.region_12.13_spmd, body=%wide.region_10.12_spmd.sunk | while | flops 979100160 | bytes 179130960 | solution.py:208
  626.7 21.2 %dynamic_update_slice.29 = f32[6,384,640]{1,0,2:T(8,128)} dynamic-update-slice(f32[6,384,640]{1,0,2:T(8,128)} %get-tuple-element.565, f32[1,384,640]{1,0,2:T(1,128)S(1)} %copy.167, s32[]{:T(128)} %get-tuple-element.563, s32[]{:T(128)} %constant.38.clone.1..sunk, s32[]{:T(128)} %constant.38.clone.1..sunk) | dynamic-update-slice | bytes 1966084 | tf_op jit(solution)/shard_map/while/body/jit(dynamic_update_index_in_dim)/dynamic_update_slice | solution.py:163
  652.5 21.2 %dynamic_update_slice.28 = f32[6,384,640]{1,0,2:T(8,128)} dynamic-update-slice(f32[6,384,640]{1,0,2:T(8,128)} %get-tuple-element.564, f32[1,384,640]{1,0,2:T(1,128)S(1)} %copy.166, s32[]{:T(128)} %get-tuple-element.563, s32[]{:T(128)} %constant.38.clone.1..sunk, s32[]{:T(128)} %constant.38.clone.1..sunk) | dynamic-update-slice | bytes 1966084 | tf_op jit(solution)/shard_map/while/body/jit(dynamic_update_index_in_dim)/dynamic_update_slice | solution.py:163
  711.5 21.2 %dynamic_update_slice.29 = f32[6,384,640]{1,0,2:T(8,128)} dynamic-update-slice(f32[6,384,640]{1,0,2:T(8,128)} %get-tuple-element.565, f32[1,384,640]{1,0,2:T(1,128)S(1)} %copy.167, s32[]{:T(128)} %get-tuple-element.563, s32[]{:T(128)} %constant.38.clone.1..sunk, s32[]{:T(128)} %constant.38.clone.1..sunk) | dynamic-update-slice | bytes 1966084 | tf_op jit(solution)/shard_map/while/body/jit(dynamic_update_index_in_dim)/dynamic_update_slice | solution.py:163
  737.3 21.2 %dynamic_update_slice.28 = f32[6,384,640]{1,0,2:T(8,128)} dynamic-update-slice(f32[6,384,640]{1,0,2:T(8,128)} %get-tuple-element.564, f32[1,384,640]{1,0,2:T(1,128)S(1)} %copy.166, s32[]{:T(128)} %get-tuple-element.563, s32[]{:T(128)} %constant.38.clone.1..sunk, s32[]{:T(128)} %constant.38.clone.1..sunk) | dynamic-update-slice | bytes 1966084 | tf_op jit(solution)/shard_map/while/body/jit(dynamic_update_index_in_dim)/dynamic_update_slice | solution.py:163
  796.3 21.2 %dynamic_update_slice.29 = f32[6,384,640]{1,0,2:T(8,128)} dynamic-update-slice(f32[6,384,640]{1,0,2:T(8,128)} %get-tuple-element.565, f32[1,384,640]{1,0,2:T(1,128)S(1)} %copy.167, s32[]{:T(128)} %get-tuple-element.563, s32[]{:T(128)} %constant.38.clone.1..sunk, s32[]{:T(128)} %constant.38.clone.1..sunk) | dynamic-update-slice | bytes 1966084 | tf_op jit(solution)/shard_map/while/body/jit(dynamic_update_index_in_dim)/dynamic_update_slice | solution.py:163
  822.1 21.2 %dynamic_update_slice.28 = f32[6,384,640]{1,0,2:T(8,128)} dynamic-update-slice(f32[6,384,640]{1,0,2:T(8,128)} %get-tuple-element.564, f32[1,384,640]{1,0,2:T(1,128)S(1)} %copy.166, s32[]{:T(128)} %get-tuple-element.563, s32[]{:T(128)} %constant.38.clone.1..sunk, s32[]{:T(128)} %constant.38.clone.1..sunk) | dynamic-update-slice | bytes 1966084 | tf_op jit(solution)/shard_map/while/body/jit(dynamic_update_index_in_dim)/dynamic_update_slice | solution.py:163
  881.1 21.2 %dynamic_update_slice.29 = f32[6,384,640]{1,0,2:T(8,128)} dynamic-update-slice(f32[6,384,640]{1,0,2:T(8,128)} %get-tuple-element.565, f32[1,384,640]{1,0,2:T(1,128)S(1)} %copy.167, s32[]{:T(128)} %get-tuple-element.563, s32[]{:T(128)} %constant.38.clone.1..sunk, s32[]{:T(128)} %constant.38.clone.1..sunk) | dynamic-update-slice | bytes 1966084 | tf_op jit(solution)/shard_map/while/body/jit(dynamic_update_index_in_dim)/dynamic_update_slice | solution.py:163
  906.9 21.2 %dynamic_update_slice.28 = f32[6,384,640]{1,0,2:T(8,128)} dynamic-update-slice(f32[6,384,640]{1,0,2:T(8,128)} %get-tuple-element.564, f32[1,384,640]{1,0,2:T(1,128)S(1)} %copy.166, s32[]{:T(128)} %get-tuple-element.563, s32[]{:T(128)} %constant.38.clone.1..sunk, s32[]{:T(128)} %constant.38.clone.1..sunk) | dynamic-update-slice | bytes 1966084 | tf_op jit(solution)/shard_map/while/body/jit(dynamic_update_index_in_dim)/dynamic_update_slice | solution.py:163
  965.9 21.2 %dynamic_update_slice.29 = f32[6,384,640]{1,0,2:T(8,128)} dynamic-update-slice(f32[6,384,640]{1,0,2:T(8,128)} %get-tuple-element.565, f32[1,384,640]{1,0,2:T(1,128)S(1)} %copy.167, s32[]{:T(128)} %get-tuple-element.563, s32[]{:T(128)} %constant.38.clone.1..sunk, s32[]{:T(128)} %constant.38.clone.1..sunk) | dynamic-update-slice | bytes 1966084 | tf_op jit(solution)/shard_map/while/body/jit(dynamic_update_index_in_dim)/dynamic_update_slice | solution.py:163
  991.7 21.2 %dynamic_update_slice.28 = f32[6,384,640]{1,0,2:T(8,128)} dynamic-update-slice(f32[6,384,640]{1,0,2:T(8,128)} %get-tuple-element.564, f32[1,384,640]{1,0,2:T(1,128)S(1)} %copy.166, s32[]{:T(128)} %get-tuple-element.563, s32[]{:T(128)} %constant.38.clone.1..sunk, s32[]{:T(128)} %constant.38.clone.1..sunk) | dynamic-update-slice | bytes 1966084 | tf_op jit(solution)/shard_map/while/body/jit(dynamic_update_index_in_dim)/dynamic_update_slice | solution.py:163
  1050.7 21.2 %dynamic_update_slice.29 = f32[6,384,640]{1,0,2:T(8,128)} dynamic-update-slice(f32[6,384,640]{1,0,2:T(8,128)} %get-tuple-element.565, f32[1,384,640]{1,0,2:T(1,128)S(1)} %copy.167, s32[]{:T(128)} %get-tuple-element.563, s32[]{:T(128)} %constant.38.clone.1..sunk, s32[]{:T(128)} %constant.38.clone.1..sunk) | dynamic-update-slice | bytes 1966084 | tf_op jit(solution)/shard_map/while/body/jit(dynamic_update_index_in_dim)/dynamic_update_slice | solution.py:163
  1076.5 21.2 %dynamic_update_slice.28 = f32[6,384,640]{1,0,2:T(8,128)} dynamic-update-slice(f32[6,384,640]{1,0,2:T(8,128)} %get-tuple-element.564, f32[1,384,640]{1,0,2:T(1,128)S(1)} %copy.166, s32[]{:T(128)} %get-tuple-element.563, s32[]{:T(128)} %constant.38.clone.1..sunk, s32[]{:T(128)} %constant.38.clone.1..sunk) | dynamic-update-slice | bytes 1966084 | tf_op jit(solution)/shard_map/while/body/jit(dynamic_update_index_in_dim)/dynamic_update_slice | solution.py:163
  1113.5 14.8 fusion.30
  1128.3 45.3 %convert_reduce_fusion = (f32[3,20,32]{2,1,0:T(8,128)S(1)}, bf16[6,384,3,20,32]{1,0,4,3,2:T(8,128)(2,1)}) fusion(bf16[6,384,1,20,32]{1,0,4,3,2:T(8,128)(2,1)S(1)} %bitcast.246, bf16[6,384,1,20,32]{1,0,4,3,2:T(8,128)(2,1)} %get-tuple-element.310, bf16[6,384,1,20,32]{1,0,4,3,2:T(8,128)(2,1)} %get-tuple-element.309), kind=kLoop, calls=%fused_computation.32 | loop fusion | flops 17692800 | bytes 17702400 | tf_op jit(solution)/shard_map/reduce_sum | solution.py:219
  1254.7 45.5 %all-reduce.13 = (f32[2560]{0:T(1024)S(1)}, f32[2,640]{1,0:T(2,128)S(1)}, f32[2,640]{1,0:T(2,128)S(1)}, f32[3,640]{1,0:T(4,128)S(1)}, f32[2,640]{1,0:T(2,128)S(1...) all-reduce(f32[2560]{0:T(1024)S(1)} %copy-done.41, ...), channel_id=6, replica_groups=mesh['wa'=8,'an'=4] {'wa','an'}, use_global_device_ids=true, to_apply=%region_20.21.clone | all-reduce | flops 8324 | bytes 66592
  1306.6 24.0 %while.31 = (s32[]{:T(128)}, bf16[6,640,640]{2,1,0:T(8,128)(2,1)}, s32[6,3]{0,1:T(4,128)S(1)}, bf16[6,512,640]{2,1,0:T(8,128)(2,1)}, s32[]{:T(128)}) while((s32[]{:T(128)}, bf16[6,640,640]{2,1,0:T(8,128)(2,1)}, s32[6,3]{0,1:T(4,128)S(1)}, bf16[6,512,640]{2,1,0:T(8,128)(2,1)}, s32[]{:T(128)}) %tuple.151), condition=%wide.while_cond.1, body=%wide.while_body.1.sunk | while | flops 2 | bytes 1312361 | solution.py:41
  1330.6 235.0 %all-reduce.17.cloned.1.call-done = (f32[1228800]{0:T(1024)}, f32[409600]{0:T(1024)}, f32[1638400]{0:T(1024)}, f32[1638400]{0:T(1024)}) async-done(((f32[1228800]{0:T(1024)}, f32[409600]{0:T(1024)}, f32[1638400]{0:T(1024)}, f32[1638400]{0:T(1024)}), (f32[1228800]{0:T(1024)}, f32[409600]{0:T(1024)}, f32[1638400]{0:T(1024)}, f32[1638400]{0:T(1024)})) %all-reduce.17.cloned.1.call-update) | async-done | bytes 19660816
  (445 shorter events, 650.1 us)
Async XLA Ops:
  7.2 26.0 %copy-start.51 = (bf16[2,80]{1,0:T(2,128)(2,1)S(1)}, bf16[2,80]{1,0:T(2,128)(2,1)}, u32[]{:S(2)}) copy-start(bf16[2,80]{1,0:T(2,128)(2,1)} %param.26) | copy-start | bytes 964
  7.2 48.4 %copy-start.52 = (bf16[2,80]{1,0:T(2,128)(2,1)S(1)}, bf16[2,80]{1,0:T(2,128)(2,1)}, u32[]{:S(2)}) copy-start(bf16[2,80]{1,0:T(2,128)(2,1)} %param.27) | copy-start | bytes 964
  7.2 64.8 %copy-start.50 = (bf16[3,80]{1,0:T(4,128)(2,1)S(1)}, bf16[3,80]{1,0:T(4,128)(2,1)}, u32[]{:S(2)}) copy-start(bf16[3,80]{1,0:T(4,128)(2,1)} %param.28) | copy-start | bytes 1444
  7.2 209.1 %all-gather.14.cloned.1.call-start = ((), (), s32[]{:S(2)}) async-start(), calls=%async_computation.2 | async-start | bytes 5068800 | tf_op jit(solution)/shard_map/all_gather | solution.py:122
  8.9 422.9 %all-gather.10.cloned.1.call-start = ((), (), s32[]{:S(2)}) async-start(), calls=%async_computation | async-start | bytes 3379200 | tf_op jit(solution)/shard_map/all_gather | solution.py:124
  9.7 490.2 %all-gather.12.cloned.1.call-start = ((), (), s32[]{:S(2)}) async-start(), calls=%async_computation.1 | async-start | bytes 3379200 | tf_op jit(solution)/shard_map/all_gather | solution.py:125
  10.4 1555.2 %all-reduce.17.cloned.1.call-start = ((), (), s32[]{:S(2)}) async-start(), calls=%async_computation.3 | async-start | bytes 39321600
  12.5 81.5 %copy-start.54 = (s32[6]{0:T(128)S(1)}, s32[6]{0:T(128)}, u32[]{:S(2)}) copy-start(s32[6]{0:T(128)} %param.19) | copy-start | bytes 76
  12.5 81.5 %copy-start.36 = (bf16[12800]{0:T(1024)(128)(2,1)S(1)}, bf16[12800]{0:T(1024)(128)(2,1)}, u32[]{:S(2)}) copy-start(bf16[12800]{0:T(1024)(128)(2,1)} %param.22) | copy-start | bytes 76804
  31.0 182.9 %copy-start.2 = (bf16[6,384,640]{2,1,0:T(8,128)(2,1)}, bf16[6,384,640]{2,1,0:T(8,128)(2,1)S(1)}, u32[]{:S(2)}) copy-start(bf16[6,384,640]{2,1,0:T(8,128)(2,1)S(1)} %get-tuple-element.116) | copy-start | bytes 8847364
  31.5 118.3 %copy-start.53 = (bf16[2,80]{1,0:T(2,128)(2,1)S(1)}, bf16[2,80]{1,0:T(2,128)(2,1)}, u32[]{:S(2)}) copy-start(bf16[2,80]{1,0:T(2,128)(2,1)} %param.29) | copy-start | bytes 964
  31.5 135.8 %copy-start.57 = (bf16[80]{0:T(256)(128)(2,1)S(1)}, bf16[80]{0:T(256)(128)(2,1)}, u32[]{:S(2)}) copy-start(bf16[80]{0:T(256)(128)(2,1)} %param.25) | copy-start | bytes 484
  93.1 222.8 %copy-start.12 = (f32[6,384,32]{1,0,2:T(8,128)}, f32[6,384,32]{1,0,2:T(8,128)S(1)}, u32[]{:S(2)}) copy-start(f32[6,384,32]{1,0,2:T(8,128)S(1)} %get-tuple-element.317) | copy-start | bytes 884740
  207.3 9.0 copy-start.34
  299.9 10.3 slice-start.2
  315.9 9.1 copy-start.14
  341.7 79.9 %copy-start.3 = (bf16[6,384,640]{2,1,0:T(8,128)(2,1)S(1)}, bf16[6,384,640]{2,1,0:T(8,128)(2,1)}, u32[]{:S(2)}) copy-start(bf16[6,384,640]{2,1,0:T(8,128)(2,1)} %copy-done.2) | copy-start | bytes 8847364
  341.7 79.9 %copy-start.46 = (f32[640]{0:T(1024)S(1)}, f32[640]{0:T(1024)}, u32[]{:S(2)}) copy-start(f32[640]{0:T(1024)} %get-tuple-element.198) | copy-start | bytes 7684
  438.3 61.5 %copy-start.16 = (bf16[640,2560]{1,0:T(8,128)(2,1)}, bf16[640,2560]{1,0:T(8,128)(2,1)S(1)}, u32[]{:S(2)}) copy-start(bf16[640,2560]{1,0:T(8,128)(2,1)S(1)} %reshape.547) | copy-start | bytes 9830404
  531.5 13.5 copy-start.10
  545.0 13.6 copy-start.45
  558.6 16.6 %copy-start.29 = (f32[2304]{0:T(1024)S(1)}, f32[2304]{0:T(1024)}, u32[]{:S(2)}) copy-start(f32[2304]{0:T(1024)} %copy-done.28) | copy-start | bytes 27652
  588.4 509.3 %copy-start.13 = (f32[6,384,32]{1,0,2:T(8,128)S(1)}, f32[6,384,32]{1,0,2:T(8,128)}, u32[]{:S(2)}) copy-start(f32[6,384,32]{1,0,2:T(8,128)} %copy-done.12) | copy-start | bytes 884740
  1173.6 10.0 copy-start.18
  1183.5 24.6 %slice-start = ((s8[5898240]{0:T(1024)(128)(4,1)}), s8[4194304]{0:T(1024)(128)(4,1)S(1)}, s32[]{:S(2)}) async-start(s8[5898240]{0:T(1024)(128)(4,1)} %bitcast.228), calls=%async_computation.4 | async-start | bytes 8388608
  1183.6 10.7 copy-start.4
  1183.6 10.7 copy-start.11
  1183.6 10.7 copy-start.23
  1183.6 10.7 copy-start.32
  1183.6 24.6 %slice-start.1 = ((s8[5898240]{0:T(1024)(128)(4,1)}), s8[1703936]{0:T(1024)(128)(4,1)S(1)}, s32[]{:S(2)}) async-start(s8[5898240]{0:T(1024)(128)(4,1)} %bitcast.228), calls=%async_computation.5 | async-start | bytes 3407872
  1194.2 10.7 copy-start.33
  1249.9 56.7 %copy-start.30 = (s32[6,3]{0,1:T(4,128)S(1)}, s32[6,3]{0,1:T(4,128)}, u32[]{:S(2)}) copy-start(s32[6,3]{0,1:T(4,128)} %get-tuple-element.589) | copy-start | bytes 220
  (44 other events, 189.7 us)
Sparse Core Ops, SparseCore 0:
  11.4 66.9 all-gather.13
  81.2 60.7 all-gather.9
  144.9 59.4 all-gather.11
  1249.4 316.1 all-reduce.16
where the time goes:
time: 1600 us; the launch traced here: 1580 us
  local copies, waits for them, and re-layouts  513 us (32%)
  matrix products  380 us (24%)
  waiting for transfers between devices  236 us (15%)
  other arithmetic  227 us (14%)
  blocking collectives  204 us (13%)
  between operations  16.4 us (1%)
    dynamic_update_slice x42, local copies, waits for them, and re-layouts, body(): lax.map(attend, (queries, key_rows, value_rows, key_mask))  291 us
    unnamed x5, waiting for transfers between devices  236 us
    unnamed x2, blocking collectives  84.7 us
    dot_general x1, matrix products, body(): jnp.dot(normed_two_low, w_up, preferred_element_type=jnp.float32) + bias_up  61.5 us
    dot_general x12, matrix products, window_scores(): jnp.einsum('qhd,khd->hqk', queries, key_rows, preferred_element_type=jnp....  52.8 us
    all_gather x1, blocking collectives, body(): lax.all_gather(out_weight, ('wa', 'an'), axis=0, tiled=True)  45.8 us
    reduce_sum x1, other arithmetic, body(): jnp.sum(grad_projected.astype(jnp.float32), axis=0).reshape(3, D)  45.3 us
    gather x36, local copies, waits for them, and re-layouts  42.4 us
  transfers between devices with their start and end apart: 4, of which 1 were waited for; matrix products, arithmetic and copies ran while one was open for 23% of the time, Pallas kernels for 0%

commit v1 on v0

v1 whole, which is shorter than its diff:
```python
import math

import jax
import jax.numpy as jnp
from jax import lax
from jax.experimental import pallas as pl
from jax.experimental.pallas import tpu as pltpu
from jax.sharding import PartitionSpec as P

D = 640
HEADS = 20
FF = 2560
L = 384
CROP = 128
SPAN = L + CROP
HW = D // HEADS
LANES = 128
TILES = D // LANES
GROUP = LANES // HW
SCALE = HW**-0.5
F32 = jnp.float32
BF16 = jnp.bfloat16
BOTH = ("wa", "an")


def nn(a, b):
    return lax.dot_general(a, b, (((1,), (0,)), ((), ())), preferred_element_type=F32)


def nt(a, b):
    return lax.dot_general(a, b, (((1,), (1,)), ((), ())), preferred_element_type=F32)


def tn(a, b):
    return lax.dot_general(a, b, (((0,), (0,)), ((), ())), preferred_element_type=F32)


def lane_iota(rows, cols):
    return lax.broadcasted_iota(jnp.int32, (rows, cols), 1)


def normalize(v):
    centred = v - jnp.mean(v, axis=-1, keepdims=True)
    inverse = lax.rsqrt(jnp.mean(centred * centred, axis=-1, keepdims=True) + 1e-05)
    return centred * inverse, inverse


def norm_back(d, n, inverse):
    return inverse * (
        d - jnp.mean(d, axis=-1, keepdims=True) - n * jnp.mean(d * n, axis=-1, keepdims=True)
    )


def col_sum(v):
    return jnp.sum(v, axis=0, keepdims=True)


def split_lanes(v, last):
    high = v.astype(BF16).astype(F32)
    rest = v - high
    mid = rest.astype(BF16).astype(F32)
    low = rest - mid
    at = lane_iota(*v.shape) % HW
    out = jnp.where(at == 0, high, jnp.where(at == 1, mid, jnp.where(at == 2, low, 0.0)))
    return jnp.where(at == 3, last, out).astype(BF16)


def rolled(v):
    first = (lane_iota(*v.shape) % HW) < HW // 2
    ahead = pltpu.roll(v, LANES - HW // 2, 1)
    behind = pltpu.roll(v, HW // 2, 1)
    return jnp.where(first, ahead, behind)


def stack_heads(wide):
    head = (lane_iota(1, 2 * LANES) % LANES) // HW
    return [jnp.where(head == h, wide, jnp.zeros_like(wide)) for h in range(GROUP)]


def key_side(length):
    at = lane_iota(L, LANES) % HW
    row = lax.broadcasted_iota(jnp.int32, (L, LANES), 0)
    bias = jnp.where(row < length, 0.0, -1e30)
    return jnp.where(at < 3, 1.0, jnp.where(at == 3, bias, 0.0)).astype(BF16)


def take_rows(full, start):
    return pltpu.roll(full, (SPAN - start) % SPAN, 0)[:L]


def front_kernel(
    offsets, lengths, span, w_qkv, vecs, bias_qkv, cosine, sine,
    x_out, q_out, k_out, v_out, lse_out, mixed_out,
    proj, keys_big, values_big,
):
    window = pl.program_id(0)
    start = offsets[window]
    length = lengths[window]
    x = take_rows(span[0].astype(F32), start)
    x_out[0] = x.astype(BF16)
    n, _ = normalize(x)
    normed = (n * vecs[0:1, :] + vecs[1:2, :]).astype(BF16)
    proj[...] = nn(normed, w_qkv[...]) + bias_qkv[...]
    cos = take_rows(cosine[...], start)
    sin = take_rows(sine[...], start)
    for t in range(TILES):
        lanes = slice(t * LANES, (t + 1) * LANES)
        q = proj[:, t * LANES : (t + 1) * LANES] * SCALE
        q_out[0, t] = (q * cos + rolled(q) * sin).astype(BF16)
        k = proj[:, D + t * LANES : D + (t + 1) * LANES]
        k_out[0, t] = (k * cos + rolled(k) * sin).astype(BF16)
        v_out[0, t] = proj[:, 2 * D + t * LANES : 2 * D + (t + 1) * LANES].astype(BF16)

    key_lanes = key_side(length)
    ones = jnp.ones((L, LANES), BF16)
    query_lanes = jnp.where(lane_iota(LANES, LANES) % HW == 3, 1.0, 0.0).astype(BF16)
    head = lane_iota(LANES, LANES) // HW

    def tile(t, carry):
        for h, part in enumerate(stack_heads(jnp.concatenate([k_out[0, t], key_lanes], axis=1))):
            keys_big[h * L : (h + 1) * L, :] = part
        for h, part in enumerate(stack_heads(jnp.concatenate([v_out[0, t], ones], axis=1))):
            values_big[h * L : (h + 1) * L, :] = part
        for block in range(L // LANES):
            rows = slice(block * LANES, (block + 1) * LANES)
            queries = jnp.concatenate([q_out[0, t, rows, :], query_lanes], axis=1)
            raised = []
            tops = jnp.zeros((LANES, LANES), F32)
            for h in range(GROUP):
                scores = nt(queries, keys_big[h * L : (h + 1) * L, :])
                top = jnp.max(scores, axis=1, keepdims=True)
                raised.append(jnp.exp(scores - top).astype(BF16))
                tops = jnp.where(head == h, top, tops)
            sums = nn(jnp.concatenate(raised, axis=1), values_big[...])
            total = sums[:, LANES:]
            mixed_out[0, t, rows, :] = (sums[:, :LANES] / total).astype(BF16)
            lse_out[0, t, rows, :] = split_lanes(-(tops + jnp.log(total)), 1.0)
        return carry

    lax.fori_loop(0, TILES, tile, 0)


def middle_kernel(
    lengths, x_in, mixed_in, cotangent, w_out, w_up, w_down, vecs, bias_up,
    act_out, grad_mid_out, grad_mixed_out, dots_out,
    g_out, g_up, g_down, g_vecs, g_bias_up, stats,
    a_out, a_up, a_down, a_vecs, a_bias_up,
):
    window = pl.program_id(0)

    @pl.when(window == 0)
    def _():
        for ref in (a_out, a_up, a_down, a_vecs, a_bias_up, stats):
            ref[...] = jnp.zeros_like(ref)

    x = x_in[0].astype(F32)
    mixed = jnp.concatenate([mixed_in[0, t] for t in range(TILES)], axis=1)
    attn = nn(mixed, w_out[...]) + vecs[2:3, :]
    middle = x + attn
    n, inverse = normalize(middle)
    normed = (n * vecs[0:1, :] + vecs[1:2, :]).astype(BF16)
    row = lax.broadcasted_iota(jnp.int32, (L, 1), 0)
    valid = jnp.where(row < lengths[window], 1.0, 0.0)
    grad_result = cotangent[0].astype(F32) * valid
    grad_ffn = grad_result.astype(BF16)
    ffn = jnp.zeros((L, D), F32)
    grad_normed = jnp.zeros((L, D), F32)
    for c in range(FF // D):
        cols = slice(c * D, (c + 1) * D)
        up = w_up[:, cols]
        down = w_down[cols, :]
        pre = nn(normed, up) + bias_up[:, cols]
        phi = 0.5 + 0.5 * lax.erf(pre * math.sqrt(0.5))
        hidden = (pre * phi).astype(BF16)
        slope = phi + pre * (jnp.exp(-0.5 * pre * pre) * (1.0 / math.sqrt(2.0 * math.pi)))
        ffn = ffn + nn(hidden, down)
        grad_pre_f = nt(grad_ffn, down) * slope
        grad_pre = grad_pre_f.astype(BF16)
        a_up[:, cols] += tn(normed, grad_pre)
        a_down[cols, :] += tn(hidden, grad_ffn)
        a_bias_up[:, cols] += col_sum(grad_pre.astype(F32))
        grad_normed = grad_normed + nt(grad_pre, up)
    ffn = ffn + vecs[3:4, :]
    result = middle + ffn
    act_out[0] = result.astype(BF16)
    stats[0:1, :] += col_sum(valid * result * result)
    stats[1:2, :] += col_sum(valid * attn * attn)
    stats[2:3, :] += col_sum(valid * ffn * ffn)
    grad_middle = grad_result + norm_back(grad_normed * vecs[0:1, :], n, inverse)
    grad_mid_out[0] = grad_middle
    grad_attn = grad_middle.astype(BF16)
    a_out[...] += tn(mixed, grad_attn)
    a_vecs[0:1, :] += col_sum(grad_normed * n)
    a_vecs[1:2, :] += col_sum(grad_normed)
    a_vecs[2:3, :] += col_sum(grad_attn.astype(F32))
    a_vecs[3:4, :] += col_sum(grad_ffn.astype(F32))
    grad_mixed = nt(grad_attn, w_out[...]).astype(BF16)
    first = lax.broadcasted_iota(jnp.int32, (LANES, LANES), 0) // HW
    same = jnp.where(first == lane_iota(LANES, LANES) // HW, 1.0, 0.0).astype(BF16)
    for t in range(TILES):
        lanes = slice(t * LANES, (t + 1) * LANES)
        part = grad_mixed[:, lanes]
        grad_mixed_out[0, t] = part
        product = part.astype(F32) * mixed[:, lanes].astype(F32)
        high = product.astype(BF16)
        low = (product - high.astype(F32)).astype(BF16)
        dots_out[0, t] = split_lanes(-(nn(high, same) + nn(low, same)), 0.0)

    @pl.when(window == pl.num_programs(0) - 1)
    def _():
        g_out[...] = a_out[...].astype(g_out.dtype)
        g_up[...] = a_up[...].astype(g_up.dtype)
        g_down[...] = a_down[...].astype(g_down.dtype)
        g_vecs[...] = a_vecs[...]
        g_bias_up[...] = a_bias_up[...]


def back_kernel(
    offsets, lengths, x_in, q_in, k_in, v_in, lse_in, gm_in, dots_in, grad_mid, w_qkv, vecs,
    cosine, sine,
    span_grad, g_qkv, g_vecs, g_bias,
    a_qkv, grad_proj, queries_big, mixed_big, scores_back,
):
    window = pl.program_id(0)
    start = offsets[window]
    length = lengths[window]

    @pl.when(window == 0)
    def _():
        for ref in (a_qkv, g_vecs, g_bias):
            ref[...] = jnp.zeros_like(ref)

    cos = take_rows(cosine[...], start)
    sin = take_rows(sine[...], start)
    key_lanes = key_side(length)
    at = lane_iota(L, LANES) % HW
    value_lanes = jnp.where(at < 3, 1.0, 0.0).astype(BF16)
    for t in range(TILES):
        queries = jnp.concatenate([q_in[0, t], lse_in[0, t]], axis=1)
        for h, part in enumerate(stack_heads(queries)):
            queries_big[h * L : (h + 1) * L, :] = part
        mixed = jnp.concatenate([gm_in[0, t], dots_in[0, t]], axis=1)
        for h, part in enumerate(stack_heads(mixed)):
            mixed_big[h * L : (h + 1) * L, :] = part
        keys = jnp.concatenate([k_in[0, t], key_lanes], axis=1)
        values = jnp.concatenate([v_in[0, t], value_lanes], axis=1)
        for block in range(L // LANES):
            rows = slice(block * LANES, (block + 1) * LANES)
            low_probs = []
            for h in range(GROUP):
                part = slice(h * L, (h + 1) * L)
                probs = jnp.exp(nt(keys[rows, :], queries_big[part, :]))
                back = probs * nt(values[rows, :], mixed_big[part, :])
                scores_back[rows, h * L : (h + 1) * L] = back.astype(BF16)
                low_probs.append(probs.astype(BF16))
            grad_v = nn(jnp.concatenate(low_probs, axis=1), mixed_big[:, :LANES])
            grad_k = nn(scores_back[rows, :], queries_big[:, :LANES])
            grad_k = grad_k * cos[rows, :] - rolled(grad_k) * sin[rows, :]
            grad_proj[rows, D + t * LANES : D + (t + 1) * LANES] = grad_k.astype(BF16)
            grad_proj[rows, 2 * D + t * LANES : 2 * D + (t + 1) * LANES] = grad_v.astype(BF16)
        turned = nn(k_in[0, t].T, scores_back[...])
        grad_q = jnp.concatenate(
            [turned[h * HW : (h + 1) * HW, h * L : (h + 1) * L] for h in range(GROUP)], axis=0
        ).T
        grad_q = (grad_q * cos - rolled(grad_q) * sin) * SCALE
        grad_proj[:, t * LANES : (t + 1) * LANES] = grad_q.astype(BF16)
    x = x_in[0].astype(F32)
    n, inverse = normalize(x)
    normed = (n * vecs[0:1, :] + vecs[1:2, :]).astype(BF16)
    grads = grad_proj[...]
    a_qkv[...] += tn(normed, grads)
    g_bias[...] += col_sum(grads.astype(F32))
    grad_normed = nt(grads, w_qkv[...])
    g_vecs[0:1, :] += col_sum(grad_normed * n)
    g_vecs[1:2, :] += col_sum(grad_normed)
    grad_x = grad_mid[0] + norm_back(grad_normed * vecs[0:1, :], n, inverse)
    wide = jnp.concatenate([grad_x, jnp.zeros((CROP, D), F32)], axis=0)
    span_grad[0] = pltpu.roll(wide, start, 0).astype(BF16)

    @pl.when(window == pl.num_programs(0) - 1)
    def _():
        g_qkv[...] = a_qkv[...].astype(g_qkv.dtype)


def rows_spec(*dims):
    rank = len(dims)
    return pl.BlockSpec((1,) + dims, lambda w, *_: (w,) + (0,) * rank)


def whole_spec(*dims):
    rank = len(dims)
    return pl.BlockSpec(dims, lambda w, *_: (0,) * rank, pipeline_mode=pl.Buffered(1))


def call(kernel, scalars, windows, in_specs, outs, scratch, name):
    return pl.pallas_call(
        kernel,
        out_shape=[jax.ShapeDtypeStruct(shape, dtype) for _, shape, dtype in outs],
        grid_spec=pltpu.PrefetchScalarGridSpec(
            num_scalar_prefetch=scalars,
            grid=(windows,),
            in_specs=in_specs,
            out_specs=[spec for spec, _, _ in outs],
            scratch_shapes=scratch,
        ),
        compiler_params=pltpu.CompilerParams(
            dimension_semantics=("arbitrary",), vmem_limit_bytes=60 * 1024 * 1024
        ),
        name=name,
    )


def gather_rows(shard, cols, devices):
    if shard.shape[0] % cols == 0:
        full = lax.all_gather(shard.reshape(-1, cols), BOTH, axis=0, tiled=True)
        return full
    return lax.all_gather(shard, BOTH, axis=0, tiled=True).reshape(-1, cols)


def rotary_tables():
    inverse = 10000.0 ** (-jnp.arange(0, HW, 2, dtype=F32) / HW)
    angles = jnp.arange(SPAN, dtype=jnp.int32).astype(F32)[:, None] * inverse
    cosine = jnp.tile(jnp.cos(angles), (1, 2 * GROUP))
    sine = jnp.sin(angles)
    sine = jnp.tile(jnp.concatenate([-sine, sine], axis=1), (1, GROUP))
    return cosine, sine


def body(
    span_states,
    offsets,
    lengths,
    cotangent,
    qkv_weight,
    out_weight,
    up_weight,
    down_weight,
    up_bias,
    norm_gains,
    norm_shifts,
    qkv_bias,
    out_biases,
):
    windows = span_states.shape[0]
    wa, an = lax.axis_size("wa"), lax.axis_size("an")
    devices = wa * an
    w_qkv = gather_rows(qkv_weight, 3 * D, devices)
    rest = jnp.concatenate([out_weight, up_weight, down_weight])
    sizes = (out_weight.shape[0], up_weight.shape[0], down_weight.shape[0])
    wide = math.gcd(LANES, *sizes)
    rest = lax.all_gather(rest.reshape(-1, wide), BOTH, axis=0, tiled=False).reshape(devices, -1)
    w_out = rest[:, : sizes[0]].reshape(D, D)
    w_up = rest[:, sizes[0] : sizes[0] + sizes[1]].reshape(D, FF)
    w_down = rest[:, sizes[0] + sizes[1] :].reshape(FF, D)
    bias_up = lax.all_gather(up_bias, BOTH, axis=0, tiled=True).astype(F32).reshape(1, FF)
    small = jnp.concatenate([norm_gains, norm_shifts, qkv_bias, out_biases], axis=0)
    small = lax.all_gather(small, "wa", axis=1, tiled=True).astype(F32)
    vec_one = jnp.stack([small[0], small[2]])
    vec_two = jnp.stack([small[1], small[3], small[7], small[8]])
    bias_qkv = small[4:7].reshape(1, 3 * D)
    cosine, sine = rotary_tables()

    tiled_spec = rows_spec(TILES, L, LANES)
    tiled_shape = (windows, TILES, L, LANES)
    flat_spec = rows_spec(L, D)
    flat_shape = (windows, L, D)
    table_spec = whole_spec(SPAN, LANES)

    tiled_out = (tiled_spec, tiled_shape, BF16)
    x, q, k, v, lse, mixed = call(
        front_kernel,
        2,
        windows,
        [
            rows_spec(SPAN, D),
            whole_spec(D, 3 * D),
            whole_spec(2, D),
            whole_spec(1, 3 * D),
            table_spec,
            table_spec,
        ],
        [(flat_spec, flat_shape, BF16)] + [tiled_out] * 5,
        [
            pltpu.VMEM((L, 3 * D), F32),
            pltpu.VMEM((GROUP * L, 2 * LANES), BF16),
            pltpu.VMEM((GROUP * L, 2 * LANES), BF16),
        ],
        "front",
    )(offsets, lengths, span_states, w_qkv, vec_one, bias_qkv, cosine, sine)

    def kept(shape, dtype):
        return (whole_spec(*shape), shape, dtype)

    (
        activations,
        grad_mid,
        grad_mixed,
        dots,
        g_out,
        g_up,
        g_down,
        g_vec_two,
        g_bias_up,
        stats,
    ) = call(
        middle_kernel,
        1,
        windows,
        [
            flat_spec,
            tiled_spec,
            flat_spec,
            whole_spec(D, D),
            whole_spec(D, FF),
            whole_spec(FF, D),
            whole_spec(4, D),
            whole_spec(1, FF),
        ],
        [
            (flat_spec, flat_shape, BF16),
            (flat_spec, flat_shape, F32),
            tiled_out,
            tiled_out,
            kept((D, D), BF16),
            kept((D, FF), BF16),
            kept((FF, D), BF16),
            kept((4, D), F32),
            kept((1, FF), F32),
            kept((3, D), F32),
        ],
        [
            pltpu.VMEM((D, D), F32),
            pltpu.VMEM((D, FF), F32),
            pltpu.VMEM((FF, D), F32),
            pltpu.VMEM((4, D), F32),
            pltpu.VMEM((1, FF), F32),
        ],
        "middle",
    )(lengths, x, mixed, cotangent, w_out, w_up, w_down, vec_two, bias_up)

    grads = jnp.concatenate(
        [g.reshape(devices, -1, wide) for g in (g_out, g_up, g_down)], axis=1
    )
    rest_shard = lax.psum_scatter(grads, BOTH, scatter_dimension=0, tiled=False)
    rest_shard = rest_shard.reshape(-1).astype(F32)

    span_grad, g_qkv, g_vec_one, g_bias_qkv = call(
        back_kernel,
        2,
        windows,
        [flat_spec]
        + [tiled_spec] * 6
        + [flat_spec, whole_spec(D, 3 * D), whole_spec(2, D), table_spec, table_spec],
        [
            (rows_spec(SPAN, D), (windows, SPAN, D), BF16),
            kept((D, 3 * D), BF16),
            kept((2, D), F32),
            kept((1, 3 * D), F32),
        ],
        [
            pltpu.VMEM((D, 3 * D), F32),
            pltpu.VMEM((L, 3 * D), BF16),
            pltpu.VMEM((GROUP * L, 2 * LANES), BF16),
            pltpu.VMEM((GROUP * L, 2 * LANES), BF16),
            pltpu.VMEM((L, GROUP * L), BF16),
        ],
        "back",
    )(offsets, lengths, x, q, k, v, lse, grad_mixed, dots, grad_mid, w_qkv, vec_one, cosine, sine)

    qkv_shard = lax.psum_scatter(
        g_qkv.reshape(devices, -1, math.gcd(LANES, qkv_weight.shape[0])), BOTH, scatter_dimension=0, tiled=False
    )
    qkv_shard = qkv_shard.reshape(-1).astype(F32)

    token_count = jnp.sum(lengths).astype(F32)
    square = jnp.sum(stats, axis=1)
    tail = jnp.concatenate([square, token_count[None], jnp.zeros((D - 4,), F32)])
    packed = jnp.concatenate(
        [
            g_vec_one,
            g_vec_two,
            g_bias_qkv.reshape(3, D),
            g_bias_up.reshape(FF // D, D),
            tail[None],
        ],
        axis=0,
    )
    packed = lax.psum(packed, BOTH)
    share = D // wa
    first_col = lax.axis_index("wa") * share
    rows = packed[:9]
    rows = lax.dynamic_slice_in_dim(rows, first_col, share, 1)
    up_share = up_bias.shape[0]
    flat_index = lax.axis_index("wa") * an + lax.axis_index("an")
    up_bias_grad = lax.dynamic_slice_in_dim(
        packed[9:13].reshape(FF), flat_index * up_share, up_share, 0
    )
    totals = packed[13]
    root_means = jnp.sqrt(totals[:3] / (totals[3] * D))
    return (
        activations,
        span_grad,
        qkv_shard,
        rest_shard[: sizes[0]],
        rest_shard[sizes[0] : sizes[0] + sizes[1]],
        rest_shard[sizes[0] + sizes[1] :],
        up_bias_grad,
        jnp.stack([rows[0], rows[2]]),
        jnp.stack([rows[1], rows[3]]),
        rows[6:9],
        rows[4:6],
        root_means,
    )


def solution(mesh):
    return jax.shard_map(
        body,
        mesh=mesh,
        in_specs=(
            P(("wa", "an"), None, None),
            P(("wa", "an")),
            P(("wa", "an")),
            P(("wa", "an"), None, None),
            P(("wa", "an")),
            P(("wa", "an")),
            P(("wa", "an")),
            P(("wa", "an")),
            P(("wa", "an")),
            P(None, "wa"),
            P(None, "wa"),
            P(None, "wa"),
            P(None, "wa"),
        ),
        out_specs=(
            P(("wa", "an"), None, None),
            P(("wa", "an"), None, None),
            P(("wa", "an")),
            P(("wa", "an")),
            P(("wa", "an")),
            P(("wa", "an")),
            P(("wa", "an")),
            P(None, "wa"),
            P(None, "wa"),
            P(None, "wa"),
            P(None, "wa"),
            P(),
        ),
        check_vma=False,
    )
```

time: 1600 us -> 697 us (0.44); the launches traced: 1580 us -> 693 us
  local copies, waits for them, and re-layouts: 513 us -> 55.5 us
  matrix products: 380 us -> 0 us
  Pallas kernels: 0 us -> 264 us
  other arithmetic: 227 us -> 14.8 us
  blocking collectives: 204 us -> 114 us
    dot_general x54 -> x0, matrix products: 380 us -> none  [the longest x1 61.5 us: body(): jnp.dot(normed_two_low, w_up, preferred_element_type=jnp.float32) + bias_up]
    dynamic_update_slice x42 -> x0, local copies, waits for them, and re-layouts: 291 us -> none  [body(): lax.map(attend, (queries, key_rows, value_rows, key_mask))]
    pallas_call x0 -> x3, Pallas kernels: none -> 264 us  [the longest x1 104 us: body(): call(back_kernel, 2, windows, [flat_spec] + [tiled_spec] * 6 + [flat_spec...]
    all_gather x5 -> x1, blocking collectives: 120 us -> 32.5 us  [body(): small = lax.all_gather(small, 'wa', axis=1, tiled=True).astype(F32)]
    unnamed x5, waiting for transfers between devices: 236 us -> 158 us
    reduce_sum x16 -> x2, other arithmetic: 74.6 us -> 0.75 us  [the longest x1 0.63 us: body(): token_count = jnp.sum(lengths).astype(F32)]
    reduce_scatter x0 -> x1, waiting for transfers between devices: none -> 70.5 us  [body(): lax.psum_scatter(g_qkv.reshape(devices, -1, math.gcd(LANES, qkv_weight.sh...]
    convert_element_type x17 -> x4, other arithmetic: 61.2 us -> 2.54 us  [the longest x1 1.56 us: body(): qkv_shard = qkv_shard.reshape(-1).astype(F32)]
  transfers between devices with their start and end apart: 4 -> 4, of which waited for: 1 -> 2; matrix products, arithmetic and copies ran while one was open for 23% -> 6% of each run, Pallas kernels for 0% -> 10%
where the time goes in v1:
time: 697 us; the launch traced here: 693 us
  Pallas kernels  264 us (38%)
  waiting for transfers between devices  228 us (33%)
  blocking collectives  114 us (16%)
  local copies, waits for them, and re-layouts  55.5 us (8%)
  between operations  15.5 us (2%)
  other arithmetic  14.8 us (2%)
    unnamed x5, waiting for transfers between devices  158 us
    pallas_call x1, Pallas kernels, body(): call(back_kernel, 2, windows, [flat_spec] + [tiled_spec] * 6 + [flat_spec...  104 us
    pallas_call x1, Pallas kernels, body(): call(middle_kernel, 1, windows, [flat_spec, tiled_spec, flat_spec, whole_...  93.1 us
    reduce_scatter x1, waiting for transfers between devices, body(): lax.psum_scatter(g_qkv.reshape(devices, -1, math.gcd(LANES, qkv_weight.sh...  70.5 us
    pallas_call x1, Pallas kernels, body(): call(front_kernel, 2, windows, [rows_spec(SPAN, D), whole_spec(D, 3 * D),...  67.7 us
    psum x1, blocking collectives, body(): packed = lax.psum(packed, BOTH)  41.3 us
    unnamed x1, blocking collectives  40.1 us
    all_gather x1, blocking collectives, body(): small = lax.all_gather(small, 'wa', axis=1, tiled=True).astype(F32)  32.5 us
  transfers between devices with their start and end apart: 4, of which 2 were waited for; matrix products, arithmetic and copies ran while one was open for 6% of the time, Pallas kernels for 10%

profile of v1, /device:TPU:0, one launch (start us, length us, event | category | flops | bytes accessed | tf_op | source)
XLA Modules:
  0.0 692.6 jit_solution(514573572753216354)
XLA Ops:
  7.2 1.6 reshape.147
  8.9 1.7 maximum_bitcast_fusion
  10.7 0.7 maximum_bitcast_fusion.1
  11.4 32.5 %all-gather.1 = bf16[8,80,9]{1,2,0:T(8,128)(2,1)S(1)} all-gather(bf16[1,80,9]{1,2,0:T(8,128)(2,1)S(1)} %maximum_bitcast_fusion.1), channel_id=1, replica_groups=mesh['wa'=8,'an'=4] {'wa'}, dimensions={0}, use_global_device_ids=true | all-gather | bytes 12960 | tf_op jit(solution)/shard_map/all_gather | solution.py:357
  44.3 0.8 copy.38.sine
  45.2 0.9 copy.37.cosine
  46.7 0.8 dynamic-update-slice
  47.5 40.1 %all-reduce = bf16[2560]{0:T(1024)(128)(2,1)S(1)} all-reduce(bf16[2560]{0:T(1024)(128)(2,1)S(1)} %dynamic-update-slice), channel_id=1, replica_groups=mesh['wa'=8,'an'=4] {'wa','an'}, use_global_device_ids=true, to_apply=%add | all-reduce | flops 2560 | bytes 10240
  89.4 4.2 reshape.148.w_qkv
  93.6 67.7 %front.1 = (bf16[6,384,640]{2,1,0:T(8,128)(2,1)}, bf16[6,5,384,128]{3,2,1,0:T(8,128)(2,1)}, bf16[6,5,384,128]{3,2,1,0:T(8,128)(2,1)}, bf16[6,5,384,128]{3,2,1,0:...) custom-call(s32[6]{0:T(128)} %offsets.3, s32[6]{0:T(128)} %lengths.5, ...), custom_call_target="tpu_custom_call" | custom-call | tf_op jit(solution)/shard_map/front/pallas_call | solution.py:370
  161.4 4.1 copy.45
  165.4 2.1 fusion.3
  167.5 0.9 slice.110
  168.5 7.3 %reshape.131.w_up = bf16[640,2560]{1,0:T(8,128)(2,1)} reshape(bf16[32,51200]{1,0:T(8,128)(2,1)} %get-tuple-element.53) | data formatting | bytes 6553600 | tf_op jit(solution)/shard_map/reshape | solution.py:353
  175.8 2.9 reshape.132.w_down
  178.7 3.1 reshape.130.w_out
  181.8 93.1 %middle.1 = (bf16[6,384,640]{2,1,0:T(8,128)(2,1)}, f32[6,384,640]{2,1,0:T(8,128)}, bf16[6,5,384,128]{3,2,1,0:T(8,128)(2,1)}, bf16[6,5,384,128]{3,2,1,0:T(8,128)(...) custom-call(s32[6]{0:T(128)} %lengths.5, ...), custom_call_target="tpu_custom_call" | custom-call | tf_op jit(solution)/shard_map/middle/pallas_call | solution.py:405
  274.9 103.6 %back.1 = (bf16[6,512,640]{2,1,0:T(8,128)(2,1)}, bf16[640,1920]{1,0:T(8,128)(2,1)}, f32[2,640]{1,0:T(2,128)}, f32[1,1920]{1,0:T(1,128)}) custom-call(s32[6]{0:T(128)} %offsets.3, s32[6]{0:T(128)} %lengths.5, bf16[6,384,640]{2,1,0:T(8,128)(2,1)} %get-tuple-element.32.x_in, bf16[6,5,384,128]{3,2,1,0:T(8,128)(2,1)} %get-tuple-element.35.q_in, ...), custom_call_target="tpu_custom_call" | custom-call | tf_op jit(solution)/shard_map/back/pallas_call | solution.py:447
  378.5 5.5 reshape.135
  384.1 6.2 reshape.137
  390.3 6.5 reshape.138
  396.7 2.4 reshape.136
  399.2 6.4 pad_maximum_fusion
  406.3 0.6 reduce_sum.19
  408.1 41.3 %psum.7 = f32[14,640]{1,0:T(8,128)S(1)} all-reduce(f32[14,640]{1,0:T(8,128)S(1)} %concatenate.23), channel_id=1, replica_groups=mesh['wa'=8,'an'=4] {'wa','an'}, use_global_device_ids=true, to_apply=%region_4.0 | all-reduce | flops 8960 | bytes 71680 | tf_op jit(solution)/shard_map/psum | solution.py:488
  450.0 0.7 dynamic-slice.5
  450.6 0.6 dynamic-slice.6
  453.7 70.5 %reduce-scatter.6.cloned.1.call-done = bf16[1,300,128]{2,1,0:T(8,128)(2,1)} async-done(((bf16[32,300,128]{2,1,0:T(8,128)(2,1)}), bf16[1,300,128]{2,1,0:T(8,128)(2,1)}) %reduce-scatter.6.cloned.1.call-update) | async-done | bytes 76816 | tf_op jit(solution)/shard_map/reduce_scatter | solution.py:470
  524.2 1.6 bitcast_convert_fusion
  525.7 157.8 %reduce-scatter.8.cloned.1.call-done = bf16[1,900,128]{2,1,0:T(8,128)(2,1)} async-done(((bf16[32,900,128]{2,1,0:T(8,128)(2,1)}), bf16[1,900,128]{2,1,0:T(8,128)(2,1)}) %reduce-scatter.8.cloned.1.call-update) | async-done | bytes 230416
  683.5 1.0 convert_element_type.34
  684.5 0.8 slice_bitcast_fusion
  (55 shorter events, 7.1 us)
Async XLA Ops:
  7.2 82.3 %all-gather.7.cloned.1.call-start = ((), (), s32[]{:S(2)}) async-start(), calls=%async_computation.4 | async-start | bytes 3041280 | tf_op jit(solution)/shard_map/all_gather | solution.py:315
  8.9 152.5 %all-gather.5.cloned.1.call-start = ((), (), s32[]{:S(2)}) async-start(), calls=%async_computation.2 | async-start | bytes 7636992 | tf_op jit(solution)/shard_map/all_gather | solution.py:351
  10.7 513.5 %reduce-scatter.6.cloned.1.call-start = ((), (), s32[]{:S(2)}) async-start(), calls=%async_computation.3 | async-start | bytes 2568192 | tf_op jit(solution)/shard_map/reduce_scatter | solution.py:470
  384.0 299.5 %reduce-scatter.8.cloned.1.call-start = ((), (), s32[]{:S(2)}) async-start(), calls=%async_computation.5 | async-start | bytes 7636992
  405.6 0.7 copy-start.5
  405.6 1.9 copy-start.3
  405.6 2.0 copy-start.2
  405.6 2.1 copy-start.1
  405.6 2.3 copy-start
  405.6 2.3 copy-start.4
Sparse Core Ops, SparseCore 0:
  11.4 61.8 all-gather.6
  76.7 71.6 all-gather.4
  384.2 139.9 reduce-scatter.5
  526.3 157.1 reduce-scatter.7

commit v2 on v1

--- a/solution.py
+++ b/solution.py
@@ -1,3 +1,4 @@
+import functools
 import math
 
 import jax
@@ -88,12 +89,41 @@
     return pltpu.roll(full, (SPAN - start) % SPAN, 0)[:L]
 
 
+def unpack_rows(parts, rows, staging, dest):
+    def group(i, carry):
+        for ref, first, col, cols in parts:
+            for j in range(4):
+                low = first // 16 * 16
+                high = min(-(-(first + rows) // 16) * 16, ref.shape[1])
+                block = ref[4 * i + j, low:high, :].astype(F32)
+                staging[j * rows : (j + 1) * rows, col : col + cols] = block[
+                    first - low : first - low + rows
+                ]
+        at = pl.multiple_of(i * 4 * rows, 4 * rows)
+        dest[pl.ds(at, 4 * rows), :] = staging[: 4 * rows, : dest.shape[1]].astype(BF16)
+        return carry
+
+    lax.fori_loop(0, dest.shape[0] // (4 * rows), group, 0)
+
+
 def front_kernel(
-    offsets, lengths, span, w_qkv, vecs, bias_qkv, cosine, sine,
-    x_out, q_out, k_out, v_out, lse_out, mixed_out,
-    proj, keys_big, values_big,
+    rows,
+    offsets, lengths, span, w_first, w_second, vecs, bias_qkv, cosine, sine,
+    x_out, q_out, k_out, v_out, lse_out, mixed_out, w_qkv,
+    proj, keys_big, values_big, staging,
 ):
     window = pl.program_id(0)
+
+    @pl.when(window == 0)
+    def _():
+        if rows:
+            cut = w_first.shape[2]
+            parts = [(w_first, 0, 0, cut), (w_second, 0, cut, 3 * D - cut)]
+            unpack_rows(parts, rows, staging, w_qkv)
+        else:
+            w_qkv[:, : w_first.shape[1]] = w_first[...]
+            w_qkv[:, w_first.shape[1] :] = w_second[...]
+
     start = offsets[window]
     length = lengths[window]
     x = take_rows(span[0].astype(F32), start)
@@ -122,8 +152,8 @@
         for h, part in enumerate(stack_heads(jnp.concatenate([v_out[0, t], ones], axis=1))):
             values_big[h * L : (h + 1) * L, :] = part
         for block in range(L // LANES):
-            rows = slice(block * LANES, (block + 1) * LANES)
-            queries = jnp.concatenate([q_out[0, t, rows, :], query_lanes], axis=1)
+            part = slice(block * LANES, (block + 1) * LANES)
+            queries = jnp.concatenate([q_out[0, t, part, :], query_lanes], axis=1)
             raised = []
             tops = jnp.zeros((LANES, LANES), F32)
             for h in range(GROUP):
@@ -133,25 +163,43 @@
                 tops = jnp.where(head == h, top, tops)
             sums = nn(jnp.concatenate(raised, axis=1), values_big[...])
             total = sums[:, LANES:]
-            mixed_out[0, t, rows, :] = (sums[:, :LANES] / total).astype(BF16)
-            lse_out[0, t, rows, :] = split_lanes(-(tops + jnp.log(total)), 1.0)
+            mixed_out[0, t, part, :] = (sums[:, :LANES] / total).astype(BF16)
+            lse_out[0, t, part, :] = split_lanes(-(tops + jnp.log(total)), 1.0)
         return carry
 
     lax.fori_loop(0, TILES, tile, 0)
 
 
 def middle_kernel(
-    lengths, x_in, mixed_in, cotangent, w_out, w_up, w_down, vecs, bias_up,
+    rows,
+    lengths, x_in, mixed_in, cotangent, packed, vecs, bias_up,
     act_out, grad_mid_out, grad_mixed_out, dots_out,
-    g_out, g_up, g_down, g_vecs, g_bias_up, stats,
-    a_out, a_up, a_down, a_vecs, a_bias_up,
+    g_packed, g_vecs, g_bias_up, stats,
+    w_out, w_up, w_down, a_out, a_up, a_down, staging,
 ):
     window = pl.program_id(0)
 
     @pl.when(window == 0)
     def _():
-        for ref in (a_out, a_up, a_down, a_vecs, a_bias_up, stats):
+        for ref in (a_out, a_up, a_down, g_vecs, g_bias_up, stats):
             ref[...] = jnp.zeros_like(ref)
+        if rows:
+            steps = FF // D
+
+            def copy_down(i, carry):
+                at = pl.multiple_of(i * steps * rows, steps * rows)
+                w_down[pl.ds(at, steps * rows), :] = packed[i, : steps * rows, :]
+                return carry
+
+            lax.fori_loop(0, D // rows, copy_down, 0)
+            parts = [(packed, (steps + c) * rows, c * D, D) for c in range(steps)]
+            unpack_rows(parts, rows, staging, w_up)
+            unpack_rows([(packed, 2 * steps * rows, 0, D)], rows, staging, w_out)
+        else:
+            w_down[...] = packed[:FF, :]
+            for c in range(FF // D):
+                w_up[:, c * D : (c + 1) * D] = packed[FF + c * D : FF + (c + 1) * D, :]
+            w_out[...] = packed[2 * FF :, :]
 
     x = x_in[0].astype(F32)
     mixed = jnp.concatenate([mixed_in[0, t] for t in range(TILES)], axis=1)
@@ -178,7 +226,7 @@
         grad_pre = grad_pre_f.astype(BF16)
         a_up[:, cols] += tn(normed, grad_pre)
         a_down[cols, :] += tn(hidden, grad_ffn)
-        a_bias_up[:, cols] += col_sum(grad_pre.astype(F32))
+        g_bias_up[:, cols] += col_sum(grad_pre.astype(F32))
         grad_normed = grad_normed + nt(grad_pre, up)
     ffn = ffn + vecs[3:4, :]
     result = middle + ffn
@@ -190,10 +238,10 @@
     grad_mid_out[0] = grad_middle
     grad_attn = grad_middle.astype(BF16)
     a_out[...] += tn(mixed, grad_attn)
-    a_vecs[0:1, :] += col_sum(grad_normed * n)
-    a_vecs[1:2, :] += col_sum(grad_normed)
-    a_vecs[2:3, :] += col_sum(grad_attn.astype(F32))
-    a_vecs[3:4, :] += col_sum(grad_ffn.astype(F32))
+    g_vecs[0:1, :] += col_sum(grad_normed * n)
+    g_vecs[1:2, :] += col_sum(grad_normed)
+    g_vecs[2:3, :] += col_sum(grad_attn.astype(F32))
+    g_vecs[3:4, :] += col_sum(grad_ffn.astype(F32))
     grad_mixed = nt(grad_attn, w_out[...]).astype(BF16)
     first = lax.broadcasted_iota(jnp.int32, (LANES, LANES), 0) // HW
     same = jnp.where(first == lane_iota(LANES, LANES) // HW, 1.0, 0.0).astype(BF16)
@@ -208,17 +256,42 @@
 
     @pl.when(window == pl.num_programs(0) - 1)
     def _():
-        g_out[...] = a_out[...].astype(g_out.dtype)
-        g_up[...] = a_up[...].astype(g_up.dtype)
-        g_down[...] = a_down[...].astype(g_down.dtype)
-        g_vecs[...] = a_vecs[...]
-        g_bias_up[...] = a_bias_up[...]
+        steps = FF // D
+        if rows:
+            parts = [((steps + c) * rows, a_up, c * D) for c in range(steps)]
+            parts.append((2 * steps * rows, a_out, 0))
+
+            def group(i, carry):
+                at = pl.multiple_of(i * 2 * rows, 2 * rows)
+                for first, ref, col in parts:
+                    block = ref[pl.ds(at, 2 * rows), col : col + D]
+                    staging[first : first + rows, :D] = block[:rows]
+                    staging[first : first + rows, D : 2 * D] = block[rows:]
+                for j in range(2):
+                    top = pl.multiple_of((2 * i + j) * steps * rows, steps * rows)
+                    g_packed[2 * i + j, : steps * rows, :] = a_down[
+                        pl.ds(top, steps * rows), :
+                    ].astype(BF16)
+                    g_packed[2 * i + j, steps * rows :, :] = staging[
+                        steps * rows : g_packed.shape[1], j * D : (j + 1) * D
+                    ].astype(BF16)
+                return carry
+
+            lax.fori_loop(0, D // (2 * rows), group, 0)
+        else:
+            g_packed[:FF, :] = a_down[...].astype(BF16)
+            for c in range(steps):
+                g_packed[FF + c * D : FF + (c + 1) * D, :] = a_up[
+                    :, c * D : (c + 1) * D
+                ].astype(BF16)
+            g_packed[2 * FF :, :] = a_out[...].astype(BF16)
 
 
 def back_kernel(
+    rows,
     offsets, lengths, x_in, q_in, k_in, v_in, lse_in, gm_in, dots_in, grad_mid, w_qkv, vecs,
     cosine, sine,
-    span_grad, g_qkv, g_vecs, g_bias,
+    span_grad, g_first, g_second, g_vecs, g_bias,
     a_qkv, grad_proj, queries_big, mixed_big, scores_back,
 ):
     window = pl.program_id(0)
@@ -245,19 +318,19 @@
         keys = jnp.concatenate([k_in[0, t], key_lanes], axis=1)
         values = jnp.concatenate([v_in[0, t], value_lanes], axis=1)
         for block in range(L // LANES):
-            rows = slice(block * LANES, (block + 1) * LANES)
+            here = slice(block * LANES, (block + 1) * LANES)
             low_probs = []
             for h in range(GROUP):
-                part = slice(h * L, (h + 1) * L)
-                probs = jnp.exp(nt(keys[rows, :], queries_big[part, :]))
-                back = probs * nt(values[rows, :], mixed_big[part, :])
-                scores_back[rows, h * L : (h + 1) * L] = back.astype(BF16)
+                heads = slice(h * L, (h + 1) * L)
+                probs = jnp.exp(nt(keys[here, :], queries_big[heads, :]))
+                back = probs * nt(values[here, :], mixed_big[heads, :])
+                scores_back[here, h * L : (h + 1) * L] = back.astype(BF16)
                 low_probs.append(probs.astype(BF16))
             grad_v = nn(jnp.concatenate(low_probs, axis=1), mixed_big[:, :LANES])
-            grad_k = nn(scores_back[rows, :], queries_big[:, :LANES])
-            grad_k = grad_k * cos[rows, :] - rolled(grad_k) * sin[rows, :]
-            grad_proj[rows, D + t * LANES : D + (t + 1) * LANES] = grad_k.astype(BF16)
-            grad_proj[rows, 2 * D + t * LANES : 2 * D + (t + 1) * LANES] = grad_v.astype(BF16)
+            grad_k = nn(scores_back[here, :], queries_big[:, :LANES])
+            grad_k = grad_k * cos[here, :] - rolled(grad_k) * sin[here, :]
+            grad_proj[here, D + t * LANES : D + (t + 1) * LANES] = grad_k.astype(BF16)
+            grad_proj[here, 2 * D + t * LANES : 2 * D + (t + 1) * LANES] = grad_v.astype(BF16)
         turned = nn(k_in[0, t].T, scores_back[...])
         grad_q = jnp.concatenate(
             [turned[h * HW : (h + 1) * HW, h * L : (h + 1) * L] for h in range(GROUP)], axis=0
@@ -279,7 +352,22 @@
 
     @pl.when(window == pl.num_programs(0) - 1)
     def _():
-        g_qkv[...] = a_qkv[...].astype(g_qkv.dtype)
+        cut = g_first.shape[-1]
+        if rows:
+
+            def group(i, carry):
+                at = pl.multiple_of(i * 2 * rows, 2 * rows)
+                block = a_qkv[pl.ds(at, 2 * rows), :]
+                for j in range(2):
+                    part = block[j * rows : (j + 1) * rows].astype(BF16)
+                    g_first[2 * i + j] = part[:, :cut]
+                    g_second[2 * i + j] = part[:, cut:]
+                return carry
+
+            lax.fori_loop(0, D // (2 * rows), group, 0)
+        else:
+            g_first[...] = a_qkv[:, :cut].astype(BF16)
+            g_second[...] = a_qkv[:, cut:].astype(BF16)
 
 
 def rows_spec(*dims):
@@ -310,11 +398,54 @@
     )
 
 
-def gather_rows(shard, cols, devices):
-    if shard.shape[0] % cols == 0:
-        full = lax.all_gather(shard.reshape(-1, cols), BOTH, axis=0, tiled=True)
-        return full
-    return lax.all_gather(shard, BOTH, axis=0, tiled=True).reshape(-1, cols)
+def flat_index():
+    return lax.axis_index("wa") * lax.axis_size("an") + lax.axis_index("an")
+
+
+def swap(value, bit, devices):
+    return lax.ppermute(value, BOTH, [(i, i ^ (1 << bit)) for i in range(devices)])
+
+
+def gather_steps(shards, orders, devices):
+    index = flat_index()
+    done = [[] for _ in shards]
+    values = list(shards)
+    for step in range(len(orders[0])):
+        for i, order in enumerate(orders):
+            bit = order[step]
+            mine = values[i]
+            other = swap(mine, bit, devices)
+            low = ((index >> bit) & 1) == 0
+            axis = sum(1 for b in done[i] if b > bit)
+            values[i] = jnp.stack(
+                [jnp.where(low, mine, other), jnp.where(low, other, mine)], axis=axis
+            )
+            done[i].append(bit)
+    return [v.reshape((devices,) + s.shape) for v, s in zip(values, shards)]
+
+
+def scatter_steps(arrays, orders, devices):
+    index = flat_index()
+    bits = devices.bit_length() - 1
+    left = [sorted(range(bits), reverse=True) for _ in arrays]
+    values = [a.reshape((2,) * bits + a.shape[1:]) for a in arrays]
+    for step in range(bits):
+        for i, order in enumerate(orders):
+            bit = order[step]
+            axis = left[i].index(bit)
+            own = (index >> bit) & 1
+            send = lax.dynamic_index_in_dim(values[i], 1 - own, axis, keepdims=False)
+            keep = lax.dynamic_index_in_dim(values[i], own, axis, keepdims=False)
+            got = swap(send.astype(BF16), bit, devices)
+            values[i] = keep.astype(F32) + got.astype(F32)
+            left[i].remove(bit)
+    return values
+
+
+def sum_steps(value, devices):
+    for bit in range(devices.bit_length() - 1):
+        value = value + swap(value, bit, devices)
+    return value
 
 
 def rotary_tables():
@@ -344,17 +475,39 @@
     windows = span_states.shape[0]
     wa, an = lax.axis_size("wa"), lax.axis_size("an")
     devices = wa * an
-    w_qkv = gather_rows(qkv_weight, 3 * D, devices)
-    rest = jnp.concatenate([out_weight, up_weight, down_weight])
-    sizes = (out_weight.shape[0], up_weight.shape[0], down_weight.shape[0])
-    wide = math.gcd(LANES, *sizes)
-    rest = lax.all_gather(rest.reshape(-1, wide), BOTH, axis=0, tiled=False).reshape(devices, -1)
-    w_out = rest[:, : sizes[0]].reshape(D, D)
-    w_up = rest[:, sizes[0] : sizes[0] + sizes[1]].reshape(D, FF)
-    w_down = rest[:, sizes[0] + sizes[1] :].reshape(FF, D)
-    bias_up = lax.all_gather(up_bias, BOTH, axis=0, tiled=True).astype(F32).reshape(1, FF)
+    bits = devices.bit_length() - 1
+    steps = FF // D
+    rows = D // devices if D % (4 * devices) == 0 and devices == 1 << bits else 0
+    cut = 8 * LANES
     small = jnp.concatenate([norm_gains, norm_shifts, qkv_bias, out_biases], axis=0)
-    small = lax.all_gather(small, "wa", axis=1, tiled=True).astype(F32)
+    if rows:
+        down_order = list(range(bits))[::-1]
+        other_order = list(down_order)
+        other_order[-2], other_order[-3] = other_order[-3], other_order[-2]
+        shard = qkv_weight.reshape(rows, 3 * D)
+        extra = jnp.concatenate([small, up_bias.reshape(1, -1)], axis=0)
+        w_first, w_second, extra = gather_steps(
+            [shard[:, :cut], shard[:, cut:], extra],
+            [down_order, other_order, down_order],
+            devices,
+        )
+        small = extra[::an, :-1].transpose(1, 0, 2).reshape(9, D).astype(F32)
+        bias_up = extra[:, -1].astype(F32).reshape(1, FF)
+        up = up_weight.reshape(rows, steps, D).transpose(1, 0, 2).reshape(steps * rows, D)
+        pack_rows = -(-(2 * steps + 1) * rows // 32) * 32
+        pad = jnp.zeros((pack_rows - (2 * steps + 1) * rows, D), BF16)
+        packed = jnp.concatenate([down_weight.reshape(-1, D), up, out_weight.reshape(-1, D), pad])
+        packed = lax.all_gather(packed, BOTH, axis=0, tiled=False)
+    else:
+        w_qkv = lax.all_gather(qkv_weight, BOTH, axis=0, tiled=True).reshape(D, 3 * D)
+        w_first, w_second = w_qkv[:, :cut], w_qkv[:, cut:]
+        small = lax.all_gather(small, "wa", axis=1, tiled=True).astype(F32)
+        bias_up = lax.all_gather(up_bias, BOTH, axis=0, tiled=True).astype(F32).reshape(1, FF)
+        w_down = lax.all_gather(down_weight, BOTH, axis=0, tiled=True).reshape(FF, D)
+        w_up = lax.all_gather(up_weight, BOTH, axis=0, tiled=True)
+        w_up = w_up.reshape(D, steps, D).transpose(1, 0, 2).reshape(FF, D)
+        w_out = lax.all_gather(out_weight, BOTH, axis=0, tiled=True).reshape(D, D)
+        packed = jnp.concatenate([w_down, w_up, w_out], axis=0)
     vec_one = jnp.stack([small[0], small[2]])
     vec_two = jnp.stack([small[1], small[3], small[7], small[8]])
     bias_qkv = small[4:7].reshape(1, 3 * D)
@@ -367,52 +520,42 @@
     table_spec = whole_spec(SPAN, LANES)
 
     tiled_out = (tiled_spec, tiled_shape, BF16)
-    x, q, k, v, lse, mixed = call(
-        front_kernel,
+
+    def kept(shape, dtype):
+        return (whole_spec(*shape), shape, dtype)
+
+    x, q, k, v, lse, mixed, w_qkv = call(
+        functools.partial(front_kernel, rows),
         2,
         windows,
         [
             rows_spec(SPAN, D),
-            whole_spec(D, 3 * D),
+            whole_spec(*w_first.shape),
+            whole_spec(*w_second.shape),
             whole_spec(2, D),
             whole_spec(1, 3 * D),
             table_spec,
             table_spec,
         ],
-        [(flat_spec, flat_shape, BF16)] + [tiled_out] * 5,
+        [(flat_spec, flat_shape, BF16)] + [tiled_out] * 5 + [kept((D, 3 * D), BF16)],
         [
             pltpu.VMEM((L, 3 * D), F32),
             pltpu.VMEM((GROUP * L, 2 * LANES), BF16),
             pltpu.VMEM((GROUP * L, 2 * LANES), BF16),
+            pltpu.VMEM((max(4 * rows, 8), 3 * D), F32),
         ],
         "front",
-    )(offsets, lengths, span_states, w_qkv, vec_one, bias_qkv, cosine, sine)
-
-    def kept(shape, dtype):
-        return (whole_spec(*shape), shape, dtype)
-
-    (
-        activations,
-        grad_mid,
-        grad_mixed,
-        dots,
-        g_out,
-        g_up,
-        g_down,
-        g_vec_two,
-        g_bias_up,
-        stats,
-    ) = call(
-        middle_kernel,
+    )(offsets, lengths, span_states, w_first, w_second, vec_one, bias_qkv, cosine, sine)
+
+    activations, grad_mid, grad_mixed, dots, g_packed, g_vec_two, g_bias_up, stats = call(
+        functools.partial(middle_kernel, rows),
         1,
         windows,
         [
             flat_spec,
             tiled_spec,
             flat_spec,
-            whole_spec(D, D),
-            whole_spec(D, FF),
-            whole_spec(FF, D),
+            whole_spec(*packed.shape),
             whole_spec(4, D),
             whole_spec(1, FF),
         ],
@@ -421,31 +564,43 @@
             (flat_spec, flat_shape, F32),
             tiled_out,
             tiled_out,
-            kept((D, D), BF16),
-            kept((D, FF), BF16),
-            kept((FF, D), BF16),
+            kept(packed.shape, BF16),
             kept((4, D), F32),
             kept((1, FF), F32),
             kept((3, D), F32),
         ],
         [
+            pltpu.VMEM((D, D), BF16),
+            pltpu.VMEM((D, FF), BF16),
+            pltpu.VMEM((FF, D), BF16),
             pltpu.VMEM((D, D), F32),
             pltpu.VMEM((D, FF), F32),
             pltpu.VMEM((FF, D), F32),
-            pltpu.VMEM((4, D), F32),
-            pltpu.VMEM((1, FF), F32),
+            pltpu.VMEM((packed.shape[1] if rows else 8, FF), F32),
         ],
         "middle",
-    )(lengths, x, mixed, cotangent, w_out, w_up, w_down, vec_two, bias_up)
-
-    grads = jnp.concatenate(
-        [g.reshape(devices, -1, wide) for g in (g_out, g_up, g_down)], axis=1
-    )
-    rest_shard = lax.psum_scatter(grads, BOTH, scatter_dimension=0, tiled=False)
-    rest_shard = rest_shard.reshape(-1).astype(F32)
-
-    span_grad, g_qkv, g_vec_one, g_bias_qkv = call(
-        back_kernel,
+    )(lengths, x, mixed, cotangent, packed, vec_two, bias_up)
+
+    if rows:
+        packed_shard = lax.psum_scatter(g_packed, BOTH, scatter_dimension=0, tiled=False)
+        packed_shard = packed_shard.astype(F32)
+        down_grad = packed_shard[: steps * rows].reshape(-1)
+        up_grad = packed_shard[steps * rows : 2 * steps * rows].reshape(steps, rows, D)
+        up_grad = up_grad.transpose(1, 0, 2).reshape(-1)
+        out_grad = packed_shard[2 * steps * rows : (2 * steps + 1) * rows].reshape(-1)
+    else:
+
+        def scatter_flat(grad):
+            flat = grad.reshape(devices, -1)
+            return lax.psum_scatter(flat, BOTH, scatter_dimension=0, tiled=False).astype(F32)
+
+        down_grad = scatter_flat(g_packed[:FF])
+        g_up = g_packed[FF : 2 * FF].reshape(steps, D, D).transpose(1, 0, 2)
+        up_grad = scatter_flat(g_up)
+        out_grad = scatter_flat(g_packed[2 * FF :])
+
+    span_grad, g_first, g_second, g_vec_one, g_bias_qkv = call(
+        functools.partial(back_kernel, rows),
         2,
         windows,
         [flat_spec]
@@ -453,7 +608,8 @@
         + [flat_spec, whole_spec(D, 3 * D), whole_spec(2, D), table_spec, table_spec],
         [
             (rows_spec(SPAN, D), (windows, SPAN, D), BF16),
-            kept((D, 3 * D), BF16),
+            kept(w_first.shape, BF16),
+            kept(w_second.shape, BF16),
             kept((2, D), F32),
             kept((1, 3 * D), F32),
         ],
@@ -467,10 +623,13 @@
         "back",
     )(offsets, lengths, x, q, k, v, lse, grad_mixed, dots, grad_mid, w_qkv, vec_one, cosine, sine)
 
-    qkv_shard = lax.psum_scatter(
-        g_qkv.reshape(devices, -1, math.gcd(LANES, qkv_weight.shape[0])), BOTH, scatter_dimension=0, tiled=False
-    )
-    qkv_shard = qkv_shard.reshape(-1).astype(F32)
+    if rows:
+        g_first, g_second = scatter_steps(
+            [g_first, g_second], [down_order[::-1], other_order[::-1]], devices
+        )
+        qkv_grad = jnp.concatenate([g_first, g_second], axis=1).reshape(-1)
+    else:
+        qkv_grad = scatter_flat(jnp.concatenate([g_first, g_second], axis=1))
 
     token_count = jnp.sum(lengths).astype(F32)
     square = jnp.sum(stats, axis=1)
@@ -485,30 +644,28 @@
         ],
         axis=0,
     )
-    packed = lax.psum(packed, BOTH)
+    packed = sum_steps(packed, devices) if rows else lax.psum(packed, BOTH)
     share = D // wa
     first_col = lax.axis_index("wa") * share
-    rows = packed[:9]
-    rows = lax.dynamic_slice_in_dim(rows, first_col, share, 1)
+    shares = lax.dynamic_slice_in_dim(packed[:9], first_col, share, 1)
     up_share = up_bias.shape[0]
-    flat_index = lax.axis_index("wa") * an + lax.axis_index("an")
     up_bias_grad = lax.dynamic_slice_in_dim(
-        packed[9:13].reshape(FF), flat_index * up_share, up_share, 0
+        packed[9:13].reshape(FF), flat_index() * up_share, up_share, 0
     )
     totals = packed[13]
     root_means = jnp.sqrt(totals[:3] / (totals[3] * D))
     return (
         activations,
         span_grad,
-        qkv_shard,
-        rest_shard[: sizes[0]],
-        rest_shard[sizes[0] : sizes[0] + sizes[1]],
-        rest_shard[sizes[0] + sizes[1] :],
+        qkv_grad,
+        out_grad,
+        up_grad,
+        down_grad,
         up_bias_grad,
-        jnp.stack([rows[0], rows[2]]),
-        jnp.stack([rows[1], rows[3]]),
-        rows[6:9],
-        rows[4:6],
+        jnp.stack([shares[0], shares[2]]),
+        jnp.stack([shares[1], shares[3]]),
+        shares[6:9],
+        shares[4:6],
         root_means,
     )
 

time: 697 us -> 416 us (0.60)
  waiting for transfers between devices: 228 us -> 61.2 us
  blocking collectives: 114 us -> 0 us
  starting transfers between devices: 0.16 us -> 35.2 us
  local copies, waits for them, and re-layouts: 55.5 us -> 26.1 us
    unnamed x5 -> x2, waiting for transfers between devices: 158 us -> 0.03 us
    reduce_scatter x1, waiting for transfers between devices: 70.5 us -> 0.01 us  [body(): lax.psum_scatter(g_packed, BOTH, scatter_dimension=0, tiled=False)]
    ppermute x0 -> x30, waiting for transfers between devices: none -> 61.2 us  [swap(): lax.ppermute(value, BOTH, [(i, i ^ 1 << bit) for i in range(devices)])]
    psum x1 -> x0, blocking collectives: 41.3 us -> none  [body(): packed = lax.psum(packed, BOTH)]
    unnamed x1 -> x0, blocking collectives: 40.1 us -> none
    ppermute x0 -> x30, starting transfers between devices: none -> 35.1 us  [swap(): lax.ppermute(value, BOTH, [(i, i ^ 1 << bit) for i in range(devices)])]
    all_gather x1 -> x0, blocking collectives: 32.5 us -> none  [body(): small = lax.all_gather(small, 'wa', axis=1, tiled=True).astype(F32)]
    reshape x8 -> x11, local copies, waits for them, and re-layouts: 34.5 us -> 6.34 us  [the longest x2 1 us: body(): up_weight.reshape(rows, steps, D).transpose(1, 0, 2)]
  transfers between devices with their start and end apart: 4 -> 32, of which waited for: 2 -> 21; matrix products, arithmetic and copies ran while one was open for 6% -> 7% of each run, Pallas kernels for 10% -> 40%
where the time goes in v2:
time: 416 us; the launch traced here: 408 us
  Pallas kernels  259 us (62%)
  waiting for transfers between devices  61.2 us (15%)
  starting transfers between devices  35.2 us (8%)
  local copies, waits for them, and re-layouts  26.1 us (6%)
  between operations  16.3 us (4%)
  other arithmetic  10.1 us (2%)
    pallas_call x1, Pallas kernels, body(): call(functools.partial(middle_kernel, rows), 1, windows, [flat_spec, tile...  95.4 us
    pallas_call x1, Pallas kernels, body(): call(functools.partial(back_kernel, rows), 2, windows, [flat_spec] + [til...  94.1 us
    pallas_call x1, Pallas kernels, body(): call(functools.partial(front_kernel, rows), 2, windows, [rows_spec(SPAN,...  69.6 us
    ppermute x30, waiting for transfers between devices, swap(): lax.ppermute(value, BOTH, [(i, i ^ 1 << bit) for i in range(devices)])  61.2 us
    ppermute x30, starting transfers between devices, swap(): lax.ppermute(value, BOTH, [(i, i ^ 1 << bit) for i in range(devices)])  35.1 us
  transfers between devices with their start and end apart: 32, of which 21 were waited for; matrix products, arithmetic and copies ran while one was open for 7% of the time, Pallas kernels for 40%

profile of v2, /device:TPU:0, one launch (start us, length us, event | category | flops | bytes accessed | tf_op | source)
XLA Modules:
  0.0 408.1 jit_solution(13805400792878529280)
XLA Ops:
  11.3 4.1 %collective-permute-start.10 = (bf16[10,80]{1,0:T(8,128)(2,1)S(1)}, bf16[10,80]{1,0:T(8,128)(2,1)S(1)}, u32[]{:S(2)}, u32[]{:S(2)}) collective-permute-start(bf16[10,80]{1,0:T(8,128)(2,1)S(1)} %concatenate.18), channel_id=1, source_target_pairs={{0,16},{1,17},{2,18},{3,19},{4,20},{5,21},{6,22},{7,23},{8,24},{9,... | collective-permute-start | bytes 4808 | tf_op jit(solution)/shard_map/ppermute | solution.py:406
  15.6 2.9 collective-permute-start
  18.5 1.6 collective-permute-start.11
  20.2 2.5 collective-permute-done.11
  22.7 1.6 collective-permute-start.12
  24.5 2.3 collective-permute-done.12
  26.8 1.6 collective-permute-start.13
  33.4 3.4 collective-permute-done.6
  36.9 1.6 collective-permute-start.7
  40.1 4.8 %collective-permute-done.7 = bf16[2,2,20,896]{3,2,0,1:T(8,128)(2,1)S(1)} collective-permute-done((bf16[2,2,20,896]{3,2,0,1:T(8,128)(2,1)S(1)}, bf16[2,2,20,896]{3,2,0,1:T(8,128)(2,1)S(1)}, u32[]{:S(2)}, u32[]{:S(2)}) %collective-permute-start.7) | collective-permute-done | bytes 143392 | tf_op jit(solution)/shard_map/ppermute | solution.py:406
  45.2 5.5 %collective-permute-done.2 = bf16[2,2,20,1024]{3,2,0,1:T(8,128)(2,1)S(1)} collective-permute-done((bf16[2,2,20,1024]{3,2,0,1:T(8,128)(2,1)S(1)}, bf16[2,2,20,1024]{3,2,0,1:T(8,128)(2,1)S(1)}, u32[]{:S(2)}, u32[]{:S(2)}) %collective-permute-start.2) | collective-permute-done | bytes 163872 | tf_op jit(solution)/shard_map/ppermute | solution.py:406
  50.8 1.6 collective-permute-start.3
  52.4 7.5 %collective-permute-done.8 = bf16[2,2,2,20,896]{4,3,0,1,2:T(8,128)(2,1)S(1)} collective-permute-done((bf16[2,2,2,20,896]{4,3,0,1,2:T(8,128)(2,1)S(1)}, bf16[2,2,2,20,896]{4,3,0,1,2:T(8,128)(2,1)S(1)}, u32[]{:S(2)}, u32[]{:S(2)}) %collective-permute-start.8) | collective-permute-done | bytes 286752 | tf_op jit(solution)/shard_map/ppermute | solution.py:406
  69.6 69.6 %front.1 = (bf16[6,384,640]{2,1,0:T(8,128)(2,1)}, bf16[6,5,384,128]{3,2,1,0:T(8,128)(2,1)}, bf16[6,5,384,128]{3,2,1,0:T(8,128)(2,1)}, bf16[6,5,384,128]{3,2,1,0:...) custom-call(s32[6]{0:T(128)} %offsets.3, s32[6]{0:T(128)} %lengths.5, ...), custom_call_target="tpu_custom_call" | custom-call | tf_op jit(solution)/shard_map/front/pallas_call | solution.py:527
  139.3 95.4 %middle.1 = (bf16[6,384,640]{2,1,0:T(8,128)(2,1)}, f32[6,384,640]{2,1,0:T(8,128)}, bf16[6,5,384,128]{3,2,1,0:T(8,128)(2,1)}, bf16[6,5,384,128]{3,2,1,0:T(8,128)(...) custom-call(s32[6]{0:T(128)} %lengths.5, ...), custom_call_target="tpu_custom_call" | custom-call | tf_op jit(solution)/shard_map/middle/pallas_call | solution.py:550
  236.7 94.1 %back.1 = (bf16[6,512,640]{2,1,0:T(8,128)(2,1)}, bf16[32,20,1024]{2,1,0:T(8,128)(2,1)}, bf16[32,20,896]{2,1,0:T(8,128)(2,1)}, f32[2,640]{1,0:T(2,128)}, f32[1,1920]{1,0:T(1,128)}) custom-call(s32[6]{0:T(128)} %offsets.3, s32[6]{0:T(128)} %lengths.5, bf16[6,384,640]{2,1,0:T(8,128)(2,1)} %get-tuple-element.32.x_in, ...), custom_call_target="tpu_custom_call" | custom-call | tf_op jit(solution)/shard_map/back/pallas_call | solution.py:602
  333.9 1.5 collective-permute-start.26
  335.4 2.5 collective-permute-done.26
  339.2 2.8 collective-permute-done.27
  342.7 1.6 constant_dynamic-slice_fusion.1
  345.5 1.6 collective-permute-done.28
  348.3 5.1 %collective-permute-done.29 = f32[14,640]{1,0:T(8,128)S(1)} collective-permute-done((f32[14,640]{1,0:T(8,128)S(1)}, f32[14,640]{1,0:T(8,128)S(1)}, u32[]{:S(2)}, u32[]{:S(2)}) %collective-permute-start.29) | collective-permute-done | bytes 35872 | tf_op jit(solution)/shard_map/ppermute | solution.py:406
  363.6 1.7 collective-permute-done.21
  365.4 3.0 collective-permute-start.22
  368.4 3.1 collective-permute-done.16
  373.8 4.2 %collective-permute-done.23 = bf16[2,20,896]{2,1,0:T(8,128)(2,1)S(1)} collective-permute-done((bf16[2,20,896]{2,1,0:T(8,128)(2,1)S(1)}, bf16[2,20,896]{2,1,0:T(8,128)(2,1)S(1)}, u32[]{:S(2)}, u32[]{:S(2)}) %collective-permute-start.23) | collective-permute-done | bytes 71712 | tf_op jit(solution)/shard_map/ppermute | solution.py:406
  380.7 2.7 collective-permute-done.24
  383.4 2.1 collective-permute-done.17
  386.0 2.1 collective-permute-start.18
  388.3 2.8 collective-permute-done.18
  391.3 1.7 collective-permute-start.19
  393.1 3.3 collective-permute-done.19
  (192 shorter events, 49.9 us)
Async XLA Ops:
  7.2 132.1 %all-gather.3.cloned.1.call-start = ((), (), s32[]{:S(2)}) async-start(), calls=%async_computation.2 | async-start | bytes 8110080 | tf_op jit(solution)/shard_map/all_gather | solution.py:500
  11.0 386.1 %reduce-scatter.2.cloned.1.call-start = ((), (), s32[]{:S(2)}) async-start(), calls=%async_computation.1 | async-start | bytes 8110080 | tf_op jit(solution)/shard_map/reduce_scatter | solution.py:585
  11.3 7.3 %collective-permute-start.10 = (bf16[10,80]{1,0:T(8,128)(2,1)S(1)}, bf16[10,80]{1,0:T(8,128)(2,1)S(1)}, u32[]{:S(2)}, u32[]{:S(2)}) collective-permute-start(bf16[10,80]{1,0:T(8,128)(2,1)S(1)} %concatenate.18), channel_id=1, source_target_pairs={{0,16},{1,17},{2,18},{3,19},{4,20},{5,21},{6,22},{7,23},{8,24},{9,... | collective-permute-start | bytes 4808 | tf_op jit(solution)/shard_map/ppermute | solution.py:406
  15.5 15.4 %collective-permute-start.5 = (bf16[20,896]{1,0:T(8,128)(2,1)S(1)}, bf16[20,896]{1,0:T(8,128)(2,1)S(1)}, u32[]{:S(2)}, u32[]{:S(2)}) collective-permute-start(bf16[20,896]{1,0:T(8,128)(2,1)S(1)} %slice.124), channel_id=1, source_target_pairs={{0,16},{1,17},{2,18},{3,19},{4,20},{5,21},{6,22},{7,23},{8,24},{9,... | collective-permute-start | bytes 107528 | tf_op jit(solution)/shard_map/ppermute | solution.py:406
  15.6 16.5 %collective-permute-start = (bf16[20,1024]{1,0:T(8,128)(2,1)S(1)}, bf16[20,1024]{1,0:T(8,128)(2,1)S(1)}, u32[]{:S(2)}, u32[]{:S(2)}) collective-permute-start(bf16[20,1024]{1,0:T(8,128)(2,1)S(1)} %slice.123), channel_id=1, source_target_pairs={{0,16},{1,17},{2,18},{3,19},{4,20},{5,21},{6,22},{7,23},{8,24},{9,... | collective-permute-start | bytes 122888 | tf_op jit(solution)/shard_map/ppermute | solution.py:406
  18.5 4.2 %collective-permute-start.11 = (bf16[2,10,80]{2,1,0:T(8,128)(2,1)S(1)}, bf16[2,10,80]{2,1,0:T(8,128)(2,1)S(1)}, u32[]{:S(2)}, u32[]{:S(2)}) collective-permute-start(bf16[2,10,80]{2,1,0:T(8,128)(2,1)S(1)} %pad_maximum_fusion.17), channel_id=1, source_target_pairs={{0,8},{1,9},{2,10},{3,11},{4,12},{5,13},{6,14},{7,15},{8,0},{9,1},... | collective-permute-start | bytes 9608 | tf_op jit(solution)/shard_map/ppermute | solution.py:406
  22.7 4.1 %collective-permute-start.12 = (bf16[2,2,10,80]{3,2,0,1:T(8,128)(2,1)S(1)}, bf16[2,2,10,80]{3,2,0,1:T(8,128)(2,1)S(1)}, u32[]{:S(2)}, u32[]{:S(2)}) collective-permute-start(bf16[2,2,10,80]{3,2,0,1:T(8,128)(2,1)S(1)} %pad_maximum_fusion.15), channel_id=1, source_target_pairs={{0,4},{1,5},{2,6},{3,7},{4,0},{5,1},{6,2},{7,3},{8,12},{9,13},{10,... | collective-permute-start | bytes 19208 | tf_op jit(solution)/shard_map/ppermute | solution.py:406
  26.8 4.0 collective-permute-start.13
  30.9 2.3 collective-permute-start.14
  31.0 5.9 %collective-permute-start.6 = (bf16[2,20,896]{2,1,0:T(8,128)(2,1)S(1)}, bf16[2,20,896]{2,1,0:T(8,128)(2,1)S(1)}, u32[]{:S(2)}, u32[]{:S(2)}) collective-permute-start(bf16[2,20,896]{2,1,0:T(8,128)(2,1)S(1)} %pad_maximum_fusion.11), channel_id=1, source_target_pairs={{0,8},{1,9},{2,10},{3,11},{4,12},{5,13},{6,14},{7,15},{8,0},{9,1},... | collective-permute-start | bytes 215048 | tf_op jit(solution)/shard_map/ppermute | solution.py:406
  32.2 6.6 %collective-permute-start.1 = (bf16[2,20,1024]{2,1,0:T(8,128)(2,1)S(1)}, bf16[2,20,1024]{2,1,0:T(8,128)(2,1)S(1)}, u32[]{:S(2)}, u32[]{:S(2)}) collective-permute-start(bf16[2,20,1024]{2,1,0:T(8,128)(2,1)S(1)} %pad_maximum_fusion.10), channel_id=1, source_target_pairs={{0,8},{1,9},{2,10},{3,11},{4,12},{5,13},{6,14},{7,15},{8,0},{9,1},... | collective-permute-start | bytes 245768 | tf_op jit(solution)/shard_map/ppermute | solution.py:406
  36.9 8.0 %collective-permute-start.7 = (bf16[2,2,20,896]{3,2,0,1:T(8,128)(2,1)S(1)}, bf16[2,2,20,896]{3,2,0,1:T(8,128)(2,1)S(1)}, u32[]{:S(2)}, u32[]{:S(2)}) collective-permute-start(bf16[2,2,20,896]{3,2,0,1:T(8,128)(2,1)S(1)} %pad_maximum_fusion.8), channel_id=1, source_target_pairs={{0,2},{1,3},{2,0},{3,1},{4,6},{5,7},{6,4},{7,5},{8,10},{9,11},{10,... | collective-permute-start | bytes 430088 | tf_op jit(solution)/shard_map/ppermute | solution.py:406
  38.8 11.9 %collective-permute-start.2 = (bf16[2,2,20,1024]{3,2,0,1:T(8,128)(2,1)S(1)}, bf16[2,2,20,1024]{3,2,0,1:T(8,128)(2,1)S(1)}, u32[]{:S(2)}, u32[]{:S(2)}) collective-permute-start(bf16[2,2,20,1024]{3,2,0,1:T(8,128)(2,1)S(1)} %pad_maximum_fusion.6), channel_id=1, source_target_pairs={{0,4},{1,5},{2,6},{3,7},{4,0},{5,1},{6,2},{7,3},{8,12},{9,13},{10,... | collective-permute-start | bytes 491528 | tf_op jit(solution)/shard_map/ppermute | solution.py:406
  45.0 14.9 %collective-permute-start.8 = (bf16[2,2,2,20,896]{4,3,0,1,2:T(8,128)(2,1)S(1)}, bf16[2,2,2,20,896]{4,3,0,1,2:T(8,128)(2,1)S(1)}, u32[]{:S(2)}, u32[]{:S(2)}) collective-permute-start(bf16[2,2,2,20,896]{4,3,0,1,2:T(8,128)(2,1)S(1)} %pad_maximum_fusion.5), channel_id=1, source_target_pairs={{0,4},{1,5},{2,6},{3,7},{4,0},{5,1},{6,2},{7,3},{8,12},{9,13},{10,... | collective-permute-start | bytes 860168 | tf_op jit(solution)/shard_map/ppermute | solution.py:406
  50.8 9.9 %collective-permute-start.3 = (bf16[2,2,2,20,1024]{4,3,0,1,2:T(8,128)(2,1)S(1)}, bf16[2,2,2,20,1024]{4,3,0,1,2:T(8,128)(2,1)S(1)}, u32[]{:S(2)}, u32[]{:S(2)}) collective-permute-start(bf16[2,2,2,20,1024]{4,3,0,1,2:T(8,128)(2,1)S(1)} %pad_maximum_fusion.4), channel_id=1, source_target_pairs={{0,2},{1,3},{2,0},{3,1},{4,6},{5,7},{6,4},{7,5},{8,10},{9,11},{10,... | collective-permute-start | bytes 983048 | tf_op jit(solution)/shard_map/ppermute | solution.py:406
  60.6 4.5 %collective-permute-start.9 = (bf16[2,2,2,2,20,896]{5,3,4,2,1,0:T(2,128)(2,1)S(1)}, bf16[2,2,2,2,20,896]{5,3,4,2,1,0:T(2,128)(2,1)}, u32[]{:S(2)}, u32[]{:S(2)}) collective-permute-start(bf16[2,2,2,2,20,896]{5,3,4,2,1,0:T(2,128)(2,1)S(1)} %copy.154), channel_id=1, source_target_pairs={{0,1},{1,0},{2,3},{3,2},{4,5},{5,4},{6,7},{7,6},{8,9},{9,8},{10,11... | collective-permute-start | bytes 1720328 | tf_op jit(solution)/shard_map/ppermute | solution.py:406
  61.6 6.3 %collective-permute-start.4 = (bf16[2,2,2,2,20,1024]{5,3,4,2,1,0:T(2,128)(2,1)S(1)}, bf16[2,2,2,2,20,1024]{5,3,4,2,1,0:T(2,128)(2,1)S(1)}, u32[]{:S(2)}, u32[]{:S(2)}) collective-permute-start(bf16[2,2,2,2,20,1024]{5,3,4,2,1,0:T(2,128)(2,1)S(1)} %copy.150), channel_id=1, source_target_pairs={{0,1},{1,0},{2,3},{3,2},{4,5},{5,4},{6,7},{7,6},{8,9},{9,8},{10,11... | collective-permute-start | bytes 1966088 | tf_op jit(solution)/shard_map/ppermute | solution.py:406
  332.7 1.3 collective-permute-start.25
  333.9 4.0 collective-permute-start.26
  338.0 4.0 collective-permute-start.27
  342.0 5.2 %collective-permute-start.28 = (f32[14,640]{1,0:T(8,128)S(1)}, f32[14,640]{1,0:T(8,128)S(1)}, u32[]{:S(2)}, u32[]{:S(2)}) collective-permute-start(f32[14,640]{1,0:T(8,128)S(1)} %add.136), channel_id=1, source_target_pairs={{0,8},{1,9},{2,10},{3,11},{4,12},{5,13},{6,14},{7,15},{8,0},{9,1},... | collective-permute-start | bytes 107528 | tf_op jit(solution)/shard_map/ppermute | solution.py:406
  345.5 12.3 %collective-permute-start.20 = (bf16[2,2,2,2,20,896]{5,3,4,2,1,0:T(2,128)(2,1)}, bf16[2,2,2,2,20,896]{5,3,4,2,1,0:T(2,128)(2,1)S(1)}, u32[]{:S(2)}, u32[]{:S(2)}) collective-permute-start(bf16[2,2,2,2,20,896]{5,3,4,2,1,0:T(2,128)(2,1)} %bitcast.126), channel_id=1, source_target_pairs={{0,1},{1,0},{2,3},{3,2},{4,5},{5,4},{6,7},{7,6},{8,9},{9,8},{10,11... | collective-permute-start | bytes 1720328 | tf_op jit(solution)/shard_map/ppermute | solution.py:406
  347.2 6.3 %collective-permute-start.29 = (f32[14,640]{1,0:T(8,128)S(1)}, f32[14,640]{1,0:T(8,128)S(1)}, u32[]{:S(2)}, u32[]{:S(2)}) collective-permute-start(f32[14,640]{1,0:T(8,128)S(1)} %add.137), channel_id=1, source_target_pairs={{0,16},{1,17},{2,18},{3,19},{4,20},{5,21},{6,22},{7,23},{8,24},{9,... | collective-permute-start | bytes 107528 | tf_op jit(solution)/shard_map/ppermute | solution.py:406
  348.0 11.3 %collective-permute-start.15 = (bf16[2,2,2,2,20,1024]{5,3,4,2,1,0:T(2,128)(2,1)S(1)}, bf16[2,2,2,2,20,1024]{5,3,4,2,1,0:T(2,128)(2,1)S(1)}, u32[]{:S(2)}, u32[]{:S(2)}) collective-permute-start(bf16[2,2,2,2,20,1024]{5,3,4,2,1,0:T(2,128)(2,1)S(1)} %bitcast.140), channel_id=1, source_target_pairs={{0,1},{1,0},{2,3},{3,2},{4,5},{5,4},{6,7},{7,6},{8,9},{9,8},{10,11... | collective-permute-start | bytes 1966088 | tf_op jit(solution)/shard_map/ppermute | solution.py:406
  358.0 7.3 %collective-permute-start.21 = (bf16[2,2,2,20,896]{4,3,0,1,2:T(8,128)(2,1)S(1)}, bf16[2,2,2,20,896]{4,3,0,1,2:T(8,128)(2,1)S(1)}, u32[]{:S(2)}, u32[]{:S(2)}) collective-permute-start(bf16[2,2,2,20,896]{4,3,0,1,2:T(8,128)(2,1)S(1)} %fusion), channel_id=1, source_target_pairs={{0,4},{1,5},{2,6},{3,7},{4,0},{5,1},{6,2},{7,3},{8,12},{9,13},{10,... | collective-permute-start | bytes 860168 | tf_op jit(solution)/shard_map/ppermute | solution.py:406
  361.4 10.1 %collective-permute-start.16 = (bf16[2,2,2,20,1024]{4,2,3,1,0:T(2,128)(2,1)S(1)}, bf16[2,2,2,20,1024]{4,2,3,1,0:T(2,128)(2,1)S(1)}, u32[]{:S(2)}, u32[]{:S(2)}) collective-permute-start(bf16[2,2,2,20,1024]{4,2,3,1,0:T(2,128)(2,1)S(1)} %bitcast.142), channel_id=1, source_target_pairs={{0,2},{1,3},{2,0},{3,1},{4,6},{5,7},{6,4},{7,5},{8,10},{9,11},{10,... | collective-permute-start | bytes 983048 | tf_op jit(solution)/shard_map/ppermute | solution.py:406
  365.4 8.0 %collective-permute-start.22 = (bf16[2,2,20,896]{3,2,0,1:T(8,128)(2,1)S(1)}, bf16[2,2,20,896]{3,2,0,1:T(8,128)(2,1)S(1)}, u32[]{:S(2)}, u32[]{:S(2)}) collective-permute-start(bf16[2,2,20,896]{3,2,0,1:T(8,128)(2,1)S(1)} %fusion.1), channel_id=1, source_target_pairs={{0,2},{1,3},{2,0},{3,1},{4,6},{5,7},{6,4},{7,5},{8,10},{9,11},{10,... | collective-permute-start | bytes 430088 | tf_op jit(solution)/shard_map/ppermute | solution.py:406
  373.4 4.6 %collective-permute-start.23 = (bf16[2,20,896]{2,1,0:T(8,128)(2,1)S(1)}, bf16[2,20,896]{2,1,0:T(8,128)(2,1)S(1)}, u32[]{:S(2)}, u32[]{:S(2)}) collective-permute-start(bf16[2,20,896]{2,1,0:T(8,128)(2,1)S(1)} %fusion.2), channel_id=1, source_target_pairs={{0,8},{1,9},{2,10},{3,11},{4,12},{5,13},{6,14},{7,15},{8,0},{9,1},... | collective-permute-start | bytes 215048 | tf_op jit(solution)/shard_map/ppermute | solution.py:406
  378.0 5.3 %collective-permute-start.24 = (bf16[20,896]{1,0:T(8,128)(2,1)S(1)}, bf16[20,896]{1,0:T(8,128)(2,1)S(1)}, u32[]{:S(2)}, u32[]{:S(2)}) collective-permute-start(bf16[20,896]{1,0:T(8,128)(2,1)S(1)} %fusion.3), channel_id=1, source_target_pairs={{0,16},{1,17},{2,18},{3,19},{4,20},{5,21},{6,22},{7,23},{8,24},{9,... | collective-permute-start | bytes 107528 | tf_op jit(solution)/shard_map/ppermute | solution.py:406
  380.0 5.4 %collective-permute-start.17 = (bf16[2,2,20,1024]{3,1,2,0:T(2,128)(2,1)S(1)}, bf16[2,2,20,1024]{3,1,2,0:T(2,128)(2,1)S(1)}, u32[]{:S(2)}, u32[]{:S(2)}) collective-permute-start(bf16[2,2,20,1024]{3,1,2,0:T(2,128)(2,1)S(1)} %bitcast.143), channel_id=1, source_target_pairs={{0,4},{1,5},{2,6},{3,7},{4,0},{5,1},{6,2},{7,3},{8,12},{9,13},{10,... | collective-permute-start | bytes 491528 | tf_op jit(solution)/shard_map/ppermute | solution.py:406
  386.0 5.0 %collective-permute-start.18 = (bf16[2,20,1024]{2,0,1:T(2,128)(2,1)S(1)}, bf16[2,20,1024]{2,0,1:T(2,128)(2,1)S(1)}, u32[]{:S(2)}, u32[]{:S(2)}) collective-permute-start(bf16[2,20,1024]{2,0,1:T(2,128)(2,1)S(1)} %bitcast.146), channel_id=1, source_target_pairs={{0,8},{1,9},{2,10},{3,11},{4,12},{5,13},{6,14},{7,15},{8,0},{9,1},... | collective-permute-start | bytes 245768 | tf_op jit(solution)/shard_map/ppermute | solution.py:406
  391.3 5.1 %collective-permute-start.19 = (bf16[20,1024]{1,0:T(8,128)(2,1)S(1)}, bf16[20,1024]{1,0:T(8,128)(2,1)S(1)}, u32[]{:S(2)}, u32[]{:S(2)}) collective-permute-start(bf16[20,1024]{1,0:T(8,128)(2,1)S(1)} %bitcast.150), channel_id=1, source_target_pairs={{0,16},{1,17},{2,18},{3,19},{4,20},{5,21},{6,22},{7,23},{8,24},{9,... | collective-permute-start | bytes 122888 | tf_op jit(solution)/shard_map/ppermute | solution.py:406
  (11 other events, 317.8 us)
Sparse Core Ops, SparseCore 0:
  11.1 84.7 all-gather.2
  234.9 122.5 reduce-scatter.1

commit v3 on v2

--- a/solution.py
+++ b/solution.py
@@ -19,6 +19,7 @@
 TILES = D // LANES
 GROUP = LANES // HW
 SCALE = HW**-0.5
+CHUNK = 512
 F32 = jnp.float32
 BF16 = jnp.bfloat16
 BOTH = ("wa", "an")
@@ -172,17 +173,21 @@
 
 def middle_kernel(
     rows,
-    lengths, x_in, mixed_in, cotangent, packed, vecs, bias_up,
+    lengths, x_in, mixed_in, cotangent, packed_hbm, vecs, bias_up,
     act_out, grad_mid_out, grad_mixed_out, dots_out,
     g_packed, g_vecs, g_bias_up, stats,
-    w_out, w_up, w_down, a_out, a_up, a_down, staging,
+    w_out, w_up, w_down, a_out, a_up, a_down, staging, arrived,
 ):
     window = pl.program_id(0)
+    packed = g_packed
 
     @pl.when(window == 0)
     def _():
         for ref in (a_out, a_up, a_down, g_vecs, g_bias_up, stats):
             ref[...] = jnp.zeros_like(ref)
+        fetch = pltpu.make_async_copy(packed_hbm, packed, arrived)
+        fetch.start()
+        fetch.wait()
         if rows:
             steps = FF // D
 
@@ -201,20 +206,30 @@
                 w_up[:, c * D : (c + 1) * D] = packed[FF + c * D : FF + (c + 1) * D, :]
             w_out[...] = packed[2 * FF :, :]
 
-    x = x_in[0].astype(F32)
-    mixed = jnp.concatenate([mixed_in[0, t] for t in range(TILES)], axis=1)
+    count = x_in.shape[0]
+    height = count * L
+    x = x_in[...].reshape(height, D).astype(F32)
+    mixed = jnp.concatenate(
+        [
+            jnp.concatenate([mixed_in[w, t] for t in range(TILES)], axis=1)
+            for w in range(count)
+        ],
+        axis=0,
+    )
     attn = nn(mixed, w_out[...]) + vecs[2:3, :]
     middle = x + attn
     n, inverse = normalize(middle)
     normed = (n * vecs[0:1, :] + vecs[1:2, :]).astype(BF16)
     row = lax.broadcasted_iota(jnp.int32, (L, 1), 0)
-    valid = jnp.where(row < lengths[window], 1.0, 0.0)
-    grad_result = cotangent[0].astype(F32) * valid
+    valid = jnp.concatenate(
+        [jnp.where(row < lengths[window * count + w], 1.0, 0.0) for w in range(count)], axis=0
+    )
+    grad_result = cotangent[...].reshape(height, D).astype(F32) * valid
     grad_ffn = grad_result.astype(BF16)
-    ffn = jnp.zeros((L, D), F32)
-    grad_normed = jnp.zeros((L, D), F32)
-    for c in range(FF // D):
-        cols = slice(c * D, (c + 1) * D)
+    ffn = jnp.zeros((height, D), F32)
+    grad_normed = jnp.zeros((height, D), F32)
+    for c in range(FF // CHUNK):
+        cols = slice(c * CHUNK, (c + 1) * CHUNK)
         up = w_up[:, cols]
         down = w_down[cols, :]
         pre = nn(normed, up) + bias_up[:, cols]
@@ -222,20 +237,19 @@
         hidden = (pre * phi).astype(BF16)
         slope = phi + pre * (jnp.exp(-0.5 * pre * pre) * (1.0 / math.sqrt(2.0 * math.pi)))
         ffn = ffn + nn(hidden, down)
-        grad_pre_f = nt(grad_ffn, down) * slope
-        grad_pre = grad_pre_f.astype(BF16)
+        grad_pre = (nt(grad_ffn, down) * slope).astype(BF16)
         a_up[:, cols] += tn(normed, grad_pre)
         a_down[cols, :] += tn(hidden, grad_ffn)
         g_bias_up[:, cols] += col_sum(grad_pre.astype(F32))
         grad_normed = grad_normed + nt(grad_pre, up)
     ffn = ffn + vecs[3:4, :]
     result = middle + ffn
-    act_out[0] = result.astype(BF16)
+    act_out[...] = result.astype(BF16).reshape(count, L, D)
     stats[0:1, :] += col_sum(valid * result * result)
     stats[1:2, :] += col_sum(valid * attn * attn)
     stats[2:3, :] += col_sum(valid * ffn * ffn)
     grad_middle = grad_result + norm_back(grad_normed * vecs[0:1, :], n, inverse)
-    grad_mid_out[0] = grad_middle
+    grad_mid_out[...] = grad_middle.reshape(count, L, D)
     grad_attn = grad_middle.astype(BF16)
     a_out[...] += tn(mixed, grad_attn)
     g_vecs[0:1, :] += col_sum(grad_normed * n)
@@ -248,11 +262,13 @@
     for t in range(TILES):
         lanes = slice(t * LANES, (t + 1) * LANES)
         part = grad_mixed[:, lanes]
-        grad_mixed_out[0, t] = part
         product = part.astype(F32) * mixed[:, lanes].astype(F32)
         high = product.astype(BF16)
         low = (product - high.astype(F32)).astype(BF16)
-        dots_out[0, t] = split_lanes(-(nn(high, same) + nn(low, same)), 0.0)
+        dots = split_lanes(-(nn(high, same) + nn(low, same)), 0.0)
+        for w in range(count):
+            grad_mixed_out[w, t] = part[w * L : (w + 1) * L]
+            dots_out[w, t] = dots[w * L : (w + 1) * L]
 
     @pl.when(window == pl.num_programs(0) - 1)
     def _():
@@ -370,9 +386,9 @@
             g_second[...] = a_qkv[:, cut:].astype(BF16)
 
 
-def rows_spec(*dims):
+def rows_spec(*dims, count=1):
     rank = len(dims)
-    return pl.BlockSpec((1,) + dims, lambda w, *_: (w,) + (0,) * rank)
+    return pl.BlockSpec((count,) + dims, lambda w, *_: (w,) + (0,) * rank)
 
 
 def whole_spec(*dims):
@@ -392,7 +408,7 @@
             scratch_shapes=scratch,
         ),
         compiler_params=pltpu.CompilerParams(
-            dimension_semantics=("arbitrary",), vmem_limit_bytes=60 * 1024 * 1024
+            dimension_semantics=("arbitrary",), vmem_limit_bytes=63 * 1024 * 1024
         ),
         name=name,
     )
@@ -440,12 +456,6 @@
             values[i] = keep.astype(F32) + got.astype(F32)
             left[i].remove(bit)
     return values
-
-
-def sum_steps(value, devices):
-    for bit in range(devices.bit_length() - 1):
-        value = value + swap(value, bit, devices)
-    return value
 
 
 def rotary_tables():
@@ -485,14 +495,20 @@
         other_order = list(down_order)
         other_order[-2], other_order[-3] = other_order[-3], other_order[-2]
         shard = qkv_weight.reshape(rows, 3 * D)
-        extra = jnp.concatenate([small, up_bias.reshape(1, -1)], axis=0)
-        w_first, w_second, extra = gather_steps(
-            [shard[:, :cut], shard[:, cut:], extra],
-            [down_order, other_order, down_order],
+        extra = jnp.concatenate([small.reshape(-1), up_bias])
+        extra = jnp.pad(extra, (0, cut - extra.shape[0]))[None]
+        w_first, w_second = gather_steps(
+            [jnp.concatenate([shard[:, :cut], extra], axis=0), shard[:, cut:]],
+            [down_order, other_order],
             devices,
         )
-        small = extra[::an, :-1].transpose(1, 0, 2).reshape(9, D).astype(F32)
-        bias_up = extra[:, -1].astype(F32).reshape(1, FF)
+        extra = w_first[:, rows]
+        share = D // wa
+        small = extra[::an, : 9 * share].reshape(wa, 9, share).transpose(1, 0, 2)
+        small = small.reshape(9, D).astype(F32)
+        up_share = FF // devices
+        extra = extra[:, 9 * share : 9 * share + up_share]
+        bias_up = extra.astype(F32).reshape(1, FF)
         up = up_weight.reshape(rows, steps, D).transpose(1, 0, 2).reshape(steps * rows, D)
         pack_rows = -(-(2 * steps + 1) * rows // 32) * 32
         pad = jnp.zeros((pack_rows - (2 * steps + 1) * rows, D), BF16)
@@ -517,6 +533,9 @@
     tiled_shape = (windows, TILES, L, LANES)
     flat_spec = rows_spec(L, D)
     flat_shape = (windows, L, D)
+    pair = 2 if windows % 2 == 0 else 1
+    tiled_pair = rows_spec(TILES, L, LANES, count=pair)
+    flat_pair = rows_spec(L, D, count=pair)
     table_spec = whole_spec(SPAN, LANES)
 
     tiled_out = (tiled_spec, tiled_shape, BF16)
@@ -550,20 +569,20 @@
     activations, grad_mid, grad_mixed, dots, g_packed, g_vec_two, g_bias_up, stats = call(
         functools.partial(middle_kernel, rows),
         1,
-        windows,
+        windows // pair,
         [
-            flat_spec,
-            tiled_spec,
-            flat_spec,
-            whole_spec(*packed.shape),
+            flat_pair,
+            tiled_pair,
+            flat_pair,
+            pl.BlockSpec(memory_space=pl.ANY),
             whole_spec(4, D),
             whole_spec(1, FF),
         ],
         [
-            (flat_spec, flat_shape, BF16),
-            (flat_spec, flat_shape, F32),
-            tiled_out,
-            tiled_out,
+            (flat_pair, flat_shape, BF16),
+            (flat_pair, flat_shape, F32),
+            (tiled_pair, tiled_shape, BF16),
+            (tiled_pair, tiled_shape, BF16),
             kept(packed.shape, BF16),
             kept((4, D), F32),
             kept((1, FF), F32),
@@ -577,6 +596,7 @@
             pltpu.VMEM((D, FF), F32),
             pltpu.VMEM((FF, D), F32),
             pltpu.VMEM((packed.shape[1] if rows else 8, FF), F32),
+            pltpu.SemaphoreType.DMA(()),
         ],
         "middle",
     )(lengths, x, mixed, cotangent, packed, vec_two, bias_up)
@@ -608,7 +628,7 @@
         + [flat_spec, whole_spec(D, 3 * D), whole_spec(2, D), table_spec, table_spec],
         [
             (rows_spec(SPAN, D), (windows, SPAN, D), BF16),
-            kept(w_first.shape, BF16),
+            kept((devices, rows, cut) if rows else w_first.shape, BF16),
             kept(w_second.shape, BF16),
             kept((2, D), F32),
             kept((1, 3 * D), F32),
@@ -623,36 +643,37 @@
         "back",
     )(offsets, lengths, x, q, k, v, lse, grad_mixed, dots, grad_mid, w_qkv, vec_one, cosine, sine)
 
+    token_count = jnp.sum(lengths).astype(F32)
+    totals = jnp.concatenate([jnp.sum(stats, axis=1), token_count[None]])
+    vec_sums = jnp.concatenate([g_vec_one, g_vec_two, g_bias_qkv.reshape(3, D)], axis=0)
+    share = D // wa
+    up_share = FF // devices
     if rows:
+        vec_sums = vec_sums.reshape(9, wa, share).transpose(1, 0, 2).reshape(wa, 1, 9 * share)
+        vec_sums = jnp.broadcast_to(vec_sums, (wa, an, 9 * share)).reshape(devices, 9 * share)
+        ride = jnp.concatenate(
+            [
+                vec_sums,
+                g_bias_up.reshape(devices, up_share),
+                jnp.broadcast_to(totals, (devices, 4)),
+                jnp.zeros((devices, cut - 9 * share - up_share - 4), F32),
+            ],
+            axis=1,
+        )
+        g_first = jnp.concatenate([g_first, ride.astype(BF16)[:, None]], axis=1)
         g_first, g_second = scatter_steps(
             [g_first, g_second], [down_order[::-1], other_order[::-1]], devices
         )
-        qkv_grad = jnp.concatenate([g_first, g_second], axis=1).reshape(-1)
+        qkv_grad = jnp.concatenate([g_first[:rows], g_second], axis=1).reshape(-1)
+        ride = g_first[rows]
+        shares = ride[: 9 * share].reshape(9, share)
+        up_bias_grad = ride[9 * share : 9 * share + up_share]
+        totals = ride[9 * share + up_share : 9 * share + up_share + 4]
     else:
         qkv_grad = scatter_flat(jnp.concatenate([g_first, g_second], axis=1))
-
-    token_count = jnp.sum(lengths).astype(F32)
-    square = jnp.sum(stats, axis=1)
-    tail = jnp.concatenate([square, token_count[None], jnp.zeros((D - 4,), F32)])
-    packed = jnp.concatenate(
-        [
-            g_vec_one,
-            g_vec_two,
-            g_bias_qkv.reshape(3, D),
-            g_bias_up.reshape(FF // D, D),
-            tail[None],
-        ],
-        axis=0,
-    )
-    packed = sum_steps(packed, devices) if rows else lax.psum(packed, BOTH)
-    share = D // wa
-    first_col = lax.axis_index("wa") * share
-    shares = lax.dynamic_slice_in_dim(packed[:9], first_col, share, 1)
-    up_share = up_bias.shape[0]
-    up_bias_grad = lax.dynamic_slice_in_dim(
-        packed[9:13].reshape(FF), flat_index() * up_share, up_share, 0
-    )
-    totals = packed[13]
+        vec_sums, up_sums, totals = lax.psum((vec_sums, g_bias_up.reshape(FF), totals), BOTH)
+        shares = lax.dynamic_slice_in_dim(vec_sums, lax.axis_index("wa") * share, share, 1)
+        up_bias_grad = lax.dynamic_slice_in_dim(up_sums, flat_index() * up_share, up_share, 0)
     root_means = jnp.sqrt(totals[:3] / (totals[3] * D))
     return (
         activations,

time: 416 us -> 405 us (0.974)
  waiting for transfers between devices: 61.2 us -> 49.6 us
  starting transfers between devices: 35.2 us -> 25.6 us
  other arithmetic: 10.1 us -> 16.8 us
    ppermute x30 -> x20, waiting for transfers between devices: 61.2 us -> 49.5 us  [swap(): lax.ppermute(value, BOTH, [(i, i ^ 1 << bit) for i in range(devices)])]
    ppermute x30 -> x20, starting transfers between devices: 35.1 us -> 25.5 us  [swap(): lax.ppermute(value, BOTH, [(i, i ^ 1 << bit) for i in range(devices)])]
    concatenate x2 -> x6, other arithmetic: 0.09 us -> 5.09 us  [the longest x1 4.89 us: body(): g_first = jnp.concatenate([g_first, ride.astype(BF16)[:, None]], axis=1)]
  transfers between devices with their start and end apart: 32 -> 22, of which waited for: 21 -> 14; matrix products, arithmetic and copies ran while one was open for 7% -> 9% of each run, Pallas kernels for 40% -> 41%
where the time goes in v3:
time: 405 us; the launch traced here: 397 us
  Pallas kernels  258 us (64%)
  waiting for transfers between devices  49.6 us (12%)
  local copies, waits for them, and re-layouts  29.6 us (7%)
  starting transfers between devices  25.6 us (6%)
  other arithmetic  16.8 us (4%)
  between operations  16.5 us (4%)
    pallas_call x1, Pallas kernels, body(): call(functools.partial(middle_kernel, rows), 1, windows // pair, [flat_pa...  95.1 us
    pallas_call x1, Pallas kernels, body(): call(functools.partial(back_kernel, rows), 2, windows, [flat_spec] + [til...  93.7 us
    pallas_call x1, Pallas kernels, body(): call(functools.partial(front_kernel, rows), 2, windows, [rows_spec(SPAN,...  69.7 us
    ppermute x20, waiting for transfers between devices, swap(): lax.ppermute(value, BOTH, [(i, i ^ 1 << bit) for i in range(devices)])  49.5 us
    ppermute x20, starting transfers between devices, swap(): lax.ppermute(value, BOTH, [(i, i ^ 1 << bit) for i in range(devices)])  25.5 us
  transfers between devices with their start and end apart: 22, of which 14 were waited for; matrix products, arithmetic and copies ran while one was open for 9% of the time, Pallas kernels for 41%

profile of v3, /device:TPU:0, one launch (start us, length us, event | category | flops | bytes accessed | tf_op | source)
XLA Modules:
  0.0 396.5 jit_solution(14836015266064911656)
XLA Ops:
  11.4 4.1 %collective-permute-start = (bf16[21,1024]{1,0:T(8,128)(2,1)S(1)}, bf16[21,1024]{1,0:T(8,128)(2,1)S(1)}, u32[]{:S(2)}, u32[]{:S(2)}) collective-permute-start(bf16[21,1024]{1,0:T(8,128)(2,1)S(1)} %pad_maximum_fusion.12), channel_id=1, source_target_pairs={{0,16},{1,17},{2,18},{3,19},{4,20},{5,21},{6,22},{7,23},{8,24},{9,... | collective-permute-start | bytes 129032 | tf_op jit(solution)/shard_map/ppermute | solution.py:422
  15.7 4.9 %collective-permute-done.5 = bf16[20,896]{1,0:T(8,128)(2,1)S(1)} collective-permute-done((bf16[20,896]{1,0:T(8,128)(2,1)S(1)}, bf16[20,896]{1,0:T(8,128)(2,1)S(1)}, u32[]{:S(2)}, u32[]{:S(2)}) %collective-permute-start.5) | collective-permute-done | bytes 35872 | tf_op jit(solution)/shard_map/ppermute | solution.py:422
  20.6 1.6 collective-permute-start.6
  22.8 3.0 collective-permute-done.6
  25.9 1.6 collective-permute-start.7
  28.3 1.5 collective-permute-start.2
  29.9 1.5 collective-permute-done.7
  31.5 1.6 collective-permute-start.8
  33.1 3.1 collective-permute-done.2
  36.3 1.5 collective-permute-start.3
  37.8 3.1 collective-permute-done.8
  42.4 4.3 %collective-permute-done.3 = bf16[2,2,2,21,1024]{4,3,0,1,2:T(8,128)(2,1)S(1)} collective-permute-done((bf16[2,2,2,21,1024]{4,3,0,1,2:T(8,128)(2,1)S(1)}, bf16[2,2,2,21,1024]{4,3,0,1,2:T(8,128)(2,1)S(1)}, u32[]{:S(2)}, u32[]{:S(2)}) %collective-permute-start.3) | collective-permute-done | bytes 344096 | tf_op jit(solution)/shard_map/ppermute | solution.py:422
  49.5 1.3 select_bitcast_fusion.3
  56.9 69.7 %front.1 = (bf16[6,384,640]{2,1,0:T(8,128)(2,1)}, bf16[6,5,384,128]{3,2,1,0:T(8,128)(2,1)}, bf16[6,5,384,128]{3,2,1,0:T(8,128)(2,1)}, bf16[6,5,384,128]{3,2,1,0:...) custom-call(s32[6]{0:T(128)} %offsets.3, s32[6]{0:T(128)} %lengths.5, ...), custom_call_target="tpu_custom_call" | custom-call | tf_op jit(solution)/shard_map/front/pallas_call | solution.py:546
  127.3 95.1 %middle.1 = (bf16[6,384,640]{2,1,0:T(8,128)(2,1)}, f32[6,384,640]{2,1,0:T(8,128)}, bf16[6,5,384,128]{3,2,1,0:T(8,128)(2,1)}, bf16[6,5,384,128]{3,2,1,0:T(8,128)(...) custom-call(s32[6]{0:T(128)} %lengths.5, ...), custom_call_target="tpu_custom_call" | custom-call | tf_op jit(solution)/shard_map/middle/pallas_call | solution.py:569
  224.4 93.7 %back.1 = (bf16[6,512,640]{2,1,0:T(8,128)(2,1)}, bf16[32,20,1024]{2,1,0:T(8,128)(2,1)}, bf16[32,20,896]{2,1,0:T(8,128)(2,1)}, f32[2,640]{1,0:T(2,128)}, f32[1,1920]{1,0:T(1,128)}) custom-call(s32[6]{0:T(128)} %offsets.3, s32[6]{0:T(128)} %lengths.5, bf16[6,384,640]{2,1,0:T(8,128)(2,1)} %get-tuple-element.32.x_in, ...), custom_call_target="tpu_custom_call" | custom-call | tf_op jit(solution)/shard_map/back/pallas_call | solution.py:622
  320.0 2.9 copy.199
  323.5 1.3 copy.235
  325.3 4.9 %maximum_maximum_fusion = bf16[2,2,2,2,2,21,1024]{6,3,5,2,1,0,4:T(2,128)(2,1)S(1)} fusion(bf16[2,2,2,2,2,1,80]{6,3,5,2,1,0,4:T(2,128)(2,1)S(1)} %copy.198, bf16[2,2,2,2,2,1,720]{6,3,5,2,1,0,4:T(2,128)(2,1)S(1)} %broadcast_in_dim.26, bf16[2,2,2,2,2,20,1024]{6,3,5,2,1,0,4:T(2,128)(2,1)S(1)} %copy.199, bf16[21,1024]{1,0:T(8,128)(2,1)S(1)} %pad.15.clone, ...), kind=kLoop, calls=%fused_computation.2 | loop fusion | flops 6881280 | bytes 2824192 | tf_op jit(solution)/shard_map/concatenate | solution.py:663
  330.2 1.4 dynamic-slice_bitcast_fusion
  332.9 1.5 collective-permute-start.16
  334.4 1.8 convert_add_fusion.1
  336.2 8.9 %collective-permute-done.16 = bf16[2,2,2,20,896]{4,3,0,1,2:T(8,128)(2,1)S(1)} collective-permute-done((bf16[2,2,2,20,896]{4,3,0,1,2:T(8,128)(2,1)S(1)}, bf16[2,2,2,20,896]{4,3,0,1,2:T(8,128)(2,1)S(1)}, u32[]{:S(2)}, u32[]{:S(2)}) %collective-permute-start.16) | collective-permute-done | bytes 286752 | tf_op jit(solution)/shard_map/ppermute | solution.py:422
  345.3 2.6 collective-permute-start.17
  349.7 3.4 collective-permute-done.17
  353.2 1.8 collective-permute-start.18
  354.9 4.6 %collective-permute-done.11 = bf16[2,2,2,21,1024]{4,2,3,1,0:T(2,128)(2,1)S(1)} collective-permute-done((bf16[2,2,2,21,1024]{4,2,3,1,0:T(2,128)(2,1)S(1)}, bf16[2,2,2,21,1024]{4,2,3,1,0:T(2,128)(2,1)S(1)}, u32[]{:S(2)}, u32[]{:S(2)}) %collective-permute-start.11) | collective-permute-done | bytes 344096 | tf_op jit(solution)/shard_map/ppermute | solution.py:422
  360.4 3.4 collective-permute-start.19
  365.8 4.0 %collective-permute-done.12 = bf16[2,2,21,1024]{3,1,2,0:T(2,128)(2,1)S(1)} collective-permute-done((bf16[2,2,21,1024]{3,1,2,0:T(2,128)(2,1)S(1)}, bf16[2,2,21,1024]{3,1,2,0:T(2,128)(2,1)S(1)}, u32[]{:S(2)}, u32[]{:S(2)}) %collective-permute-start.12) | collective-permute-done | bytes 172064 | tf_op jit(solution)/shard_map/ppermute | solution.py:422
  370.3 1.7 collective-permute-start.13
  372.1 2.7 collective-permute-done.13
  375.5 4.6 %collective-permute-done.14 = bf16[21,1024]{1,0:T(8,128)(2,1)S(1)} collective-permute-done((bf16[21,1024]{1,0:T(8,128)(2,1)S(1)}, bf16[21,1024]{1,0:T(8,128)(2,1)S(1)}, u32[]{:S(2)}, u32[]{:S(2)}) %collective-permute-start.14) | collective-permute-done | bytes 43040 | tf_op jit(solution)/shard_map/ppermute | solution.py:422
  (175 shorter events, 36.8 us)
Async XLA Ops:
  7.2 3.9 copy-start.2
  7.2 4.0 %copy-start.11 = (bf16[2,80]{1,0:T(2,128)(2,1)S(1)}, bf16[2,80]{1,0:T(2,128)(2,1)}, u32[]{:S(2)}) copy-start(bf16[2,80]{1,0:T(2,128)(2,1)} %param.22) | copy-start | bytes 964
  7.2 4.0 %copy-start.10 = (bf16[2,80]{1,0:T(2,128)(2,1)S(1)}, bf16[2,80]{1,0:T(2,128)(2,1)}, u32[]{:S(2)}) copy-start(bf16[2,80]{1,0:T(2,128)(2,1)} %param.23) | copy-start | bytes 964
  7.2 4.0 %copy-start.7 = (bf16[3,80]{1,0:T(4,128)(2,1)S(1)}, bf16[3,80]{1,0:T(4,128)(2,1)}, u32[]{:S(2)}) copy-start(bf16[3,80]{1,0:T(4,128)(2,1)} %param.24) | copy-start | bytes 1444
  7.2 4.0 %copy-start.9 = (bf16[2,80]{1,0:T(2,128)(2,1)S(1)}, bf16[2,80]{1,0:T(2,128)(2,1)}, u32[]{:S(2)}) copy-start(bf16[2,80]{1,0:T(2,128)(2,1)} %param.25) | copy-start | bytes 964
  7.2 4.1 %copy-start.8 = (bf16[80]{0:T(256)(128)(2,1)S(1)}, bf16[80]{0:T(256)(128)(2,1)}, u32[]{:S(2)}) copy-start(bf16[80]{0:T(256)(128)(2,1)} %param.21) | copy-start | bytes 484
  7.2 120.0 %all-gather.3.cloned.1.call-start = ((), (), s32[]{:S(2)}) async-start(), calls=%async_computation.2 | async-start | bytes 8110080 | tf_op jit(solution)/shard_map/all_gather | solution.py:516
  11.0 374.4 %reduce-scatter.2.cloned.1.call-start = ((), (), s32[]{:S(2)}) async-start(), calls=%async_computation.1 | async-start | bytes 8110080 | tf_op jit(solution)/shard_map/reduce_scatter | solution.py:605
  11.4 10.7 %collective-permute-start = (bf16[21,1024]{1,0:T(8,128)(2,1)S(1)}, bf16[21,1024]{1,0:T(8,128)(2,1)S(1)}, u32[]{:S(2)}, u32[]{:S(2)}) collective-permute-start(bf16[21,1024]{1,0:T(8,128)(2,1)S(1)} %pad_maximum_fusion.12), channel_id=1, source_target_pairs={{0,16},{1,17},{2,18},{3,19},{4,20},{5,21},{6,22},{7,23},{8,24},{9,... | collective-permute-start | bytes 129032 | tf_op jit(solution)/shard_map/ppermute | solution.py:422
  15.6 5.0 %collective-permute-start.5 = (bf16[20,896]{1,0:T(8,128)(2,1)S(1)}, bf16[20,896]{1,0:T(8,128)(2,1)S(1)}, u32[]{:S(2)}, u32[]{:S(2)}) collective-permute-start(bf16[20,896]{1,0:T(8,128)(2,1)S(1)} %slice.157), channel_id=1, source_target_pairs={{0,16},{1,17},{2,18},{3,19},{4,20},{5,21},{6,22},{7,23},{8,24},{9,... | collective-permute-start | bytes 107528 | tf_op jit(solution)/shard_map/ppermute | solution.py:422
  20.6 5.2 %collective-permute-start.6 = (bf16[2,20,896]{2,1,0:T(8,128)(2,1)S(1)}, bf16[2,20,896]{2,1,0:T(8,128)(2,1)S(1)}, u32[]{:S(2)}, u32[]{:S(2)}) collective-permute-start(bf16[2,20,896]{2,1,0:T(8,128)(2,1)S(1)} %pad_maximum_fusion.10), channel_id=1, source_target_pairs={{0,8},{1,9},{2,10},{3,11},{4,12},{5,13},{6,14},{7,15},{8,0},{9,1},... | collective-permute-start | bytes 215048 | tf_op jit(solution)/shard_map/ppermute | solution.py:422
  22.2 6.0 %collective-permute-start.1 = (bf16[2,21,1024]{2,1,0:T(8,128)(2,1)S(1)}, bf16[2,21,1024]{2,1,0:T(8,128)(2,1)S(1)}, u32[]{:S(2)}, u32[]{:S(2)}) collective-permute-start(bf16[2,21,1024]{2,1,0:T(8,128)(2,1)S(1)} %pad_maximum_fusion.9), channel_id=1, source_target_pairs={{0,8},{1,9},{2,10},{3,11},{4,12},{5,13},{6,14},{7,15},{8,0},{9,1},... | collective-permute-start | bytes 258056 | tf_op jit(solution)/shard_map/ppermute | solution.py:422
  25.9 5.5 %collective-permute-start.7 = (bf16[2,2,20,896]{3,2,0,1:T(8,128)(2,1)S(1)}, bf16[2,2,20,896]{3,2,0,1:T(8,128)(2,1)S(1)}, u32[]{:S(2)}, u32[]{:S(2)}) collective-permute-start(bf16[2,2,20,896]{3,2,0,1:T(8,128)(2,1)S(1)} %pad_maximum_fusion.8), channel_id=1, source_target_pairs={{0,2},{1,3},{2,0},{3,1},{4,6},{5,7},{6,4},{7,5},{8,10},{9,11},{10,... | collective-permute-start | bytes 430088 | tf_op jit(solution)/shard_map/ppermute | solution.py:422
  28.3 7.8 %collective-permute-start.2 = (bf16[2,2,21,1024]{3,2,0,1:T(8,128)(2,1)S(1)}, bf16[2,2,21,1024]{3,2,0,1:T(8,128)(2,1)S(1)}, u32[]{:S(2)}, u32[]{:S(2)}) collective-permute-start(bf16[2,2,21,1024]{3,2,0,1:T(8,128)(2,1)S(1)} %pad_maximum_fusion.6), channel_id=1, source_target_pairs={{0,4},{1,5},{2,6},{3,7},{4,0},{5,1},{6,2},{7,3},{8,12},{9,13},{10,... | collective-permute-start | bytes 516104 | tf_op jit(solution)/shard_map/ppermute | solution.py:422
  31.5 9.4 %collective-permute-start.8 = (bf16[2,2,2,20,896]{4,3,0,1,2:T(8,128)(2,1)S(1)}, bf16[2,2,2,20,896]{4,3,0,1,2:T(8,128)(2,1)S(1)}, u32[]{:S(2)}, u32[]{:S(2)}) collective-permute-start(bf16[2,2,2,20,896]{4,3,0,1,2:T(8,128)(2,1)S(1)} %pad_maximum_fusion.5), channel_id=1, source_target_pairs={{0,4},{1,5},{2,6},{3,7},{4,0},{5,1},{6,2},{7,3},{8,12},{9,13},{10,... | collective-permute-start | bytes 860168 | tf_op jit(solution)/shard_map/ppermute | solution.py:422
  36.3 10.4 %collective-permute-start.3 = (bf16[2,2,2,21,1024]{4,3,0,1,2:T(8,128)(2,1)S(1)}, bf16[2,2,2,21,1024]{4,3,0,1,2:T(8,128)(2,1)S(1)}, u32[]{:S(2)}, u32[]{:S(2)}) collective-permute-start(bf16[2,2,2,21,1024]{4,3,0,1,2:T(8,128)(2,1)S(1)} %pad_maximum_fusion.4), channel_id=1, source_target_pairs={{0,2},{1,3},{2,0},{3,1},{4,6},{5,7},{6,4},{7,5},{8,10},{9,11},{10,... | collective-permute-start | bytes 1032200 | tf_op jit(solution)/shard_map/ppermute | solution.py:422
  42.4 7.2 %collective-permute-start.9 = (bf16[2,2,2,2,20,896]{5,3,4,2,1,0:T(2,128)(2,1)}, bf16[2,2,2,2,20,896]{5,3,4,2,1,0:T(2,128)(2,1)}, u32[]{:S(2)}, u32[]{:S(2)}) collective-permute-start(bf16[2,2,2,2,20,896]{5,3,4,2,1,0:T(2,128)(2,1)} %copy.184), channel_id=1, source_target_pairs={{0,1},{1,0},{2,3},{3,2},{4,5},{5,4},{6,7},{7,6},{8,9},{9,8},{10,11... | collective-permute-start | bytes 1720328 | tf_op jit(solution)/shard_map/ppermute | solution.py:422
  47.5 4.8 %collective-permute-start.4 = (bf16[2,2,2,2,21,1024]{5,3,4,2,1,0:T(2,128)(2,1)S(1)}, bf16[2,2,2,2,21,1024]{5,3,4,2,1,0:T(2,128)(2,1)S(1)}, u32[]{:S(2)}, u32[]{:S(2)}) collective-permute-start(bf16[2,2,2,2,21,1024]{5,3,4,2,1,0:T(2,128)(2,1)S(1)} %copy.180), channel_id=1, source_target_pairs={{0,1},{1,0},{2,3},{3,2},{4,5},{5,4},{6,7},{7,6},{8,9},{9,8},{10,11... | collective-permute-start | bytes 2064392 | tf_op jit(solution)/shard_map/ppermute | solution.py:422
  224.4 95.4 %copy-start.4 = (f32[4,640]{1,0:T(4,128)S(1)}, f32[4,640]{1,0:T(4,128)}, u32[]{:S(2)}) copy-start(f32[4,640]{1,0:T(4,128)} %get-tuple-element.46) | copy-start | bytes 30724
  318.1 4.8 %copy-start.3 = (f32[3,640]{1,0:T(4,128)S(1)}, f32[3,640]{1,0:T(4,128)}, u32[]{:S(2)}) copy-start(f32[3,640]{1,0:T(4,128)} %get-tuple-element.49) | copy-start | bytes 23044
  318.1 5.1 %copy-start.5 = (f32[1,2560]{1,0:T(1,128)S(1)}, f32[1,2560]{1,0:T(1,128)}, u32[]{:S(2)}) copy-start(f32[1,2560]{1,0:T(1,128)} %get-tuple-element.48) | copy-start | bytes 30724
  319.7 3.6 copy-start.1
  324.8 6.8 %collective-permute-start.15 = (bf16[2,2,2,2,20,896]{5,3,4,2,1,0:T(2,128)(2,1)}, bf16[2,2,2,2,20,896]{5,3,4,2,1,0:T(2,128)(2,1)}, u32[]{:S(2)}, u32[]{:S(2)}) collective-permute-start(bf16[2,2,2,2,20,896]{5,3,4,2,1,0:T(2,128)(2,1)} %bitcast.106), channel_id=1, source_target_pairs={{0,1},{1,0},{2,3},{3,2},{4,5},{5,4},{6,7},{7,6},{8,9},{9,8},{10,11... | collective-permute-start | bytes 1720328 | tf_op jit(solution)/shard_map/ppermute | solution.py:422
  331.6 2.8 collective-permute-start.10
  332.9 12.3 %collective-permute-start.16 = (bf16[2,2,2,20,896]{4,3,0,1,2:T(8,128)(2,1)S(1)}, bf16[2,2,2,20,896]{4,3,0,1,2:T(8,128)(2,1)S(1)}, u32[]{:S(2)}, u32[]{:S(2)}) collective-permute-start(bf16[2,2,2,20,896]{4,3,0,1,2:T(8,128)(2,1)S(1)} %fusion), channel_id=1, source_target_pairs={{0,4},{1,5},{2,6},{3,7},{4,0},{5,1},{6,2},{7,3},{8,12},{9,13},{10,... | collective-permute-start | bytes 860168 | tf_op jit(solution)/shard_map/ppermute | solution.py:422
  345.3 7.8 %collective-permute-start.17 = (bf16[2,2,20,896]{3,2,0,1:T(8,128)(2,1)S(1)}, bf16[2,2,20,896]{3,2,0,1:T(8,128)(2,1)S(1)}, u32[]{:S(2)}, u32[]{:S(2)}) collective-permute-start(bf16[2,2,20,896]{3,2,0,1:T(8,128)(2,1)S(1)} %fusion.1), channel_id=1, source_target_pairs={{0,2},{1,3},{2,0},{3,1},{4,6},{5,7},{6,4},{7,5},{8,10},{9,11},{10,... | collective-permute-start | bytes 430088 | tf_op jit(solution)/shard_map/ppermute | solution.py:422
  348.9 10.7 %collective-permute-start.11 = (bf16[2,2,2,21,1024]{4,2,3,1,0:T(2,128)(2,1)S(1)}, bf16[2,2,2,21,1024]{4,2,3,1,0:T(2,128)(2,1)S(1)}, u32[]{:S(2)}, u32[]{:S(2)}) collective-permute-start(bf16[2,2,2,21,1024]{4,2,3,1,0:T(2,128)(2,1)S(1)} %bitcast.124), channel_id=1, source_target_pairs={{0,2},{1,3},{2,0},{3,1},{4,6},{5,7},{6,4},{7,5},{8,10},{9,11},{10,... | collective-permute-start | bytes 1032200 | tf_op jit(solution)/shard_map/ppermute | solution.py:422
  353.2 7.2 %collective-permute-start.18 = (bf16[2,20,896]{2,1,0:T(8,128)(2,1)S(1)}, bf16[2,20,896]{2,1,0:T(8,128)(2,1)S(1)}, u32[]{:S(2)}, u32[]{:S(2)}) collective-permute-start(bf16[2,20,896]{2,1,0:T(8,128)(2,1)S(1)} %fusion.2), channel_id=1, source_target_pairs={{0,8},{1,9},{2,10},{3,11},{4,12},{5,13},{6,14},{7,15},{8,0},{9,1},... | collective-permute-start | bytes 215048 | tf_op jit(solution)/shard_map/ppermute | solution.py:422
  360.4 5.4 %collective-permute-start.19 = (bf16[20,896]{1,0:T(8,128)(2,1)S(1)}, bf16[20,896]{1,0:T(8,128)(2,1)S(1)}, u32[]{:S(2)}, u32[]{:S(2)}) collective-permute-start(bf16[20,896]{1,0:T(8,128)(2,1)S(1)} %fusion.3), channel_id=1, source_target_pairs={{0,16},{1,17},{2,18},{3,19},{4,20},{5,21},{6,22},{7,23},{8,24},{9,... | collective-permute-start | bytes 107528 | tf_op jit(solution)/shard_map/ppermute | solution.py:422
  364.4 5.5 %collective-permute-start.12 = (bf16[2,2,21,1024]{3,1,2,0:T(2,128)(2,1)S(1)}, bf16[2,2,21,1024]{3,1,2,0:T(2,128)(2,1)S(1)}, u32[]{:S(2)}, u32[]{:S(2)}) collective-permute-start(bf16[2,2,21,1024]{3,1,2,0:T(2,128)(2,1)S(1)} %bitcast.128), channel_id=1, source_target_pairs={{0,4},{1,5},{2,6},{3,7},{4,0},{5,1},{6,2},{7,3},{8,12},{9,13},{10,... | collective-permute-start | bytes 516104 | tf_op jit(solution)/shard_map/ppermute | solution.py:422
  370.3 4.6 %collective-permute-start.13 = (bf16[2,21,1024]{2,0,1:T(2,128)(2,1)S(1)}, bf16[2,21,1024]{2,0,1:T(2,128)(2,1)S(1)}, u32[]{:S(2)}, u32[]{:S(2)}) collective-permute-start(bf16[2,21,1024]{2,0,1:T(2,128)(2,1)S(1)} %bitcast.131), channel_id=1, source_target_pairs={{0,8},{1,9},{2,10},{3,11},{4,12},{5,13},{6,14},{7,15},{8,0},{9,1},... | collective-permute-start | bytes 258056 | tf_op jit(solution)/shard_map/ppermute | solution.py:422
  375.1 5.1 %collective-permute-start.14 = (bf16[21,1024]{1,0:T(8,128)(2,1)S(1)}, bf16[21,1024]{1,0:T(8,128)(2,1)S(1)}, u32[]{:S(2)}, u32[]{:S(2)}) collective-permute-start(bf16[21,1024]{1,0:T(8,128)(2,1)S(1)} %bitcast.132), channel_id=1, source_target_pairs={{0,16},{1,17},{2,18},{3,19},{4,20},{5,21},{6,22},{7,23},{8,24},{9,... | collective-permute-start | bytes 129032 | tf_op jit(solution)/shard_map/ppermute | solution.py:422
  (2 other events, 1.8 us)
Sparse Core Ops, SparseCore 0:
  11.1 79.0 all-gather.2
  222.5 127.3 reduce-scatter.1

commit v4 on v3

--- a/solution.py
+++ b/solution.py
@@ -107,31 +107,54 @@
     lax.fori_loop(0, dest.shape[0] // (4 * rows), group, 0)
 
 
+def unpack_cores(parts, mine, rows, staging, dest):
+    def group(i, carry):
+        for own, other, col, cols in parts:
+            for j in range(4):
+                at = 2 * i + j // 2
+                block = jnp.where(
+                    mine == j % 2, own[at].astype(F32)[:rows], other[at].astype(F32)[:rows]
+                )
+                staging[j * rows : (j + 1) * rows, col : col + cols] = block
+        at = pl.multiple_of(i * 4 * rows, 4 * rows)
+        dest[pl.ds(at, 4 * rows), :] = staging[...].astype(BF16)
+        return carry
+
+    lax.fori_loop(0, dest.shape[0] // (4 * rows), group, 0)
+
+
 def front_kernel(
     rows,
-    offsets, lengths, span, w_first, w_second, vecs, bias_qkv, cosine, sine,
-    x_out, q_out, k_out, v_out, lse_out, mixed_out, w_qkv,
-    proj, keys_big, values_big, staging,
+    offsets, lengths, core, span, *refs,
 ):
+    (
+        weights, small, cosine, sine,
+        x_out, q_out, k_out, v_out, lse_out, mixed_out, w_qkv,
+        proj, keys_big, values_big, staging,
+    ) = refs[:-14], *refs[-14:]
     window = pl.program_id(0)
 
     @pl.when(window == 0)
     def _():
         if rows:
-            cut = w_first.shape[2]
-            parts = [(w_first, 0, 0, cut), (w_second, 0, cut, 3 * D - cut)]
-            unpack_rows(parts, rows, staging, w_qkv)
+            own_first, other_first, own_second, other_second = weights
+            cut = own_first.shape[2]
+            parts = [
+                (own_first, other_first, 0, cut),
+                (own_second, other_second, cut, 3 * D - cut),
+            ]
+            unpack_cores(parts, core[0], rows, staging, w_qkv)
         else:
-            w_qkv[:, : w_first.shape[1]] = w_first[...]
-            w_qkv[:, w_first.shape[1] :] = w_second[...]
+            w_qkv[...] = weights[0][...]
 
     start = offsets[window]
     length = lengths[window]
     x = take_rows(span[0].astype(F32), start)
     x_out[0] = x.astype(BF16)
     n, _ = normalize(x)
-    normed = (n * vecs[0:1, :] + vecs[1:2, :]).astype(BF16)
-    proj[...] = nn(normed, w_qkv[...]) + bias_qkv[...]
+    normed = (n * small[0:1, :] + small[2:3, :]).astype(BF16)
+    bias = jnp.concatenate([small[4:5, :], small[5:6, :], small[6:7, :]], axis=1)
+    proj[...] = nn(normed, w_qkv[...]) + bias
     cos = take_rows(cosine[...], start)
     sin = take_rows(sine[...], start)
     for t in range(TILES):
@@ -173,7 +196,7 @@
 
 def middle_kernel(
     rows,
-    lengths, x_in, mixed_in, cotangent, packed_hbm, vecs, bias_up,
+    lengths, x_in, mixed_in, cotangent, packed_hbm, small, bias_up,
     act_out, grad_mid_out, grad_mixed_out, dots_out,
     g_packed, g_vecs, g_bias_up, stats,
     w_out, w_up, w_down, a_out, a_up, a_down, staging, arrived,
@@ -216,10 +239,10 @@
         ],
         axis=0,
     )
-    attn = nn(mixed, w_out[...]) + vecs[2:3, :]
+    attn = nn(mixed, w_out[...]) + small[7:8, :]
     middle = x + attn
     n, inverse = normalize(middle)
-    normed = (n * vecs[0:1, :] + vecs[1:2, :]).astype(BF16)
+    normed = (n * small[1:2, :] + small[3:4, :]).astype(BF16)
     row = lax.broadcasted_iota(jnp.int32, (L, 1), 0)
     valid = jnp.concatenate(
         [jnp.where(row < lengths[window * count + w], 1.0, 0.0) for w in range(count)], axis=0
@@ -242,13 +265,13 @@
         a_down[cols, :] += tn(hidden, grad_ffn)
         g_bias_up[:, cols] += col_sum(grad_pre.astype(F32))
         grad_normed = grad_normed + nt(grad_pre, up)
-    ffn = ffn + vecs[3:4, :]
+    ffn = ffn + small[8:9, :]
     result = middle + ffn
     act_out[...] = result.astype(BF16).reshape(count, L, D)
     stats[0:1, :] += col_sum(valid * result * result)
     stats[1:2, :] += col_sum(valid * attn * attn)
     stats[2:3, :] += col_sum(valid * ffn * ffn)
-    grad_middle = grad_result + norm_back(grad_normed * vecs[0:1, :], n, inverse)
+    grad_middle = grad_result + norm_back(grad_normed * small[1:2, :], n, inverse)
     grad_mid_out[...] = grad_middle.reshape(count, L, D)
     grad_attn = grad_middle.astype(BF16)
     a_out[...] += tn(mixed, grad_attn)
@@ -304,11 +327,11 @@
 
 
 def back_kernel(
-    rows,
-    offsets, lengths, x_in, q_in, k_in, v_in, lse_in, gm_in, dots_in, grad_mid, w_qkv, vecs,
-    cosine, sine,
-    span_grad, g_first, g_second, g_vecs, g_bias,
-    a_qkv, grad_proj, queries_big, mixed_big, scores_back,
+    rows, inner,
+    offsets, lengths, core, x_in, q_in, k_in, v_in, lse_in, gm_in, dots_in, grad_mid, w_qkv, small,
+    cosine, sine, vec_two, bias_up, stats,
+    span_grad, keep_first, send_first, keep_second, send_second, g_vecs, g_bias,
+    a_qkv, grad_proj, queries_big, mixed_big, scores_back, ride, staging,
 ):
     window = pl.program_id(0)
     start = offsets[window]
@@ -355,35 +378,66 @@
         grad_proj[:, t * LANES : (t + 1) * LANES] = grad_q.astype(BF16)
     x = x_in[0].astype(F32)
     n, inverse = normalize(x)
-    normed = (n * vecs[0:1, :] + vecs[1:2, :]).astype(BF16)
+    normed = (n * small[0:1, :] + small[2:3, :]).astype(BF16)
     grads = grad_proj[...]
     a_qkv[...] += tn(normed, grads)
     g_bias[...] += col_sum(grads.astype(F32))
     grad_normed = nt(grads, w_qkv[...])
     g_vecs[0:1, :] += col_sum(grad_normed * n)
     g_vecs[1:2, :] += col_sum(grad_normed)
-    grad_x = grad_mid[0] + norm_back(grad_normed * vecs[0:1, :], n, inverse)
+    grad_x = grad_mid[0] + norm_back(grad_normed * small[0:1, :], n, inverse)
     wide = jnp.concatenate([grad_x, jnp.zeros((CROP, D), F32)], axis=0)
     span_grad[0] = pltpu.roll(wide, start, 0).astype(BF16)
 
     @pl.when(window == pl.num_programs(0) - 1)
     def _():
-        cut = g_first.shape[-1]
-        if rows:
-
-            def group(i, carry):
-                at = pl.multiple_of(i * 2 * rows, 2 * rows)
-                block = a_qkv[pl.ds(at, 2 * rows), :]
-                for j in range(2):
-                    part = block[j * rows : (j + 1) * rows].astype(BF16)
-                    g_first[2 * i + j] = part[:, :cut]
-                    g_second[2 * i + j] = part[:, cut:]
-                return carry
-
-            lax.fori_loop(0, D // (2 * rows), group, 0)
-        else:
-            g_first[...] = a_qkv[:, :cut].astype(BF16)
-            g_second[...] = a_qkv[:, cut:].astype(BF16)
+        if not rows:
+            keep_first[...] = a_qkv[...].astype(BF16)
+            for ref in (send_first, keep_second, send_second):
+                ref[...] = jnp.zeros_like(ref)
+            return
+        cut = keep_first.shape[2]
+        groups, _, share = bias_up.shape
+        ride[...] = jnp.zeros_like(ride)
+        staging[...] = jnp.zeros_like(staging)
+        bias = g_bias[...]
+        vectors = jnp.concatenate(
+            [g_vecs[...], vec_two[...]] + [bias[:, i * D : (i + 1) * D] for i in range(3)], axis=0
+        )
+        parts = ride.shape[0]
+        width = D // parts
+        for w in range(parts):
+            ride[w, 0:9, 0:width] = vectors[:, w * width : (w + 1) * width]
+        sums = jnp.sum(stats[...], axis=1, keepdims=True)
+        tokens = lax.fori_loop(
+            0, pl.num_programs(0), lambda w, total: total + lengths[w], jnp.int32(0)
+        ).astype(F32)
+        at = lane_iota(1, LANES)
+        last = jnp.where(at == 3, tokens, 0.0)
+        for i in range(3):
+            last = jnp.where(at == i, sums[i : i + 1, :], last)
+        mine = core[0]
+
+        def group(i, carry):
+            at = pl.multiple_of(i * 2 * rows, 2 * rows)
+            block = a_qkv[pl.ds(at, 2 * rows), :]
+            low, high = block[:rows], block[rows:]
+            vecs = ride[2 * i // inner]
+            for j, first, second in ((0, keep_first, keep_second), (1, send_first, send_second)):
+                want = mine == j
+                staging[:rows, :] = jnp.where(want, low, high)
+                staging[rows : rows + 4, :LANES] = vecs[0:4]
+                staging[rows : rows + 4, LANES : 2 * LANES] = vecs[4:8]
+                staging[rows : rows + 1, 2 * LANES : 3 * LANES] = vecs[8:9]
+                staging[rows + 1 : rows + 2, 2 * LANES : 2 * LANES + share] = jnp.where(
+                    want, bias_up[2 * i], bias_up[2 * i + 1]
+                )
+                staging[rows + 2 : rows + 3, 2 * LANES : 3 * LANES] = last
+                first[i] = staging[:, :cut].astype(BF16)
+                second[i] = staging[:rows, cut:].astype(BF16)
+            return carry
+
+        lax.fori_loop(0, groups // 2, group, 0)
 
 
 def rows_spec(*dims, count=1):
@@ -426,7 +480,7 @@
     index = flat_index()
     done = [[] for _ in shards]
     values = list(shards)
-    for step in range(len(orders[0])):
+    for step in range(len(orders[0]) - 1):
         for i, order in enumerate(orders):
             bit = order[step]
             mine = values[i]
@@ -437,25 +491,36 @@
                 [jnp.where(low, mine, other), jnp.where(low, other, mine)], axis=axis
             )
             done[i].append(bit)
-    return [v.reshape((devices,) + s.shape) for v, s in zip(values, shards)]
-
-
-def scatter_steps(arrays, orders, devices):
+    values = [v.reshape((devices // 2,) + s.shape) for v, s in zip(values, shards)]
+    return [(v, swap(v, 0, devices)) for v in values]
+
+
+def scatter_steps(halves, orders, devices):
     index = flat_index()
     bits = devices.bit_length() - 1
-    left = [sorted(range(bits), reverse=True) for _ in arrays]
-    values = [a.reshape((2,) * bits + a.shape[1:]) for a in arrays]
-    for step in range(bits):
+    left = [list(range(bits - 1, 0, -1)) for _ in halves]
+    shape = (2,) * (bits - 1)
+    values = []
+    for keep, send in halves:
+        got = swap(send, 0, devices)
+        values.append((keep.reshape(shape + keep.shape[1:]), got.reshape(shape + keep.shape[1:])))
+    for step in range(1, bits):
         for i, order in enumerate(orders):
             bit = order[step]
             axis = left[i].index(bit)
             own = (index >> bit) & 1
-            send = lax.dynamic_index_in_dim(values[i], 1 - own, axis, keepdims=False)
-            keep = lax.dynamic_index_in_dim(values[i], own, axis, keepdims=False)
-            got = swap(send.astype(BF16), bit, devices)
-            values[i] = keep.astype(F32) + got.astype(F32)
+
+            def half(which):
+                keep, got = (
+                    lax.dynamic_index_in_dim(v, which, axis, keepdims=False).astype(F32)
+                    for v in values[i]
+                )
+                return keep + got
+
+            got = swap(half(1 - own).astype(BF16), bit, devices)
+            values[i] = (half(own), got)
             left[i].remove(bit)
-    return values
+    return [keep + got.astype(F32) for keep, got in values]
 
 
 def rotary_tables():
@@ -487,8 +552,12 @@
     devices = wa * an
     bits = devices.bit_length() - 1
     steps = FF // D
-    rows = D // devices if D % (4 * devices) == 0 and devices == 1 << bits else 0
+    even = D % (4 * devices) == 0 and devices == 1 << bits and an % 2 == 0
+    rows = D // devices if even else 0
     cut = 8 * LANES
+    share = D // wa
+    up_share = FF // devices
+    core = (flat_index() & 1).astype(jnp.int32)[None]
     small = jnp.concatenate([norm_gains, norm_shifts, qkv_bias, out_biases], axis=0)
     if rows:
         down_order = list(range(bits))[::-1]
@@ -497,18 +566,20 @@
         shard = qkv_weight.reshape(rows, 3 * D)
         extra = jnp.concatenate([small.reshape(-1), up_bias])
         extra = jnp.pad(extra, (0, cut - extra.shape[0]))[None]
-        w_first, w_second = gather_steps(
+        (own_first, other_first), (own_second, other_second) = gather_steps(
             [jnp.concatenate([shard[:, :cut], extra], axis=0), shard[:, cut:]],
             [down_order, other_order],
             devices,
         )
-        extra = w_first[:, rows]
-        share = D // wa
-        small = extra[::an, : 9 * share].reshape(wa, 9, share).transpose(1, 0, 2)
-        small = small.reshape(9, D).astype(F32)
-        up_share = FF // devices
-        extra = extra[:, 9 * share : 9 * share + up_share]
-        bias_up = extra.astype(F32).reshape(1, FF)
+        weights = [own_first, other_first, own_second, other_second]
+        small = own_first[:: an // 2, rows, : 9 * share]
+        small = small.reshape(wa, 9, share).transpose(1, 0, 2).reshape(9, D).astype(F32)
+        ups = [v[:, rows, 9 * share : 9 * share + up_share] for v in (own_first, other_first)]
+        low = core[0] == 0
+        bias_up = jnp.stack(
+            [jnp.where(low, ups[0], ups[1]), jnp.where(low, ups[1], ups[0])], axis=1
+        )
+        bias_up = bias_up.astype(F32).reshape(1, FF)
         up = up_weight.reshape(rows, steps, D).transpose(1, 0, 2).reshape(steps * rows, D)
         pack_rows = -(-(2 * steps + 1) * rows // 32) * 32
         pad = jnp.zeros((pack_rows - (2 * steps + 1) * rows, D), BF16)
@@ -516,7 +587,7 @@
         packed = lax.all_gather(packed, BOTH, axis=0, tiled=False)
     else:
         w_qkv = lax.all_gather(qkv_weight, BOTH, axis=0, tiled=True).reshape(D, 3 * D)
-        w_first, w_second = w_qkv[:, :cut], w_qkv[:, cut:]
+        weights = [w_qkv]
         small = lax.all_gather(small, "wa", axis=1, tiled=True).astype(F32)
         bias_up = lax.all_gather(up_bias, BOTH, axis=0, tiled=True).astype(F32).reshape(1, FF)
         w_down = lax.all_gather(down_weight, BOTH, axis=0, tiled=True).reshape(FF, D)
@@ -524,16 +595,13 @@
         w_up = w_up.reshape(D, steps, D).transpose(1, 0, 2).reshape(FF, D)
         w_out = lax.all_gather(out_weight, BOTH, axis=0, tiled=True).reshape(D, D)
         packed = jnp.concatenate([w_down, w_up, w_out], axis=0)
-    vec_one = jnp.stack([small[0], small[2]])
-    vec_two = jnp.stack([small[1], small[3], small[7], small[8]])
-    bias_qkv = small[4:7].reshape(1, 3 * D)
     cosine, sine = rotary_tables()
 
     tiled_spec = rows_spec(TILES, L, LANES)
     tiled_shape = (windows, TILES, L, LANES)
     flat_spec = rows_spec(L, D)
     flat_shape = (windows, L, D)
-    pair = 2 if windows % 2 == 0 else 1
+    pair = 1
     tiled_pair = rows_spec(TILES, L, LANES, count=pair)
     flat_pair = rows_spec(L, D, count=pair)
     table_spec = whole_spec(SPAN, LANES)
@@ -545,17 +613,11 @@
 
     x, q, k, v, lse, mixed, w_qkv = call(
         functools.partial(front_kernel, rows),
-        2,
+        3,
         windows,
-        [
-            rows_spec(SPAN, D),
-            whole_spec(*w_first.shape),
-            whole_spec(*w_second.shape),
-            whole_spec(2, D),
-            whole_spec(1, 3 * D),
-            table_spec,
-            table_spec,
-        ],
+        [rows_spec(SPAN, D)]
+        + [whole_spec(*w.shape) for w in weights]
+        + [whole_spec(9, D), table_spec, table_spec],
         [(flat_spec, flat_shape, BF16)] + [tiled_out] * 5 + [kept((D, 3 * D), BF16)],
         [
             pltpu.VMEM((L, 3 * D), F32),
@@ -564,7 +626,7 @@
             pltpu.VMEM((max(4 * rows, 8), 3 * D), F32),
         ],
         "front",
-    )(offsets, lengths, span_states, w_first, w_second, vec_one, bias_qkv, cosine, sine)
+    )(offsets, lengths, core, span_states, *weights, small, cosine, sine)
 
     activations, grad_mid, grad_mixed, dots, g_packed, g_vec_two, g_bias_up, stats = call(
         functools.partial(middle_kernel, rows),
@@ -575,7 +637,7 @@
             tiled_pair,
             flat_pair,
             pl.BlockSpec(memory_space=pl.ANY),
-            whole_spec(4, D),
+            whole_spec(9, D),
             whole_spec(1, FF),
         ],
         [
@@ -599,7 +661,7 @@
             pltpu.SemaphoreType.DMA(()),
         ],
         "middle",
-    )(lengths, x, mixed, cotangent, packed, vec_two, bias_up)
+    )(lengths, x, mixed, cotangent, packed, small, bias_up)
 
     if rows:
         packed_shard = lax.psum_scatter(g_packed, BOTH, scatter_dimension=0, tiled=False)
@@ -619,58 +681,57 @@
         up_grad = scatter_flat(g_up)
         out_grad = scatter_flat(g_packed[2 * FF :])
 
-    span_grad, g_first, g_second, g_vec_one, g_bias_qkv = call(
-        functools.partial(back_kernel, rows),
-        2,
+    half = devices // 2
+    if rows:
+        shape_first, shape_second = (half, rows + 4, cut), (half, rows, 3 * D - cut)
+        halves = [shape_first, shape_first, shape_second, shape_second]
+        bias_up_rows = g_bias_up.reshape(devices, 1, up_share)
+    else:
+        halves = [(D, 3 * D)] + [(8, LANES)] * 3
+        bias_up_rows = jnp.zeros((devices, 1, up_share), F32)
+    span_grad, *halves, g_vec_one, g_bias_qkv = call(
+        functools.partial(back_kernel, rows, an),
+        3,
         windows,
         [flat_spec]
         + [tiled_spec] * 6
-        + [flat_spec, whole_spec(D, 3 * D), whole_spec(2, D), table_spec, table_spec],
-        [
-            (rows_spec(SPAN, D), (windows, SPAN, D), BF16),
-            kept((devices, rows, cut) if rows else w_first.shape, BF16),
-            kept(w_second.shape, BF16),
-            kept((2, D), F32),
-            kept((1, 3 * D), F32),
-        ],
+        + [flat_spec, whole_spec(D, 3 * D), whole_spec(9, D), table_spec, table_spec]
+        + [whole_spec(4, D), whole_spec(devices, 1, up_share), whole_spec(3, D)],
+        [(rows_spec(SPAN, D), (windows, SPAN, D), BF16)]
+        + [kept(shape, BF16) for shape in halves]
+        + [kept((2, D), F32), kept((1, 3 * D), F32)],
         [
             pltpu.VMEM((D, 3 * D), F32),
             pltpu.VMEM((L, 3 * D), BF16),
             pltpu.VMEM((GROUP * L, 2 * LANES), BF16),
             pltpu.VMEM((GROUP * L, 2 * LANES), BF16),
             pltpu.VMEM((L, GROUP * L), BF16),
+            pltpu.VMEM((wa if rows else 1, 16, LANES), F32),
+            pltpu.VMEM((rows + 4, 3 * D), F32),
         ],
         "back",
-    )(offsets, lengths, x, q, k, v, lse, grad_mixed, dots, grad_mid, w_qkv, vec_one, cosine, sine)
-
-    token_count = jnp.sum(lengths).astype(F32)
-    totals = jnp.concatenate([jnp.sum(stats, axis=1), token_count[None]])
-    vec_sums = jnp.concatenate([g_vec_one, g_vec_two, g_bias_qkv.reshape(3, D)], axis=0)
-    share = D // wa
-    up_share = FF // devices
+    )(
+        offsets, lengths, core, x, q, k, v, lse, grad_mixed, dots, grad_mid, w_qkv, small,
+        cosine, sine, g_vec_two, bias_up_rows, stats,
+    )
+
     if rows:
-        vec_sums = vec_sums.reshape(9, wa, share).transpose(1, 0, 2).reshape(wa, 1, 9 * share)
-        vec_sums = jnp.broadcast_to(vec_sums, (wa, an, 9 * share)).reshape(devices, 9 * share)
-        ride = jnp.concatenate(
-            [
-                vec_sums,
-                g_bias_up.reshape(devices, up_share),
-                jnp.broadcast_to(totals, (devices, 4)),
-                jnp.zeros((devices, cut - 9 * share - up_share - 4), F32),
-            ],
-            axis=1,
-        )
-        g_first = jnp.concatenate([g_first, ride.astype(BF16)[:, None]], axis=1)
         g_first, g_second = scatter_steps(
-            [g_first, g_second], [down_order[::-1], other_order[::-1]], devices
+            [halves[:2], halves[2:]], [down_order[::-1], other_order[::-1]], devices
         )
         qkv_grad = jnp.concatenate([g_first[:rows], g_second], axis=1).reshape(-1)
-        ride = g_first[rows]
-        shares = ride[: 9 * share].reshape(9, share)
-        up_bias_grad = ride[9 * share : 9 * share + up_share]
-        totals = ride[9 * share + up_share : 9 * share + up_share + 4]
+        ride = g_first[rows:]
+        third = ride[:, 2 * LANES : 3 * LANES]
+        shares = jnp.concatenate(
+            [ride[:, :share], ride[:, LANES : LANES + share], third[:1, :share]], axis=0
+        )
+        up_bias_grad = third[1, :up_share]
+        totals = third[2, :4]
     else:
-        qkv_grad = scatter_flat(jnp.concatenate([g_first, g_second], axis=1))
+        qkv_grad = scatter_flat(halves[0])
+        token_count = jnp.sum(lengths).astype(F32)
+        totals = jnp.concatenate([jnp.sum(stats, axis=1), token_count[None]])
+        vec_sums = jnp.concatenate([g_vec_one, g_vec_two, g_bias_qkv.reshape(3, D)], axis=0)
         vec_sums, up_sums, totals = lax.psum((vec_sums, g_bias_up.reshape(FF), totals), BOTH)
         shares = lax.dynamic_slice_in_dim(vec_sums, lax.axis_index("wa") * share, share, 1)
         up_bias_grad = lax.dynamic_slice_in_dim(up_sums, flat_index() * up_share, up_share, 0)

time: 405 us -> 379 us (0.936); the launches traced: 397 us -> 377 us
  waiting for transfers between devices: 49.6 us -> 35.9 us
  Pallas kernels: 258 us -> 270 us
  other arithmetic: 16.8 us -> 5.26 us
  local copies, waits for them, and re-layouts: 29.6 us -> 21.6 us
    ppermute x20, waiting for transfers between devices: 49.5 us -> 35.8 us  [swap(): lax.ppermute(value, BOTH, [(i, i ^ 1 << bit) for i in range(devices)])]
    pallas_call x2, Pallas kernels: 163 us -> 175 us  [the longest x1 105 us: body(): call(functools.partial(back_kernel, rows, an), 3, windows, [flat_spec] +...]
    concatenate x2 -> x1, other arithmetic: 4.97 us -> 0.01 us  [body(): jnp.concatenate([ride[:, :share], ride[:, LANES:LANES + share], third[:1,...]
    concatenate x11 -> x0, local copies, waits for them, and re-layouts: 4.13 us -> none  [the longest x1 2.89 us: body(): g_first = jnp.concatenate([g_first, ride.astype(BF16)[:, None]], axis=1)]
  transfers between devices with their start and end apart: 22 -> 22, of which waited for: 14 -> 15; matrix products, arithmetic and copies ran while one was open for 9% -> 5% of each run, Pallas kernels for 41% -> 46%
where the time goes in v4:
time: 379 us; the launch traced here: 377 us
  Pallas kernels  270 us (71%)
  waiting for transfers between devices  35.9 us (9%)
  starting transfers between devices  29 us (8%)
  local copies, waits for them, and re-layouts  21.6 us (6%)
  between operations  15.4 us (4%)
  other arithmetic  5.26 us (1%)
    pallas_call x1, Pallas kernels, body(): call(functools.partial(back_kernel, rows, an), 3, windows, [flat_spec] +...  105 us
    pallas_call x1, Pallas kernels, body(): call(functools.partial(middle_kernel, rows), 1, windows // pair, [flat_pa...  94.8 us
    pallas_call x1, Pallas kernels, body(): call(functools.partial(front_kernel, rows), 3, windows, [rows_spec(SPAN,...  69.6 us
    ppermute x20, waiting for transfers between devices, swap(): lax.ppermute(value, BOTH, [(i, i ^ 1 << bit) for i in range(devices)])  35.8 us
    ppermute x20, starting transfers between devices, swap(): lax.ppermute(value, BOTH, [(i, i ^ 1 << bit) for i in range(devices)])  28.9 us
  transfers between devices with their start and end apart: 22, of which 15 were waited for; matrix products, arithmetic and copies ran while one was open for 5% of the time, Pallas kernels for 46%

profile of v4, /device:TPU:0, one launch (start us, length us, event | category | flops | bytes accessed | tf_op | source)
XLA Modules:
  0.0 376.8 jit_solution(7400076815996255593)
XLA Ops:
  8.2 1.0 reshape.216
  11.0 1.0 reshape.212
  12.0 4.1 %collective-permute-start.5 = (bf16[20,896]{1,0:T(8,128)(2,1)S(1)}, bf16[20,896]{1,0:T(8,128)(2,1)S(1)}, u32[]{:S(2)}, u32[]{:S(2)}) collective-permute-start(bf16[20,896]{1,0:T(8,128)(2,1)S(1)} %slice.103), channel_id=1, source_target_pairs={{0,16},{1,17},{2,18},{3,19},{4,20},{5,21},{6,22},{7,23},{8,24},{9,... | collective-permute-start | bytes 107528 | tf_op jit(solution)/shard_map/ppermute | solution.py:476
  18.6 1.8 collective-permute-start.6
  20.5 2.5 collective-permute-done
  23.0 1.4 collective-permute-start.1
  24.5 1.6 collective-permute-start.7
  26.1 2.1 collective-permute-done.1
  28.3 1.5 collective-permute-start.2
  30.7 1.6 collective-permute-start.8
  32.2 3.8 %collective-permute-done.2 = bf16[2,2,21,1024]{3,2,0,1:T(8,128)(2,1)S(1)} collective-permute-done((bf16[2,2,21,1024]{3,2,0,1:T(8,128)(2,1)S(1)}, bf16[2,2,21,1024]{3,2,0,1:T(8,128)(2,1)S(1)}, u32[]{:S(2)}, u32[]{:S(2)}) %collective-permute-start.2) | collective-permute-done | bytes 172064 | tf_op jit(solution)/shard_map/ppermute | solution.py:476
  36.1 1.7 collective-permute-start.3
  37.8 3.6 collective-permute-done.8
  41.5 5.1 %collective-permute-done.3 = bf16[2,2,2,21,1024]{4,3,0,1,2:T(8,128)(2,1)S(1)} collective-permute-done((bf16[2,2,2,21,1024]{4,3,0,1,2:T(8,128)(2,1)S(1)}, bf16[2,2,2,21,1024]{4,3,0,1,2:T(8,128)(2,1)S(1)}, u32[]{:S(2)}, u32[]{:S(2)}) %collective-permute-start.3) | collective-permute-done | bytes 344096 | tf_op jit(solution)/shard_map/ppermute | solution.py:476
  52.5 1.0 copy.65.refs_3_
  55.5 69.6 %front.1 = (bf16[6,384,640]{2,1,0:T(8,128)(2,1)}, bf16[6,5,384,128]{3,2,1,0:T(8,128)(2,1)}, bf16[6,5,384,128]{3,2,1,0:T(8,128)(2,1)}, bf16[6,5,384,128]{3,2,1,0:...) custom-call(s32[6]{0:T(128)} %offsets.3, s32[6]{0:T(128)} %lengths.5, ...), custom_call_target="tpu_custom_call" | custom-call | tf_op jit(solution)/shard_map/front/pallas_call | solution.py:614
  125.2 94.8 %middle.1 = (bf16[6,384,640]{2,1,0:T(8,128)(2,1)}, f32[6,384,640]{2,1,0:T(8,128)}, bf16[6,5,384,128]{3,2,1,0:T(8,128)(2,1)}, bf16[6,5,384,128]{3,2,1,0:T(8,128)(...) custom-call(s32[6]{0:T(128)} %lengths.5, ...), custom_call_target="tpu_custom_call" | custom-call | tf_op jit(solution)/shard_map/middle/pallas_call | solution.py:631
  221.5 105.2 %back.1 = (bf16[6,512,640]{2,1,0:T(8,128)(2,1)}, bf16[16,24,1024]{2,1,0:T(8,128)(2,1)}, bf16[16,24,1024]{2,1,0:T(8,128)(2,1)}, bf16[16,20,896]{2,1,0:T(8,128)(2,...) custom-call(s32[6]{0:T(128)} %offsets.3, s32[6]{0:T(128)} %lengths.5, s32[1]{0:T(128)} %bitcast.core, ...), custom_call_target="tpu_custom_call" | custom-call | tf_op jit(solution)/shard_map/back/pallas_call | solution.py:692
  326.8 1.2 copy.76
  328.6 1.5 collective-permute-done.15
  330.8 1.5 collective-permute-start.16
  332.6 2.5 collective-permute-start.11
  335.3 6.4 %collective-permute-done.16 = bf16[2,2,2,20,896]{4,3,0,1,2:T(8,128)(2,1)S(1)} collective-permute-done((bf16[2,2,2,20,896]{4,3,0,1,2:T(8,128)(2,1)S(1)}, bf16[2,2,2,20,896]{4,3,0,1,2:T(8,128)(2,1)S(1)}, u32[]{:S(2)}, u32[]{:S(2)}) %collective-permute-start.16) | collective-permute-done | bytes 286752 | tf_op jit(solution)/shard_map/ppermute | solution.py:476
  341.8 1.7 collective-permute-start.17
  345.2 2.9 collective-permute-done.17
  348.1 1.6 collective-permute-start.18
  350.7 1.5 collective-permute-start.13
  352.2 1.2 collective-permute-done.18
  353.5 2.6 collective-permute-start.19
  356.1 1.6 collective-permute-start.14
  357.6 1.3 collective-permute-done.19
  359.0 2.1 collective-permute-done.14
  (117 shorter events, 28.0 us)
Async XLA Ops:
  7.2 118.0 %all-gather.3.cloned.1.call-start = ((), (), s32[]{:S(2)}) async-start(), calls=%async_computation.2 | async-start | bytes 8110080 | tf_op jit(solution)/shard_map/all_gather | solution.py:587
  10.9 354.9 %reduce-scatter.2.cloned.1.call-start = ((), (), s32[]{:S(2)}) async-start(), calls=%async_computation.1 | async-start | bytes 8110080 | tf_op jit(solution)/shard_map/reduce_scatter | solution.py:667
  12.0 6.6 %collective-permute-start.5 = (bf16[20,896]{1,0:T(8,128)(2,1)S(1)}, bf16[20,896]{1,0:T(8,128)(2,1)S(1)}, u32[]{:S(2)}, u32[]{:S(2)}) collective-permute-start(bf16[20,896]{1,0:T(8,128)(2,1)S(1)} %slice.103), channel_id=1, source_target_pairs={{0,16},{1,17},{2,18},{3,19},{4,20},{5,21},{6,22},{7,23},{8,24},{9,... | collective-permute-start | bytes 107528 | tf_op jit(solution)/shard_map/ppermute | solution.py:476
  17.7 5.3 %collective-permute-start = (bf16[21,1024]{1,0:T(8,128)(2,1)S(1)}, bf16[21,1024]{1,0:T(8,128)(2,1)S(1)}, u32[]{:S(2)}, u32[]{:S(2)}) collective-permute-start(bf16[21,1024]{1,0:T(8,128)(2,1)S(1)} %pad_maximum_fusion.10), channel_id=1, source_target_pairs={{0,16},{1,17},{2,18},{3,19},{4,20},{5,21},{6,22},{7,23},{8,24},{9,... | collective-permute-start | bytes 129032 | tf_op jit(solution)/shard_map/ppermute | solution.py:476
  18.6 5.9 %collective-permute-start.6 = (bf16[2,20,896]{2,1,0:T(8,128)(2,1)S(1)}, bf16[2,20,896]{2,1,0:T(8,128)(2,1)S(1)}, u32[]{:S(2)}, u32[]{:S(2)}) collective-permute-start(bf16[2,20,896]{2,1,0:T(8,128)(2,1)S(1)} %pad_maximum_fusion.8), channel_id=1, source_target_pairs={{0,8},{1,9},{2,10},{3,11},{4,12},{5,13},{6,14},{7,15},{8,0},{9,1},... | collective-permute-start | bytes 215048 | tf_op jit(solution)/shard_map/ppermute | solution.py:476
  23.0 5.2 %collective-permute-start.1 = (bf16[2,21,1024]{2,1,0:T(8,128)(2,1)S(1)}, bf16[2,21,1024]{2,1,0:T(8,128)(2,1)S(1)}, u32[]{:S(2)}, u32[]{:S(2)}) collective-permute-start(bf16[2,21,1024]{2,1,0:T(8,128)(2,1)S(1)} %pad_maximum_fusion.7), channel_id=1, source_target_pairs={{0,8},{1,9},{2,10},{3,11},{4,12},{5,13},{6,14},{7,15},{8,0},{9,1},... | collective-permute-start | bytes 258056 | tf_op jit(solution)/shard_map/ppermute | solution.py:476
  24.5 6.0 %collective-permute-start.7 = (bf16[2,2,20,896]{3,2,1,0:T(8,128)(2,1)S(1)}, bf16[2,2,20,896]{3,2,1,0:T(8,128)(2,1)S(1)}, u32[]{:S(2)}, u32[]{:S(2)}) collective-permute-start(bf16[2,2,20,896]{3,2,1,0:T(8,128)(2,1)S(1)} %pad_maximum_fusion.6), channel_id=1, source_target_pairs={{0,2},{1,3},{2,0},{3,1},{4,6},{5,7},{6,4},{7,5},{8,10},{9,11},{10,... | collective-permute-start | bytes 430088 | tf_op jit(solution)/shard_map/ppermute | solution.py:476
  28.3 7.7 %collective-permute-start.2 = (bf16[2,2,21,1024]{3,2,0,1:T(8,128)(2,1)S(1)}, bf16[2,2,21,1024]{3,2,0,1:T(8,128)(2,1)S(1)}, u32[]{:S(2)}, u32[]{:S(2)}) collective-permute-start(bf16[2,2,21,1024]{3,2,0,1:T(8,128)(2,1)S(1)} %pad_maximum_fusion.4), channel_id=1, source_target_pairs={{0,4},{1,5},{2,6},{3,7},{4,0},{5,1},{6,2},{7,3},{8,12},{9,13},{10,... | collective-permute-start | bytes 516104 | tf_op jit(solution)/shard_map/ppermute | solution.py:476
  30.7 10.8 %collective-permute-start.8 = (bf16[2,2,2,20,896]{4,3,2,1,0:T(8,128)(2,1)S(1)}, bf16[2,2,2,20,896]{4,3,2,1,0:T(8,128)(2,1)S(1)}, u32[]{:S(2)}, u32[]{:S(2)}) collective-permute-start(bf16[2,2,2,20,896]{4,3,2,1,0:T(8,128)(2,1)S(1)} %pad_maximum_fusion.3), channel_id=1, source_target_pairs={{0,4},{1,5},{2,6},{3,7},{4,0},{5,1},{6,2},{7,3},{8,12},{9,13},{10,... | collective-permute-start | bytes 860168 | tf_op jit(solution)/shard_map/ppermute | solution.py:476
  36.1 10.5 %collective-permute-start.3 = (bf16[2,2,2,21,1024]{4,3,0,1,2:T(8,128)(2,1)S(1)}, bf16[2,2,2,21,1024]{4,3,0,1,2:T(8,128)(2,1)S(1)}, u32[]{:S(2)}, u32[]{:S(2)}) collective-permute-start(bf16[2,2,2,21,1024]{4,3,0,1,2:T(8,128)(2,1)S(1)} %pad_maximum_fusion.2), channel_id=1, source_target_pairs={{0,2},{1,3},{2,0},{3,1},{4,6},{5,7},{6,4},{7,5},{8,10},{9,11},{10,... | collective-permute-start | bytes 1032200 | tf_op jit(solution)/shard_map/ppermute | solution.py:476
  46.8 7.0 %copy-start = (bf16[2,2,2,2,21,1024]{5,4,3,2,1,0:T(8,128)(2,1)}, bf16[2,2,2,2,21,1024]{5,4,3,2,1,0:T(8,128)(2,1)S(1)}, u32[]{:S(2)}) copy-start(bf16[2,2,2,2,21,1024]{5,4,3,2,1,0:T(8,128)(2,1)S(1)} %copy.57) | copy-start | bytes 2064388
  47.3 6.2 %collective-permute-start.4 = (bf16[16,21,1024]{2,0,1:T(8,128)(2,1)S(1)}, bf16[16,21,1024]{2,0,1:T(8,128)(2,1)S(1)}, u32[]{:S(2)}, u32[]{:S(2)}) collective-permute-start(bf16[16,21,1024]{2,0,1:T(8,128)(2,1)S(1)} %copy.58), channel_id=1, source_target_pairs={{0,1},{1,0},{2,3},{3,2},{4,5},{5,4},{6,7},{7,6},{8,9},{9,8},{10,11... | collective-permute-start | bytes 2064392 | tf_op jit(solution)/shard_map/ppermute | solution.py:476
  47.5 0.9 copy-start.1
  49.2 3.3 collective-permute-start.9
  53.9 0.9 copy-start.2
  220.0 0.7 copy-start.5
  326.7 3.9 %copy-start.4 = (bf16[16,20,896]{2,1,0:T(8,128)(2,1)S(1)}, bf16[16,20,896]{2,1,0:T(8,128)(2,1)}, u32[]{:S(2)}) copy-start(bf16[16,20,896]{2,1,0:T(8,128)(2,1)} %get-tuple-element.49) | copy-start | bytes 1720324
  328.0 2.0 collective-permute-start.15
  328.1 4.3 %collective-permute-start.10 = (bf16[16,24,1024]{2,1,0:T(8,128)(2,1)}, bf16[16,24,1024]{2,1,0:T(8,128)(2,1)S(1)}, u32[]{:S(2)}, u32[]{:S(2)}) collective-permute-start(bf16[16,24,1024]{2,1,0:T(8,128)(2,1)} %get-tuple-element.48), channel_id=1, source_target_pairs={{0,1},{1,0},{2,3},{3,2},{4,5},{5,4},{6,7},{7,6},{8,9},{9,8},{10,11... | collective-permute-start | bytes 2359304 | tf_op jit(solution)/shard_map/ppermute | solution.py:476
  328.6 3.9 %copy-start.3 = (bf16[16,24,1024]{2,1,0:T(8,128)(2,1)S(1)}, bf16[16,24,1024]{2,1,0:T(8,128)(2,1)}, u32[]{:S(2)}) copy-start(bf16[16,24,1024]{2,1,0:T(8,128)(2,1)} %get-tuple-element.47) | copy-start | bytes 2359300
  330.8 11.0 %collective-permute-start.16 = (bf16[2,2,2,20,896]{4,3,0,1,2:T(8,128)(2,1)S(1)}, bf16[2,2,2,20,896]{4,3,0,1,2:T(8,128)(2,1)S(1)}, u32[]{:S(2)}, u32[]{:S(2)}) collective-permute-start(bf16[2,2,2,20,896]{4,3,0,1,2:T(8,128)(2,1)S(1)} %fusion.2), channel_id=1, source_target_pairs={{0,4},{1,5},{2,6},{3,7},{4,0},{5,1},{6,2},{7,3},{8,12},{9,13},{10,... | collective-permute-start | bytes 860168 | tf_op jit(solution)/shard_map/ppermute | solution.py:476
  332.6 11.7 %collective-permute-start.11 = (bf16[2,2,2,24,1024]{4,3,0,1,2:T(8,128)(2,1)S(1)}, bf16[2,2,2,24,1024]{4,3,0,1,2:T(8,128)(2,1)S(1)}, u32[]{:S(2)}, u32[]{:S(2)}) collective-permute-start(bf16[2,2,2,24,1024]{4,3,0,1,2:T(8,128)(2,1)S(1)} %fusion), channel_id=1, source_target_pairs={{0,2},{1,3},{2,0},{3,1},{4,6},{5,7},{6,4},{7,5},{8,10},{9,11},{10,... | collective-permute-start | bytes 1179656 | tf_op jit(solution)/shard_map/ppermute | solution.py:476
  341.8 6.2 %collective-permute-start.17 = (bf16[2,2,20,896]{3,2,0,1:T(8,128)(2,1)S(1)}, bf16[2,2,20,896]{3,2,0,1:T(8,128)(2,1)S(1)}, u32[]{:S(2)}, u32[]{:S(2)}) collective-permute-start(bf16[2,2,20,896]{3,2,0,1:T(8,128)(2,1)S(1)} %get-tuple-element.72), channel_id=1, source_target_pairs={{0,2},{1,3},{2,0},{3,1},{4,6},{5,7},{6,4},{7,5},{8,10},{9,11},{10,... | collective-permute-start | bytes 430088 | tf_op jit(solution)/shard_map/ppermute | solution.py:476
  344.3 6.3 %collective-permute-start.12 = (bf16[2,2,24,1024]{3,2,0,1:T(8,128)(2,1)S(1)}, bf16[2,2,24,1024]{3,2,0,1:T(8,128)(2,1)S(1)}, u32[]{:S(2)}, u32[]{:S(2)}) collective-permute-start(bf16[2,2,24,1024]{3,2,0,1:T(8,128)(2,1)S(1)} %get-tuple-element.68), channel_id=1, source_target_pairs={{0,4},{1,5},{2,6},{3,7},{4,0},{5,1},{6,2},{7,3},{8,12},{9,13},{10,... | collective-permute-start | bytes 589832 | tf_op jit(solution)/shard_map/ppermute | solution.py:476
  348.1 5.3 %collective-permute-start.18 = (bf16[2,20,896]{2,1,0:T(8,128)(2,1)S(1)}, bf16[2,20,896]{2,1,0:T(8,128)(2,1)S(1)}, u32[]{:S(2)}, u32[]{:S(2)}) collective-permute-start(bf16[2,20,896]{2,1,0:T(8,128)(2,1)S(1)} %get-tuple-element.66), channel_id=1, source_target_pairs={{0,8},{1,9},{2,10},{3,11},{4,12},{5,13},{6,14},{7,15},{8,0},{9,1},... | collective-permute-start | bytes 215048 | tf_op jit(solution)/shard_map/ppermute | solution.py:476
  350.7 5.4 %collective-permute-start.13 = (bf16[2,24,1024]{2,1,0:T(8,128)(2,1)S(1)}, bf16[2,24,1024]{2,1,0:T(8,128)(2,1)S(1)}, u32[]{:S(2)}, u32[]{:S(2)}) collective-permute-start(bf16[2,24,1024]{2,1,0:T(8,128)(2,1)S(1)} %get-tuple-element.62), channel_id=1, source_target_pairs={{0,8},{1,9},{2,10},{3,11},{4,12},{5,13},{6,14},{7,15},{8,0},{9,1},... | collective-permute-start | bytes 294920 | tf_op jit(solution)/shard_map/ppermute | solution.py:476
  353.5 5.5 %collective-permute-start.19 = (bf16[20,896]{1,0:T(8,128)(2,1)S(1)}, bf16[20,896]{1,0:T(8,128)(2,1)S(1)}, u32[]{:S(2)}, u32[]{:S(2)}) collective-permute-start(bf16[20,896]{1,0:T(8,128)(2,1)S(1)} %fusion.13), channel_id=1, source_target_pairs={{0,16},{1,17},{2,18},{3,19},{4,20},{5,21},{6,22},{7,23},{8,24},{9,... | collective-permute-start | bytes 107528 | tf_op jit(solution)/shard_map/ppermute | solution.py:476
  356.1 5.1 %collective-permute-start.14 = (bf16[24,1024]{1,0:T(8,128)(2,1)S(1)}, bf16[24,1024]{1,0:T(8,128)(2,1)S(1)}, u32[]{:S(2)}, u32[]{:S(2)}) collective-permute-start(bf16[24,1024]{1,0:T(8,128)(2,1)S(1)} %fusion.12), channel_id=1, source_target_pairs={{0,16},{1,17},{2,18},{3,19},{4,20},{5,21},{6,22},{7,23},{8,24},{9,... | collective-permute-start | bytes 147464 | tf_op jit(solution)/shard_map/ppermute | solution.py:476
Sparse Core Ops, SparseCore 0:
  11.0 78.5 all-gather.2
  220.2 124.6 reduce-scatter.1

commit v5 on v4

--- a/solution.py
+++ b/solution.py
@@ -3,6 +3,7 @@
 
 import jax
 import jax.numpy as jnp
+import numpy as np
 from jax import lax
 from jax.experimental import pallas as pl
 from jax.experimental.pallas import tpu as pltpu
@@ -86,8 +87,15 @@
     return jnp.where(at < 3, 1.0, jnp.where(at == 3, bias, 0.0)).astype(BF16)
 
 
-def take_rows(full, start):
-    return pltpu.roll(full, (SPAN - start) % SPAN, 0)[:L]
+def picks(rows, cols, shift):
+    row = lax.broadcasted_iota(jnp.int32, (rows, cols), 0)
+    return jnp.where(lane_iota(rows, cols) - row == shift, 1.0, 0.0).astype(BF16)
+
+
+def turn_tables(cosine, sine, offset):
+    cos_off, sin_off = offset[0, 0:1, :], offset[0, 1:2, :]
+    cos, sin = cosine[...], sine[...]
+    return cos * cos_off - sin * sin_off, sin * cos_off + cos * sin_off
 
 
 def unpack_rows(parts, rows, staging, dest):
@@ -128,10 +136,10 @@
     offsets, lengths, core, span, *refs,
 ):
     (
-        weights, small, cosine, sine,
+        weights, small, cosine, sine, offset,
         x_out, q_out, k_out, v_out, lse_out, mixed_out, w_qkv,
         proj, keys_big, values_big, staging,
-    ) = refs[:-14], *refs[-14:]
+    ) = refs[:-15], *refs[-15:]
     window = pl.program_id(0)
 
     @pl.when(window == 0)
@@ -149,14 +157,13 @@
 
     start = offsets[window]
     length = lengths[window]
-    x = take_rows(span[0].astype(F32), start)
+    x = nn(picks(L, SPAN, start), span[0])
     x_out[0] = x.astype(BF16)
     n, _ = normalize(x)
     normed = (n * small[0:1, :] + small[2:3, :]).astype(BF16)
     bias = jnp.concatenate([small[4:5, :], small[5:6, :], small[6:7, :]], axis=1)
     proj[...] = nn(normed, w_qkv[...]) + bias
-    cos = take_rows(cosine[...], start)
-    sin = take_rows(sine[...], start)
+    cos, sin = turn_tables(cosine, sine, offset)
     for t in range(TILES):
         lanes = slice(t * LANES, (t + 1) * LANES)
         q = proj[:, t * LANES : (t + 1) * LANES] * SCALE
@@ -329,7 +336,7 @@
 def back_kernel(
     rows, inner,
     offsets, lengths, core, x_in, q_in, k_in, v_in, lse_in, gm_in, dots_in, grad_mid, w_qkv, small,
-    cosine, sine, vec_two, bias_up, stats,
+    cosine, sine, offset, vec_two, bias_up, stats,
     span_grad, keep_first, send_first, keep_second, send_second, g_vecs, g_bias,
     a_qkv, grad_proj, queries_big, mixed_big, scores_back, ride, staging,
 ):
@@ -342,8 +349,7 @@
         for ref in (a_qkv, g_vecs, g_bias):
             ref[...] = jnp.zeros_like(ref)
 
-    cos = take_rows(cosine[...], start)
-    sin = take_rows(sine[...], start)
+    cos, sin = turn_tables(cosine, sine, offset)
     key_lanes = key_side(length)
     at = lane_iota(L, LANES) % HW
     value_lanes = jnp.where(at < 3, 1.0, 0.0).astype(BF16)
@@ -523,13 +529,12 @@
     return [keep + got.astype(F32) for keep, got in values]
 
 
-def rotary_tables():
-    inverse = 10000.0 ** (-jnp.arange(0, HW, 2, dtype=F32) / HW)
-    angles = jnp.arange(SPAN, dtype=jnp.int32).astype(F32)[:, None] * inverse
-    cosine = jnp.tile(jnp.cos(angles), (1, 2 * GROUP))
-    sine = jnp.sin(angles)
-    sine = jnp.tile(jnp.concatenate([-sine, sine], axis=1), (1, GROUP))
-    return cosine, sine
+def rotary_tables(positions):
+    inverse = 10000.0 ** (-np.arange(0, HW, 2, dtype=np.float32) / np.float32(HW))
+    inverse = jnp.asarray(np.tile(inverse.astype(np.float32), 2 * GROUP))
+    angles = positions.astype(F32)[:, None] * inverse
+    first = (lane_iota(1, LANES) % HW) < HW // 2
+    return jnp.cos(angles), jnp.where(first, -1.0, 1.0) * jnp.sin(angles)
 
 
 def body(
@@ -595,7 +600,8 @@
         w_up = w_up.reshape(D, steps, D).transpose(1, 0, 2).reshape(FF, D)
         w_out = lax.all_gather(out_weight, BOTH, axis=0, tiled=True).reshape(D, D)
         packed = jnp.concatenate([w_down, w_up, w_out], axis=0)
-    cosine, sine = rotary_tables()
+    cosine, sine = rotary_tables(jnp.arange(L, dtype=jnp.int32))
+    offset_turns = jnp.stack(rotary_tables(offsets), axis=1)
 
     tiled_spec = rows_spec(TILES, L, LANES)
     tiled_shape = (windows, TILES, L, LANES)
@@ -604,7 +610,8 @@
     pair = 1
     tiled_pair = rows_spec(TILES, L, LANES, count=pair)
     flat_pair = rows_spec(L, D, count=pair)
-    table_spec = whole_spec(SPAN, LANES)
+    table_spec = whole_spec(L, LANES)
+    turn_spec = rows_spec(2, LANES)
 
     tiled_out = (tiled_spec, tiled_shape, BF16)
 
@@ -617,7 +624,7 @@
         windows,
         [rows_spec(SPAN, D)]
         + [whole_spec(*w.shape) for w in weights]
-        + [whole_spec(9, D), table_spec, table_spec],
+        + [whole_spec(9, D), table_spec, table_spec, turn_spec],
         [(flat_spec, flat_shape, BF16)] + [tiled_out] * 5 + [kept((D, 3 * D), BF16)],
         [
             pltpu.VMEM((L, 3 * D), F32),
@@ -626,7 +633,7 @@
             pltpu.VMEM((max(4 * rows, 8), 3 * D), F32),
         ],
         "front",
-    )(offsets, lengths, core, span_states, *weights, small, cosine, sine)
+    )(offsets, lengths, core, span_states, *weights, small, cosine, sine, offset_turns)
 
     activations, grad_mid, grad_mixed, dots, g_packed, g_vec_two, g_bias_up, stats = call(
         functools.partial(middle_kernel, rows),
@@ -695,7 +702,7 @@
         windows,
         [flat_spec]
         + [tiled_spec] * 6
-        + [flat_spec, whole_spec(D, 3 * D), whole_spec(9, D), table_spec, table_spec]
+        + [flat_spec, whole_spec(D, 3 * D), whole_spec(9, D), table_spec, table_spec, turn_spec]
         + [whole_spec(4, D), whole_spec(devices, 1, up_share), whole_spec(3, D)],
         [(rows_spec(SPAN, D), (windows, SPAN, D), BF16)]
         + [kept(shape, BF16) for shape in halves]
@@ -712,7 +719,7 @@
         "back",
     )(
         offsets, lengths, core, x, q, k, v, lse, grad_mixed, dots, grad_mid, w_qkv, small,
-        cosine, sine, g_vec_two, bias_up_rows, stats,
+        cosine, sine, offset_turns, g_vec_two, bias_up_rows, stats,
     )
 
     if rows:

time: 379 us -> 373 us (0.984)
  Pallas kernels: 270 us -> 264 us
    pallas_call x1, Pallas kernels: 69.6 us -> 64.5 us  [body(): call(functools.partial(front_kernel, rows), 3, windows, [rows_spec(SPAN,...]
where the time goes in v5:
time: 373 us; the launch traced here: 371 us
  Pallas kernels  264 us (71%)
  waiting for transfers between devices  35.2 us (9%)
  starting transfers between devices  29 us (8%)
  local copies, waits for them, and re-layouts  19.1 us (5%)
  between operations  15.4 us (4%)
  other arithmetic  8 us (2%)
    pallas_call x1, Pallas kernels, body(): call(functools.partial(back_kernel, rows, an), 3, windows, [flat_spec] +...  105 us
    pallas_call x1, Pallas kernels, body(): call(functools.partial(middle_kernel, rows), 1, windows // pair, [flat_pa...  94.8 us
    pallas_call x1, Pallas kernels, body(): call(functools.partial(front_kernel, rows), 3, windows, [rows_spec(SPAN,...  64.5 us
    ppermute x20, waiting for transfers between devices, swap(): lax.ppermute(value, BOTH, [(i, i ^ 1 << bit) for i in range(devices)])  35.1 us
    ppermute x20, starting transfers between devices, swap(): lax.ppermute(value, BOTH, [(i, i ^ 1 << bit) for i in range(devices)])  28.9 us
  transfers between devices with their start and end apart: 22, of which 15 were waited for; matrix products, arithmetic and copies ran while one was open for 5% of the time, Pallas kernels for 46%

profile of v5, /device:TPU:0, one launch (start us, length us, event | category | flops | bytes accessed | tf_op | source)
XLA Modules:
  0.0 371.0 jit_solution(9582939910913121697)
XLA Ops:
  11.0 1.0 reshape.289
  12.0 4.1 %collective-permute-start.5 = (bf16[20,896]{1,0:T(8,128)(2,1)S(1)}, bf16[20,896]{1,0:T(8,128)(2,1)S(1)}, u32[]{:S(2)}, u32[]{:S(2)}) collective-permute-start(bf16[20,896]{1,0:T(8,128)(2,1)S(1)} %slice.103), channel_id=1, source_target_pairs={{0,16},{1,17},{2,18},{3,19},{4,20},{5,21},{6,22},{7,23},{8,24},{9,... | collective-permute-start | bytes 107528 | tf_op jit(solution)/shard_map/ppermute | solution.py:482
  18.6 1.8 collective-permute-start.6
  20.5 2.5 collective-permute-done
  23.0 1.9 collective-permute-start.1
  25.0 1.6 collective-permute-start.7
  26.6 1.7 collective-permute-done.1
  28.3 1.5 collective-permute-start.2
  30.7 1.6 collective-permute-start.8
  32.2 4.0 %collective-permute-done.2 = bf16[2,2,21,1024]{3,2,0,1:T(8,128)(2,1)S(1)} collective-permute-done((bf16[2,2,21,1024]{3,2,0,1:T(8,128)(2,1)S(1)}, bf16[2,2,21,1024]{3,2,0,1:T(8,128)(2,1)S(1)}, u32[]{:S(2)}, u32[]{:S(2)}) %collective-permute-start.2) | collective-permute-done | bytes 172064 | tf_op jit(solution)/shard_map/ppermute | solution.py:482
  36.3 1.5 collective-permute-start.3
  38.0 3.2 collective-permute-done.8
  41.3 5.6 %collective-permute-done.3 = bf16[2,2,2,21,1024]{4,3,0,1,2:T(8,128)(2,1)S(1)} collective-permute-done((bf16[2,2,2,21,1024]{4,3,0,1,2:T(8,128)(2,1)S(1)}, bf16[2,2,2,21,1024]{4,3,0,1,2:T(8,128)(2,1)S(1)}, u32[]{:S(2)}, u32[]{:S(2)}) %collective-permute-start.3) | collective-permute-done | bytes 344096 | tf_op jit(solution)/shard_map/ppermute | solution.py:482
  49.8 1.5 fusion.4
  52.2 1.0 copy.63.refs_3_
  55.3 64.5 %front.1 = (bf16[6,384,640]{2,1,0:T(8,128)(2,1)}, bf16[6,5,384,128]{3,2,1,0:T(8,128)(2,1)}, bf16[6,5,384,128]{3,2,1,0:T(8,128)(2,1)}, bf16[6,5,384,128]{3,2,1,0:...) custom-call(s32[6]{0:T(128)} %offsets.3, s32[6]{0:T(128)} %lengths.5, ...), custom_call_target="tpu_custom_call" | custom-call | tf_op jit(solution)/shard_map/front/pallas_call | solution.py:621
  119.8 94.8 %middle.1 = (bf16[6,384,640]{2,1,0:T(8,128)(2,1)}, f32[6,384,640]{2,1,0:T(8,128)}, bf16[6,5,384,128]{3,2,1,0:T(8,128)(2,1)}, bf16[6,5,384,128]{3,2,1,0:T(8,128)(...) custom-call(s32[6]{0:T(128)} %lengths.5, ...), custom_call_target="tpu_custom_call" | custom-call | tf_op jit(solution)/shard_map/middle/pallas_call | solution.py:638
  216.0 105.0 %back.1 = (bf16[6,512,640]{2,1,0:T(8,128)(2,1)}, bf16[16,24,1024]{2,1,0:T(8,128)(2,1)}, bf16[16,24,1024]{2,1,0:T(8,128)(2,1)}, bf16[16,20,896]{2,1,0:T(8,128)(2,...) custom-call(s32[6]{0:T(128)} %offsets.3, s32[6]{0:T(128)} %lengths.5, s32[1]{0:T(128)} %bitcast.core, ...), custom_call_target="tpu_custom_call" | custom-call | tf_op jit(solution)/shard_map/back/pallas_call | solution.py:699
  321.0 1.2 copy.70
  322.8 1.5 collective-permute-done.15
  325.0 1.5 collective-permute-start.16
  326.8 2.3 collective-permute-start.11
  329.3 6.9 %collective-permute-done.16 = bf16[2,2,2,20,896]{4,3,0,1,2:T(8,128)(2,1)S(1)} collective-permute-done((bf16[2,2,2,20,896]{4,3,0,1,2:T(8,128)(2,1)S(1)}, bf16[2,2,2,20,896]{4,3,0,1,2:T(8,128)(2,1)S(1)}, u32[]{:S(2)}, u32[]{:S(2)}) %collective-permute-start.16) | collective-permute-done | bytes 286752 | tf_op jit(solution)/shard_map/ppermute | solution.py:482
  336.3 1.5 collective-permute-start.17
  339.1 3.2 collective-permute-done.17
  342.4 1.7 collective-permute-start.18
  344.6 1.8 collective-permute-start.13
  346.5 1.3 collective-permute-done.18
  347.8 2.4 collective-permute-start.19
  350.2 1.5 collective-permute-start.14
  351.7 1.4 collective-permute-done.19
  353.1 2.1 collective-permute-done.14
  (117 shorter events, 26.3 us)
Async XLA Ops:
  7.2 112.6 %all-gather.3.cloned.1.call-start = ((), (), s32[]{:S(2)}) async-start(), calls=%async_computation.2 | async-start | bytes 8110080 | tf_op jit(solution)/shard_map/all_gather | solution.py:592
  10.9 26.9 %copy-start.6 = (f32[128]{0:T(128)S(1)}, f32[128]{0:T(128)}, u32[]{:S(2)}) copy-start(f32[128]{0:T(128)} %constant.159.clone) | copy-start | bytes 1540
  10.9 349.0 %reduce-scatter.2.cloned.1.call-start = ((), (), s32[]{:S(2)}) async-start(), calls=%async_computation.1 | async-start | bytes 8110080 | tf_op jit(solution)/shard_map/reduce_scatter | solution.py:674
  12.0 6.6 %collective-permute-start.5 = (bf16[20,896]{1,0:T(8,128)(2,1)S(1)}, bf16[20,896]{1,0:T(8,128)(2,1)S(1)}, u32[]{:S(2)}, u32[]{:S(2)}) collective-permute-start(bf16[20,896]{1,0:T(8,128)(2,1)S(1)} %slice.103), channel_id=1, source_target_pairs={{0,16},{1,17},{2,18},{3,19},{4,20},{5,21},{6,22},{7,23},{8,24},{9,... | collective-permute-start | bytes 107528 | tf_op jit(solution)/shard_map/ppermute | solution.py:482
  17.7 5.3 %collective-permute-start = (bf16[21,1024]{1,0:T(8,128)(2,1)S(1)}, bf16[21,1024]{1,0:T(8,128)(2,1)S(1)}, u32[]{:S(2)}, u32[]{:S(2)}) collective-permute-start(bf16[21,1024]{1,0:T(8,128)(2,1)S(1)} %pad_maximum_fusion.9), channel_id=1, source_target_pairs={{0,16},{1,17},{2,18},{3,19},{4,20},{5,21},{6,22},{7,23},{8,24},{9,... | collective-permute-start | bytes 129032 | tf_op jit(solution)/shard_map/ppermute | solution.py:482
  18.6 6.3 %collective-permute-start.6 = (bf16[2,20,896]{2,1,0:T(8,128)(2,1)S(1)}, bf16[2,20,896]{2,1,0:T(8,128)(2,1)S(1)}, u32[]{:S(2)}, u32[]{:S(2)}) collective-permute-start(bf16[2,20,896]{2,1,0:T(8,128)(2,1)S(1)} %pad_maximum_fusion.8), channel_id=1, source_target_pairs={{0,8},{1,9},{2,10},{3,11},{4,12},{5,13},{6,14},{7,15},{8,0},{9,1},... | collective-permute-start | bytes 215048 | tf_op jit(solution)/shard_map/ppermute | solution.py:482
  23.0 5.2 %collective-permute-start.1 = (bf16[2,21,1024]{2,1,0:T(8,128)(2,1)S(1)}, bf16[2,21,1024]{2,1,0:T(8,128)(2,1)S(1)}, u32[]{:S(2)}, u32[]{:S(2)}) collective-permute-start(bf16[2,21,1024]{2,1,0:T(8,128)(2,1)S(1)} %pad_maximum_fusion.7), channel_id=1, source_target_pairs={{0,8},{1,9},{2,10},{3,11},{4,12},{5,13},{6,14},{7,15},{8,0},{9,1},... | collective-permute-start | bytes 258056 | tf_op jit(solution)/shard_map/ppermute | solution.py:482
  25.0 5.6 %collective-permute-start.7 = (bf16[2,2,20,896]{3,2,1,0:T(8,128)(2,1)S(1)}, bf16[2,2,20,896]{3,2,1,0:T(8,128)(2,1)S(1)}, u32[]{:S(2)}, u32[]{:S(2)}) collective-permute-start(bf16[2,2,20,896]{3,2,1,0:T(8,128)(2,1)S(1)} %pad_maximum_fusion.6), channel_id=1, source_target_pairs={{0,2},{1,3},{2,0},{3,1},{4,6},{5,7},{6,4},{7,5},{8,10},{9,11},{10,... | collective-permute-start | bytes 430088 | tf_op jit(solution)/shard_map/ppermute | solution.py:482
  28.3 7.8 %collective-permute-start.2 = (bf16[2,2,21,1024]{3,2,0,1:T(8,128)(2,1)S(1)}, bf16[2,2,21,1024]{3,2,0,1:T(8,128)(2,1)S(1)}, u32[]{:S(2)}, u32[]{:S(2)}) collective-permute-start(bf16[2,2,21,1024]{3,2,0,1:T(8,128)(2,1)S(1)} %pad_maximum_fusion.4), channel_id=1, source_target_pairs={{0,4},{1,5},{2,6},{3,7},{4,0},{5,1},{6,2},{7,3},{8,12},{9,13},{10,... | collective-permute-start | bytes 516104 | tf_op jit(solution)/shard_map/ppermute | solution.py:482
  30.7 10.5 %collective-permute-start.8 = (bf16[2,2,2,20,896]{4,3,2,1,0:T(8,128)(2,1)S(1)}, bf16[2,2,2,20,896]{4,3,2,1,0:T(8,128)(2,1)S(1)}, u32[]{:S(2)}, u32[]{:S(2)}) collective-permute-start(bf16[2,2,2,20,896]{4,3,2,1,0:T(8,128)(2,1)S(1)} %pad_maximum_fusion.3), channel_id=1, source_target_pairs={{0,4},{1,5},{2,6},{3,7},{4,0},{5,1},{6,2},{7,3},{8,12},{9,13},{10,... | collective-permute-start | bytes 860168 | tf_op jit(solution)/shard_map/ppermute | solution.py:482
  36.3 10.6 %collective-permute-start.3 = (bf16[2,2,2,21,1024]{4,3,0,1,2:T(8,128)(2,1)S(1)}, bf16[2,2,2,21,1024]{4,3,0,1,2:T(8,128)(2,1)S(1)}, u32[]{:S(2)}, u32[]{:S(2)}) collective-permute-start(bf16[2,2,2,21,1024]{4,3,0,1,2:T(8,128)(2,1)S(1)} %pad_maximum_fusion.2), channel_id=1, source_target_pairs={{0,2},{1,3},{2,0},{3,1},{4,6},{5,7},{6,4},{7,5},{8,10},{9,11},{10,... | collective-permute-start | bytes 1032200 | tf_op jit(solution)/shard_map/ppermute | solution.py:482
  47.2 6.5 %copy-start = (bf16[2,2,2,2,21,1024]{5,4,3,2,1,0:T(8,128)(2,1)}, bf16[2,2,2,2,21,1024]{5,4,3,2,1,0:T(8,128)(2,1)S(1)}, u32[]{:S(2)}) copy-start(bf16[2,2,2,2,21,1024]{5,4,3,2,1,0:T(8,128)(2,1)S(1)} %copy.55) | copy-start | bytes 2064388
  47.6 5.7 %collective-permute-start.4 = (bf16[16,21,1024]{2,0,1:T(8,128)(2,1)S(1)}, bf16[16,21,1024]{2,0,1:T(8,128)(2,1)S(1)}, u32[]{:S(2)}, u32[]{:S(2)}) collective-permute-start(bf16[16,21,1024]{2,0,1:T(8,128)(2,1)S(1)} %copy.56), channel_id=1, source_target_pairs={{0,1},{1,0},{2,3},{3,2},{4,5},{5,4},{6,7},{7,6},{8,9},{9,8},{10,11... | collective-permute-start | bytes 2064392 | tf_op jit(solution)/shard_map/ppermute | solution.py:482
  47.8 0.8 copy-start.1
  48.7 3.6 collective-permute-start.9
  53.6 0.9 copy-start.2
  214.6 0.7 copy-start.5
  321.0 3.9 %copy-start.4 = (bf16[16,20,896]{2,1,0:T(8,128)(2,1)S(1)}, bf16[16,20,896]{2,1,0:T(8,128)(2,1)}, u32[]{:S(2)}) copy-start(bf16[16,20,896]{2,1,0:T(8,128)(2,1)} %get-tuple-element.49) | copy-start | bytes 1720324
  322.3 2.0 collective-permute-start.15
  322.3 4.3 %collective-permute-start.10 = (bf16[16,24,1024]{2,1,0:T(8,128)(2,1)}, bf16[16,24,1024]{2,1,0:T(8,128)(2,1)S(1)}, u32[]{:S(2)}, u32[]{:S(2)}) collective-permute-start(bf16[16,24,1024]{2,1,0:T(8,128)(2,1)} %get-tuple-element.48), channel_id=1, source_target_pairs={{0,1},{1,0},{2,3},{3,2},{4,5},{5,4},{6,7},{7,6},{8,9},{9,8},{10,11... | collective-permute-start | bytes 2359304 | tf_op jit(solution)/shard_map/ppermute | solution.py:482
  322.8 3.8 %copy-start.3 = (bf16[16,24,1024]{2,1,0:T(8,128)(2,1)S(1)}, bf16[16,24,1024]{2,1,0:T(8,128)(2,1)}, u32[]{:S(2)}) copy-start(bf16[16,24,1024]{2,1,0:T(8,128)(2,1)} %get-tuple-element.47) | copy-start | bytes 2359300
  325.0 11.2 %collective-permute-start.16 = (bf16[2,2,2,20,896]{4,3,0,1,2:T(8,128)(2,1)S(1)}, bf16[2,2,2,20,896]{4,3,0,1,2:T(8,128)(2,1)S(1)}, u32[]{:S(2)}, u32[]{:S(2)}) collective-permute-start(bf16[2,2,2,20,896]{4,3,0,1,2:T(8,128)(2,1)S(1)} %fusion.2), channel_id=1, source_target_pairs={{0,4},{1,5},{2,6},{3,7},{4,0},{5,1},{6,2},{7,3},{8,12},{9,13},{10,... | collective-permute-start | bytes 860168 | tf_op jit(solution)/shard_map/ppermute | solution.py:482
  326.8 11.4 %collective-permute-start.11 = (bf16[2,2,2,24,1024]{4,3,0,1,2:T(8,128)(2,1)S(1)}, bf16[2,2,2,24,1024]{4,3,0,1,2:T(8,128)(2,1)S(1)}, u32[]{:S(2)}, u32[]{:S(2)}) collective-permute-start(bf16[2,2,2,24,1024]{4,3,0,1,2:T(8,128)(2,1)S(1)} %fusion), channel_id=1, source_target_pairs={{0,2},{1,3},{2,0},{3,1},{4,6},{5,7},{6,4},{7,5},{8,10},{9,11},{10,... | collective-permute-start | bytes 1179656 | tf_op jit(solution)/shard_map/ppermute | solution.py:482
  336.3 6.1 %collective-permute-start.17 = (bf16[2,2,20,896]{3,2,0,1:T(8,128)(2,1)S(1)}, bf16[2,2,20,896]{3,2,0,1:T(8,128)(2,1)S(1)}, u32[]{:S(2)}, u32[]{:S(2)}) collective-permute-start(bf16[2,2,20,896]{3,2,0,1:T(8,128)(2,1)S(1)} %get-tuple-element.72), channel_id=1, source_target_pairs={{0,2},{1,3},{2,0},{3,1},{4,6},{5,7},{6,4},{7,5},{8,10},{9,11},{10,... | collective-permute-start | bytes 430088 | tf_op jit(solution)/shard_map/ppermute | solution.py:482
  338.3 6.3 %collective-permute-start.12 = (bf16[2,2,24,1024]{3,2,0,1:T(8,128)(2,1)S(1)}, bf16[2,2,24,1024]{3,2,0,1:T(8,128)(2,1)S(1)}, u32[]{:S(2)}, u32[]{:S(2)}) collective-permute-start(bf16[2,2,24,1024]{3,2,0,1:T(8,128)(2,1)S(1)} %get-tuple-element.68), channel_id=1, source_target_pairs={{0,4},{1,5},{2,6},{3,7},{4,0},{5,1},{6,2},{7,3},{8,12},{9,13},{10,... | collective-permute-start | bytes 589832 | tf_op jit(solution)/shard_map/ppermute | solution.py:482
  342.4 5.4 %collective-permute-start.18 = (bf16[2,20,896]{2,1,0:T(8,128)(2,1)S(1)}, bf16[2,20,896]{2,1,0:T(8,128)(2,1)S(1)}, u32[]{:S(2)}, u32[]{:S(2)}) collective-permute-start(bf16[2,20,896]{2,1,0:T(8,128)(2,1)S(1)} %get-tuple-element.66), channel_id=1, source_target_pairs={{0,8},{1,9},{2,10},{3,11},{4,12},{5,13},{6,14},{7,15},{8,0},{9,1},... | collective-permute-start | bytes 215048 | tf_op jit(solution)/shard_map/ppermute | solution.py:482
  344.6 5.5 %collective-permute-start.13 = (bf16[2,24,1024]{2,1,0:T(8,128)(2,1)S(1)}, bf16[2,24,1024]{2,1,0:T(8,128)(2,1)S(1)}, u32[]{:S(2)}, u32[]{:S(2)}) collective-permute-start(bf16[2,24,1024]{2,1,0:T(8,128)(2,1)S(1)} %get-tuple-element.62), channel_id=1, source_target_pairs={{0,8},{1,9},{2,10},{3,11},{4,12},{5,13},{6,14},{7,15},{8,0},{9,1},... | collective-permute-start | bytes 294920 | tf_op jit(solution)/shard_map/ppermute | solution.py:482
  347.8 5.3 %collective-permute-start.19 = (bf16[20,896]{1,0:T(8,128)(2,1)S(1)}, bf16[20,896]{1,0:T(8,128)(2,1)S(1)}, u32[]{:S(2)}, u32[]{:S(2)}) collective-permute-start(bf16[20,896]{1,0:T(8,128)(2,1)S(1)} %fusion.14), channel_id=1, source_target_pairs={{0,16},{1,17},{2,18},{3,19},{4,20},{5,21},{6,22},{7,23},{8,24},{9,... | collective-permute-start | bytes 107528 | tf_op jit(solution)/shard_map/ppermute | solution.py:482
  350.2 5.1 %collective-permute-start.14 = (bf16[24,1024]{1,0:T(8,128)(2,1)S(1)}, bf16[24,1024]{1,0:T(8,128)(2,1)S(1)}, u32[]{:S(2)}, u32[]{:S(2)}) collective-permute-start(bf16[24,1024]{1,0:T(8,128)(2,1)S(1)} %fusion.13), channel_id=1, source_target_pairs={{0,16},{1,17},{2,18},{3,19},{4,20},{5,21},{6,22},{7,23},{8,24},{9,... | collective-permute-start | bytes 147464 | tf_op jit(solution)/shard_map/ppermute | solution.py:482
Sparse Core Ops, SparseCore 0:
  11.1 78.4 all-gather.2
  214.8 124.5 reduce-scatter.1
